TPU v7x, 32 devices: a whole 2x2x4 slice. The times are simulated.
32 devices in a mesh: dp: 4 (over y, core), store: 8 (over z, x).
Axes of the slice: x: 2, y: 2, z: 4, core: 2. Of those that a mesh axis runs over, the one named last changes fastest.
Arguments:
- tokens: bfloat16 [16384, 768], P(('dp', 'store')), may hold values from -6 to 6
- datastore: bfloat16 [32768, 768], P('store'), may hold values from -6 to 6
- indices: int32 [16384, 16], P(('dp', 'store')), may hold values from 0 to 32767, as said below
- lengths: int32 [32], P(('dp', 'store')), may hold values from 64 to 512, as said below
- proj_weight: bfloat16 [768, 6, 768], replicated, may hold values from -0.21875 to 0.21875
- out_weight: bfloat16 [768, 2, 768], replicated, may hold values from -0.875 to 0.875
- proj_bias: float32 [768, 6], replicated, may hold values from -2 to 2
- norm_gain: float32 [768, 3], replicated, may hold values from 0.5 to 1.5
- norm_bias: float32 [768, 3], replicated, may hold values from -2 to 2
- inner_weight: bfloat16 [768, 3072], replicated, may hold values from -0.21875 to 0.21875
- inner_bias: float32 [3072], replicated, may hold values from -2 to 2
- outer_weight: bfloat16 [3072, 768], replicated, may hold values from -0.109375 to 0.109375
- outer_bias: float32 [768], replicated, may hold values from -2 to 2
- cotangent: bfloat16 [16384, 768], P(('dp', 'store')), may hold values from -6 to 6
Outputs:
- output: bfloat16 [16384, 768], P(('dp', 'store'))
- grad_tokens: bfloat16 [16384, 768], P(('dp', 'store'))
- grad_datastore: float32 [32768, 768], P('store')
- grad_proj_weight: float32 [768, 6, 768], P('store')
- grad_out_weight: float32 [768, 2, 768], P('store')
- grad_proj_bias: float32 [768, 6], P('store')
- grad_norm_gain: float32 [768, 3], P('store')
- grad_norm_bias: float32 [768, 3], P('store')
- grad_inner_weight: float32 [768, 3072], P('store')
- grad_inner_bias: float32 [3072], P('store')
- grad_outer_weight: float32 [3072, 768], P('store')
- grad_outer_bias: float32 [768], P('store')
Inputs may be any that keep to these rules, and one draw needn't show every extreme that they name: `indices`: row numbers of the datastore. Of the 8192 numbers of one sequence, at most 2048 lie in the rows of one store device (o * 4096 to (o + 1) * 4096 - 1), and exactly 2048 lie in those of some device. `lengths`: each is at least 64; some sequence has 512.
All inputs are finite; a program needn't handle non-finite values.
Results may differ from a plain program's by a relative error of at most 0.025.
Values may be sent and summed in bfloat16 or wider, within the bound.
A program may use at most 320 MiB of HBM per device.

v0:
```python
import jax
import jax.numpy as jnp
from jax import lax
from jax.sharding import PartitionSpec as P

D = 768
H = 12
HD = 64
K = 16


EPSILON = 1e-05


def product(matrix, factor):
    return jnp.dot(matrix, factor, preferred_element_type=jnp.float32)


def product_back(matrix, weight):
    return jnp.einsum("tf,df->td", matrix, weight, preferred_element_type=jnp.float32)


def contract_rows(matrix, factor):
    return jnp.einsum("td,tf->df", matrix, factor, preferred_element_type=jnp.float32)


def column_sum(matrix):
    return jnp.sum(matrix.astype(jnp.float32), axis=0)


def norm_forward(hidden, norm_weight, norm_shift):
    centered = hidden - jnp.mean(hidden, axis=-1, keepdims=True)
    inverse = lax.rsqrt(jnp.mean(centered * centered, axis=-1, keepdims=True) + EPSILON)
    normed = centered * inverse
    return (normed * norm_weight + norm_shift, normed, inverse)


def norm_backward(upstream, normed, inverse, norm_weight):
    scaled = upstream * norm_weight
    plain_mean = jnp.mean(scaled, axis=-1, keepdims=True)
    normed_mean = jnp.mean(scaled * normed, axis=-1, keepdims=True)
    return (
        inverse * (scaled - plain_mean - normed * normed_mean),
        jnp.sum(upstream * normed, axis=0),
        jnp.sum(upstream, axis=0),
    )


def log_total(scores):
    highest = jnp.max(scores, axis=-1, keepdims=True)
    return highest + jnp.log(jnp.sum(jnp.exp(scores - highest), axis=-1, keepdims=True))


def route_slots(picked, rows_here, owners, capacity):
    flat_ids = picked.reshape(-1)
    owner_of = flat_ids // rows_here
    local_row = flat_ids % rows_here
    by_owner = jnp.argsort(owner_of, stable=True)
    sorted_owner = owner_of[by_owner]
    owner_loads = jnp.sum(
        (owner_of[:, None] == jnp.arange(owners, dtype=jnp.int32)[None, :]).astype(jnp.int32),
        axis=0,
    )
    starts = jnp.cumsum(owner_loads) - owner_loads
    within = jnp.arange(flat_ids.shape[0], dtype=jnp.int32) - starts[sorted_owner]
    placed = jnp.zeros_like(flat_ids).at[by_owner].set(within)
    target = owner_of * capacity + placed
    request = jnp.zeros((owners * capacity,), jnp.int32).at[target].set(local_row)
    return (target, request.reshape(owners, capacity))


def fetch_rows(request, datastore):
    asked_rows = lax.all_to_all(request, "store", split_axis=0, concat_axis=0, tiled=True)
    found_rows = datastore[asked_rows.reshape(-1)].reshape(asked_rows.shape + (datastore.shape[1],))
    return (
        lax.all_to_all(found_rows, "store", split_axis=0, concat_axis=0, tiled=True),
        asked_rows,
    )


def fetch_again(request, datastore):
    asked_rows = lax.all_to_all(request, "store", split_axis=0, concat_axis=0, tiled=True)
    found_rows = datastore[asked_rows.reshape(-1)].reshape(asked_rows.shape + (datastore.shape[1],))
    return (
        lax.all_to_all(found_rows, "store", split_axis=0, concat_axis=0, tiled=True),
        asked_rows,
    )


def self_scores(queries, self_keys, allowed, score_scale):
    scores = (
        jnp.einsum("qhe,khe->hqk", queries, self_keys, preferred_element_type=jnp.float32)
        * score_scale
    )
    return jnp.where(allowed[None], scores, -1e30)


def body(
    tokens,
    datastore,
    indices,
    lengths,
    proj_weight,
    out_weight,
    proj_bias,
    norm_gain,
    norm_bias,
    inner_weight,
    inner_bias,
    outer_weight,
    outer_bias,
    cotangent,
):
    seq_len = tokens.shape[0]
    score_scale = HD ** (-0.5)
    owners = lax.axis_size("store")
    rows_here = datastore.shape[0]
    capacity = 2 * seq_len * K // owners
    position = jnp.arange(seq_len)
    length = lengths[0]
    allowed = (position[None, :] <= position[:, None]) & (position[None, :] < length)
    valid = (position < length)[:, None]
    target, request = route_slots(indices, rows_here, owners, capacity)
    returned, asked_here = fetch_rows(request, datastore)
    fetched = returned.reshape(owners * capacity, D)[target].reshape(seq_len, K, D)
    self_bias = jnp.concatenate([proj_bias[:, 0], jnp.zeros((D,), jnp.float32), proj_bias[:, 1]])
    self_proj = proj_weight[:, 0:3, :].reshape(D, 3 * D)
    joined = (product(tokens, self_proj) + self_bias).astype(jnp.bfloat16)
    queries = joined[:, :D].reshape(seq_len, H, HD)
    self_keys = joined[:, D : 2 * D].reshape(seq_len, H, HD)
    values = joined[:, 2 * D :].reshape(seq_len, H, HD)
    scores = self_scores(queries, self_keys, allowed, score_scale)
    self_lse = log_total(scores)
    self_probs = jnp.exp(scores - self_lse).astype(jnp.bfloat16)
    self_mixed = (
        jnp.einsum("hqk,khe->qhe", self_probs, values, preferred_element_type=jnp.float32)
        .reshape(seq_len, D)
        .astype(jnp.bfloat16)
    )
    first_pre = tokens.astype(jnp.float32) + (
        product(self_mixed, out_weight[:, 0, :]) + proj_bias[:, 2]
    )
    first_out, first_normed, first_inverse = norm_forward(
        first_pre, norm_gain[:, 0], norm_bias[:, 0]
    )
    first_low = first_out.astype(jnp.bfloat16)
    cross_query = (
        (product(first_low, proj_weight[:, 3, :]) + proj_bias[:, 3])
        .astype(jnp.bfloat16)
        .reshape(seq_len, H, HD)
    )
    key_heads = proj_weight[:, 4, :].reshape(D, H, HD)
    folded = (
        jnp.einsum("the,dhe->thd", cross_query, key_heads, preferred_element_type=jnp.float32)
        * score_scale
    ).astype(jnp.bfloat16)
    cross_scores = jnp.einsum("thd,tkd->thk", folded, fetched, preferred_element_type=jnp.float32)
    cross_lse = log_total(cross_scores)
    cross_full = jnp.exp(cross_scores - cross_lse)
    cross_probs = cross_full.astype(jnp.bfloat16)
    summary = jnp.einsum(
        "thk,tkd->thd", cross_probs, fetched, preferred_element_type=jnp.float32
    ).astype(jnp.bfloat16)
    value_heads = proj_weight[:, 5, :].reshape(D, H, HD)
    cross_mixed = (
        jnp.einsum(
            "thd,dhe->the", summary, value_heads, preferred_element_type=jnp.float32
        ).reshape(seq_len, D)
        + proj_bias[:, 4]
    ).astype(jnp.bfloat16)
    second_pre = first_out + (product(cross_mixed, out_weight[:, 1, :]) + proj_bias[:, 5])
    second_out, second_normed, second_inverse = norm_forward(
        second_pre, norm_gain[:, 1], norm_bias[:, 1]
    )
    second_low = second_out.astype(jnp.bfloat16)
    inner_pre = product(second_low, inner_weight) + inner_bias
    activated = jax.nn.gelu(inner_pre, approximate=False).astype(jnp.bfloat16)
    third_pre = second_out + (product(activated, outer_weight) + outer_bias)
    third_out, third_normed, third_inverse = norm_forward(
        third_pre, norm_gain[:, 2], norm_bias[:, 2]
    )
    output = jnp.where(valid, third_out, 0.0).astype(jnp.bfloat16)
    upstream = jnp.where(valid, cotangent.astype(jnp.float32), 0.0)
    third_grad, gain_three, shift_three = norm_backward(
        upstream, third_normed, third_inverse, norm_gain[:, 2]
    )
    outer_low = third_grad.astype(jnp.bfloat16)
    grad_outer_weight = contract_rows(activated, outer_low)
    grad_outer_bias = column_sum(outer_low)
    act_grad = product_back(outer_low, outer_weight)
    slope = jax.vjp(lambda activation_in: jax.nn.gelu(activation_in, approximate=False), inner_pre)[
        1
    ](act_grad)[0]
    inner_low = slope.astype(jnp.bfloat16)
    grad_inner_weight = contract_rows(second_low, inner_low)
    grad_inner_bias = column_sum(inner_low)
    second_up = third_grad + product_back(inner_low, inner_weight)
    second_grad, gain_two, shift_two = norm_backward(
        second_up, second_normed, second_inverse, norm_gain[:, 1]
    )
    cross_out_low = second_grad.astype(jnp.bfloat16)
    grad_cross_out = contract_rows(cross_mixed, cross_out_low)
    bias_five = column_sum(cross_out_low)
    mixed_low = product_back(cross_out_low, out_weight[:, 1, :]).astype(jnp.bfloat16)
    bias_four = column_sum(mixed_low)
    mixed_heads = mixed_low.reshape(seq_len, H, HD)
    grad_value_heads = jnp.einsum(
        "thd,the->dhe", summary, mixed_heads, preferred_element_type=jnp.float32
    )
    summary_low = jnp.einsum(
        "the,dhe->thd", mixed_heads, value_heads, preferred_element_type=jnp.float32
    ).astype(jnp.bfloat16)
    returned_again, asked_back = fetch_again(request, datastore)
    fetched_back = returned_again.reshape(owners * capacity, D)[target].reshape(seq_len, K, D)
    prob_grad = jnp.einsum(
        "thd,tkd->thk", summary_low, fetched_back, preferred_element_type=jnp.float32
    )
    score_low = (
        cross_full * (prob_grad - jnp.sum(cross_full * prob_grad, axis=-1, keepdims=True))
    ).astype(jnp.bfloat16)
    row_grad = (
        jnp.einsum("thk,thd->tkd", cross_probs, summary_low, preferred_element_type=jnp.float32)
        + jnp.einsum("thk,thd->tkd", score_low, folded, preferred_element_type=jnp.float32)
    ).astype(jnp.bfloat16)
    folded_low = jnp.einsum(
        "thk,tkd->thd", score_low, fetched_back, preferred_element_type=jnp.float32
    ).astype(jnp.bfloat16)
    grad_key_heads = (
        jnp.einsum("thd,the->dhe", folded_low, cross_query, preferred_element_type=jnp.float32)
        * score_scale
    )
    query_low = (
        (
            jnp.einsum("thd,dhe->the", folded_low, key_heads, preferred_element_type=jnp.float32)
            * score_scale
        )
        .astype(jnp.bfloat16)
        .reshape(seq_len, D)
    )
    bias_three = column_sum(query_low)
    grad_cross_query = contract_rows(first_low, query_low)
    grad_buffer = (
        jnp.zeros((owners * capacity, D), jnp.bfloat16)
        .at[target]
        .set(row_grad.reshape(-1, D))
        .reshape(owners, capacity, D)
    )
    arrived = lax.all_to_all(grad_buffer, "store", split_axis=0, concat_axis=0, tiled=True)
    partial_store = (
        jnp.zeros((rows_here, D), jnp.float32)
        .at[asked_back.reshape(-1)]
        .add(arrived.reshape(-1, D).astype(jnp.float32))
    )
    grad_store = lax.psum(partial_store.astype(jnp.bfloat16), "dp").astype(jnp.float32)
    first_up = second_grad + product_back(query_low, proj_weight[:, 3, :])
    first_grad, gain_one, shift_one = norm_backward(
        first_up, first_normed, first_inverse, norm_gain[:, 0]
    )
    self_out_low = first_grad.astype(jnp.bfloat16)
    grad_self_out = contract_rows(self_mixed, self_out_low)
    bias_two = column_sum(self_out_low)
    self_mixed_low = (
        product_back(self_out_low, out_weight[:, 0, :]).astype(jnp.bfloat16).reshape(seq_len, H, HD)
    )
    value_grad = jnp.einsum(
        "hqk,qhe->khe", self_probs, self_mixed_low, preferred_element_type=jnp.float32
    )
    attend_grad = jnp.einsum(
        "qhe,khe->hqk", self_mixed_low, values, preferred_element_type=jnp.float32
    )
    self_full = jnp.exp(self_scores(queries, self_keys, allowed, score_scale) - self_lse)
    self_score_low = (
        self_full * (attend_grad - jnp.sum(self_full * attend_grad, axis=-1, keepdims=True))
    ).astype(jnp.bfloat16)
    query_grad = (
        jnp.einsum("hqk,khe->qhe", self_score_low, self_keys, preferred_element_type=jnp.float32)
        * score_scale
    )
    key_grad = (
        jnp.einsum("hqk,qhe->khe", self_score_low, queries, preferred_element_type=jnp.float32)
        * score_scale
    )
    joined_low = jnp.concatenate(
        [
            query_grad.reshape(seq_len, D),
            key_grad.reshape(seq_len, D),
            value_grad.reshape(seq_len, D),
        ],
        axis=1,
    ).astype(jnp.bfloat16)
    grad_self_proj = contract_rows(tokens, joined_low).reshape(D, 3, D)
    bias_zero = column_sum(joined_low[:, :D])
    bias_one = column_sum(joined_low[:, 2 * D :])
    grad_tokens = (first_grad + product_back(joined_low, self_proj)).astype(jnp.bfloat16)
    grad_proj = jnp.stack(
        [
            grad_self_proj[:, 0],
            grad_self_proj[:, 1],
            grad_self_proj[:, 2],
            grad_cross_query,
            grad_key_heads.reshape(D, D),
            grad_value_heads.reshape(D, D),
        ],
        axis=1,
    )
    grad_out = jnp.stack([grad_self_out, grad_cross_out], axis=1)
    grad_bias = jnp.stack([bias_zero, bias_one, bias_two, bias_three, bias_four, bias_five], axis=1)
    grad_gain = jnp.stack([gain_one, gain_two, gain_three], axis=1)
    grad_shift = jnp.stack([shift_one, shift_two, shift_three], axis=1)
    shares = (
        lax.psum_scatter(
            grad_proj.astype(jnp.bfloat16), "store", scatter_dimension=0, tiled=True
        ).astype(jnp.float32),
        lax.psum_scatter(
            grad_out.astype(jnp.bfloat16), "store", scatter_dimension=0, tiled=True
        ).astype(jnp.float32),
        lax.psum_scatter(
            grad_bias.astype(jnp.bfloat16), "store", scatter_dimension=0, tiled=True
        ).astype(jnp.float32),
        lax.psum_scatter(
            grad_gain.astype(jnp.bfloat16), "store", scatter_dimension=0, tiled=True
        ).astype(jnp.float32),
        lax.psum_scatter(
            grad_shift.astype(jnp.bfloat16), "store", scatter_dimension=0, tiled=True
        ).astype(jnp.float32),
        lax.psum_scatter(
            grad_inner_weight.astype(jnp.bfloat16), "store", scatter_dimension=0, tiled=True
        ).astype(jnp.float32),
        lax.psum_scatter(
            grad_inner_bias.astype(jnp.bfloat16), "store", scatter_dimension=0, tiled=True
        ).astype(jnp.float32),
        lax.psum_scatter(
            grad_outer_weight.astype(jnp.bfloat16), "store", scatter_dimension=0, tiled=True
        ).astype(jnp.float32),
        lax.psum_scatter(
            grad_outer_bias.astype(jnp.bfloat16), "store", scatter_dimension=0, tiled=True
        ).astype(jnp.float32),
    )
    totals = (
        lax.psum(shares[0].astype(jnp.bfloat16), "dp").astype(jnp.float32),
        lax.psum(shares[1].astype(jnp.bfloat16), "dp").astype(jnp.float32),
        lax.psum(shares[2].astype(jnp.bfloat16), "dp").astype(jnp.float32),
        lax.psum(shares[3].astype(jnp.bfloat16), "dp").astype(jnp.float32),
        lax.psum(shares[4].astype(jnp.bfloat16), "dp").astype(jnp.float32),
        lax.psum(shares[5].astype(jnp.bfloat16), "dp").astype(jnp.float32),
        lax.psum(shares[6].astype(jnp.bfloat16), "dp").astype(jnp.float32),
        lax.psum(shares[7].astype(jnp.bfloat16), "dp").astype(jnp.float32),
        lax.psum(shares[8].astype(jnp.bfloat16), "dp").astype(jnp.float32),
    )
    return (
        output,
        grad_tokens,
        grad_store,
        totals[0],
        totals[1],
        totals[2],
        totals[3],
        totals[4],
        totals[5],
        totals[6],
        totals[7],
        totals[8],
    )


def solution(mesh):
    in_specs = (
        P(("dp", "store"), None),
        P("store", None),
        P(("dp", "store"), None),
        P(("dp", "store")),
        P(),
        P(),
        P(),
        P(),
        P(),
        P(),
        P(),
        P(),
        P(),
        P(("dp", "store"), None),
    )
    out_specs = (
        P(("dp", "store"), None),
        P(("dp", "store"), None),
        P("store", None),
        P("store", None, None),
        P("store", None, None),
        P("store", None),
        P("store", None),
        P("store", None),
        P("store", None),
        P("store"),
        P("store", None),
        P("store"),
    )
    return jax.shard_map(body, mesh=mesh, in_specs=in_specs, out_specs=out_specs, check_vma=False)
```

profile of v0, /device:TPU:0, one launch (start us, length us, event | category | flops | bytes accessed | tf_op | source)
XLA Modules:
  0.0 2314.0 jit_solution(18013853540505534460)
XLA Ops:
  9.2 6.8 sort.17
  16.0 45.5 %gather_fusion = s32[8192]{0:T(1024)S(1)} fusion(s32[8192]{0:T(1024)S(1)} %add_select_fusion.1, s32[8192]{0:T(1024)S(1)} %get-tuple-element.129), kind=kCustom, calls=%fused_computation | custom fusion | bytes 98304 | tf_op jit(solution)/shard_map/gather | solution.py:59
  61.7 4.7 compare_select_fusion.2
  67.0 30.5 %scatter_custom_fusion = s32[8192]{0:T(1024)S(1)} fusion(s32[8192]{0:T(1024)S(1)} %get-tuple-element.130, s32[8192]{0:T(1024)S(1)} %select_subtract_fusion, s32[]{:T(128)} %constant.53.clone.1), kind=kCustom, calls=%fused_computation.157 | custom fusion | bytes 32772 | tf_op jit(solution)/shard_map/scatter | solution.py:66
  98.2 30.5 %scatter_custom_fusion.1 = s32[16384]{0:T(1024)S(1)} fusion(s32[8192]{0:T(1024)S(1)} %get-tuple-element.119, s32[8192]{0:T(1024)S(1)} %get-tuple-element.128, s32[]{:T(128)} %constant.53.clone.1), kind=kCustom, calls=%fused_computation.150 | custom fusion | bytes 65540 | tf_op jit(solution)/shard_map/scatter | solution.py:68
  128.6 14.0 all_to_all.21
  143.3 76.6 %gather_fusion.1 = bf16[16384,768]{1,0:T(8,128)(2,1)} fusion(bf16[4096,768]{1,0:T(8,128)(2,1)} %param.15, s32[16384]{0:T(1024)S(1)} %broadcast_clamp_fusion), kind=kCustom, calls=%fused_computation.1 | custom fusion | bytes 50397184 | tf_op jit(solution)/shard_map/gather | solution.py:74
  220.0 6.9 all-to-all-start.1
  228.7 3.3 fusion.74
  232.1 2.4 copy.155
  236.8 3.7 copy.188
  240.5 4.3 fusion.22
  248.3 2.6 exponential_reduce_fusion
  252.8 3.7 convolution_convert_fusion.10
  256.5 4.6 fusion.75
  265.2 6.6 fusion.13
  271.8 496.5 %all-to-all-done.1 = bf16[8,2048,768]{2,1,0:T(8,128)(2,1)} async-done(((bf16[8,2048,768]{2,1,0:T(8,128)(2,1)}), bf16[8,2048,768]{2,1,0:T(8,128)(2,1)}, u32[]{:S(2)}, u32[]{:S(2)}) %all-to-all-start.1) | async-done | bytes 25165856 | tf_op jit(solution)/shard_map/all_to_all | solution.py:76
  768.3 48.4 %gather_fusion.2 = bf16[8192,768]{1,0:T(8,128)(2,1)} fusion(bf16[16384,768]{1,0:T(8,128)(2,1)} %bitcast.28, s32[8192]{0:T(1024)S(1)} %copy-done.43), kind=kCustom, calls=%fused_computation.2 | custom fusion | bytes 25198592 | tf_op jit(solution)/shard_map/gather | solution.py:125
  816.7 13.7 fusion.79
  830.4 14.1 exponential_reduce_fusion.1
  844.5 11.7 fusion.43
  856.3 11.5 fusion.27
  869.3 20.2 multiply_convert_fusion.2
  889.6 2.8 fusion.81
  896.2 9.9 fusion.83
  906.2 7.0 multiply_reduce_fusion.3
  917.2 5.0 convert_bitcast_fusion
  922.2 16.5 multiply_reduce_fusion.1
  938.7 16.4 fusion.2
  955.1 6.7 multiply_convert_fusion.3
  961.8 20.7 add_convert_fusion
  982.6 50.4 %scatter_custom_fusion.2 = bf16[16384,768]{1,0:T(8,128)(2,1)} fusion(s32[8192]{0:T(1024)} %copy-done.46, bf16[8192,768]{1,0:T(8,128)(2,1)} %bitcast.159, bf16[]{:T(256)} %constant.136.clone.1), kind=kCustom, calls=%fused_computation.21 | custom fusion | bytes 25166336 | tf_op jit(solution)/shard_map/scatter | solution.py:245
  1033.0 6.5 all-to-all-start.2
  1039.6 12.5 fusion.84
  1052.2 11.0 bitcast_reduce_fusion.2
  1063.2 3.7 multiply_reduce_fusion.4
  1072.0 6.7 convolution_convert_fusion
  1080.1 6.6 convolution_convert_fusion.1
  1087.9 11.0 convolution_convert_fusion.6
  1098.9 2.8 copy.174
  1101.7 11.0 multiply_convert_fusion.4
  1112.7 2.5 copy.173
  1115.1 2.5 convolution_convert_fusion.7
  1118.0 11.0 multiply_reduce_fusion
  1130.6 7.3 multiply_convert_fusion.1
  1141.2 4.0 bitcast_reduce_fusion
  1145.1 3.8 convolution_convert_fusion.2
  1148.9 4.3 copy.172
  1153.2 2.8 fusion.31
  1156.1 3.7 pad_maximum_fusion
  1163.7 445.0 %all-to-all-done.2 = bf16[8,2048,768]{2,1,0:T(8,128)(2,1)} async-done(((bf16[8,2048,768]{2,1,0:T(8,128)(2,1)}), bf16[8,2048,768]{2,1,0:T(8,128)(2,1)}, u32[]{:S(2)}, u32[]{:S(2)}) %all-to-all-start.2) | async-done | bytes 25165856 | tf_op jit(solution)/shard_map/all_to_all | solution.py:248
  1608.7 119.2 %scatter_custom_fusion.3 = f32[4096,768]{1,0:T(8,128)} fusion(s32[16384]{0:T(1024)} %bitcast.190, bf16[16384,768]{1,0:T(8,128)(2,1)} %bitcast.66, f32[]{:T(128)} %constant.47.clone.1), kind=kCustom, calls=%fused_computation.7 | custom fusion | flops 25165824 | bytes 37749248 | tf_op jit(solution)/shard_map/scatter-add | solution.py:252
  1727.9 8.0 convert_element_type.234
  1735.9 70.8 %reduce-scatter.18.cloned.1.call-done = bf16[96,3072]{1,0:T(8,128)(2,1)} async-done(((bf16[768,3072]{1,0:T(8,128)(2,1)}), bf16[96,3072]{1,0:T(8,128)(2,1)}) %reduce-scatter.18.cloned.1.call-update) | async-done | bytes 589840 | tf_op jit(solution)/shard_map/reduce_scatter | solution.py:326
  1806.7 132.4 %reduce-scatter.14.cloned.1.call-done = bf16[96,6,768]{2,0,1:T(8,128)(2,1)} async-done(((bf16[768,6,768]{2,0,1:T(8,128)(2,1)}), bf16[96,6,768]{2,0,1:T(8,128)(2,1)}) %reduce-scatter.14.cloned.1.call-update) | async-done | bytes 884752 | tf_op jit(solution)/shard_map/reduce_scatter | solution.py:311
  1941.6 20.0 all-reduce.2
  1961.8 5.2 add_convert_fusion.2
  1967.0 36.4 %reduce-scatter.26.cloned.1.call-done = bf16[96,3]{1,0:T(8,128)(2,1)} async-done(((bf16[768,3]{1,0:T(8,128)(2,1)}), bf16[96,3]{1,0:T(8,128)(2,1)}) %reduce-scatter.26.cloned.1.call-update) | async-done | bytes 592
  2004.2 63.9 %reduce-scatter.24.cloned.1.call-done = bf16[96,3]{1,0:T(8,128)(2,1)} async-done(((bf16[768,3]{1,0:T(8,128)(2,1)}), bf16[96,3]{1,0:T(8,128)(2,1)}) %reduce-scatter.24.cloned.1.call-update) | async-done | bytes 592
  2068.8 64.1 %reduce-scatter.22.cloned.1.call-done = bf16[96,6]{1,0:T(8,128)(2,1)} async-done(((bf16[768,6]{1,0:T(8,128)(2,1)}), bf16[96,6]{1,0:T(8,128)(2,1)}) %reduce-scatter.22.cloned.1.call-update) | async-done | bytes 1168
  2133.7 5.7 all-reduce.3
  2142.3 149.8 %all-reduce.7.cloned.1.call-done = (bf16[96,2,768]{2,0,1:T(8,128)(2,1)}, bf16[4096,768]{1,0:T(8,128)(2,1)}, bf16[96,6,768]{2,0,1:T(8,128)(2,1)}, bf16[96,3072]{1,0:T(8,128)(2,1)}, bf16[384,768]{1,0:T(8,128)(2,1)}) async-done(((bf16[96,2,768]{2,0,1:T(8,128)(2,1)}, bf16[4096,768]{1,0:T(8,128)(2,1)}, bf16[96,6,768]{2,0,1:T(8,128)(2,1)}, bf16[96,3072]{1,0:T(8,128)(2,1)}, bf16[384,768]{1,0:T(8,128)(2,1)}), ...) | async-done | bytes 8650768 | tf_op jit(solution)/shard_map/psum | solution.py:341
  2298.6 2.5 convert_element_type.236
  2301.2 5.8 convert_element_type.235
  (287 shorter events, 56.0 us)
Async XLA Ops:
  98.2 121.8 %copy-start.46 = (s32[8192]{0:T(1024)}, s32[8192]{0:T(1024)S(1)}, u32[]{:S(2)}) copy-start(s32[8192]{0:T(1024)S(1)} %get-tuple-element.119) | copy-start | bytes 98308
  220.0 7.5 copy-start.51
  220.0 548.3 %all-to-all-start.1 = ((bf16[8,2048,768]{2,1,0:T(8,128)(2,1)}), bf16[8,2048,768]{2,1,0:T(8,128)(2,1)}, u32[]{:S(2)}, u32[]{:S(2)}) async-start(bf16[8,2048,768]{2,1,0:T(8,128)(2,1)} %bitcast.158), calls=%async_computation.1 | async-start | bytes 50331648 | tf_op jit(solution)/shard_map/all_to_all | solution.py:76
  228.7 8.1 slice-start.3
  245.9 5.0 copy-start.22
  246.0 621.8 %copy-start.49 = (f32[768]{0:T(1024)}, f32[768]{0:T(1024)S(1)}, u32[]{:S(2)}) copy-start(f32[768]{0:T(1024)S(1)} %get-tuple-element.169) | copy-start | bytes 9220
  246.0 621.8 %copy-start.64 = (f32[768]{0:T(1024)}, f32[768]{0:T(1024)S(1)}, u32[]{:S(2)}) copy-start(f32[768]{0:T(1024)S(1)} %get-tuple-element.96) | copy-start | bytes 9220
  246.1 4.7 copy-start.8
  248.3 4.5 copy-start
  252.8 3.7 copy-start.5
  256.5 4.7 copy-start.36
  256.5 4.7 copy-start.67
  256.5 4.7 copy-start.73
  262.1 605.7 %copy-start.14 = (f32[512,768]{1,0:T(8,128)}, f32[512,768]{1,0:T(8,128)S(1)}, u32[]{:S(2)}) copy-start(f32[512,768]{1,0:T(8,128)S(1)} %get-tuple-element.142) | copy-start | bytes 4718596
  262.2 605.7 %copy-start.47 = (f32[512]{0:T(512)}, f32[512]{0:T(512)S(1)}, u32[]{:S(2)}) copy-start(f32[512]{0:T(512)S(1)} %broadcast_multiply_fusion.8) | copy-start | bytes 6148
  262.5 605.3 %copy-start.52 = (f32[512]{0:T(512)}, f32[512]{0:T(512)S(1)}, u32[]{:S(2)}) copy-start(f32[512]{0:T(512)S(1)} %add_rsqrt_fusion.2) | copy-start | bytes 6148
  265.2 6.6 copy-start.24
  265.2 503.1 %copy-start.43 = (s32[8192]{0:T(1024)S(1)}, s32[8192]{0:T(1024)}, u32[]{:S(2)}) copy-start(s32[8192]{0:T(1024)} %get-tuple-element.118) | copy-start | bytes 98308
  830.4 25.9 %copy-start.1 = (f32[512,12,16]{2,1,0:T(8,128)}, f32[512,12,16]{2,1,0:T(8,128)S(1)}, u32[]{:S(2)}) copy-start(f32[512,12,16]{2,1,0:T(8,128)S(1)} %get-tuple-element.144) | copy-start | bytes 1179652
  856.3 11.5 copy-start.32
  856.3 11.5 copy-start.65
  867.8 21.7 slice-start.4
  869.0 44.3 %copy-start.16 = (f32[512,768]{1,0:T(8,128)}, f32[512,768]{1,0:T(8,128)S(1)}, u32[]{:S(2)}) copy-start(f32[512,768]{1,0:T(8,128)S(1)} %get-tuple-element.148) | copy-start | bytes 4718596
  869.3 20.3 slice-start.5
  869.3 20.3 copy-start.76
  889.6 3.2 copy-start.28
  896.2 10.0 copy-start.34
  913.2 4.0 copy-start.21
  917.2 5.1 copy-start.26
  938.7 16.4 copy-start.2
  1033.0 575.7 %all-to-all-start.2 = ((bf16[8,2048,768]{2,1,0:T(8,128)(2,1)}), bf16[8,2048,768]{2,1,0:T(8,128)(2,1)}, u32[]{:S(2)}, u32[]{:S(2)}) async-start(bf16[8,2048,768]{2,1,0:T(8,128)(2,1)} %bitcast.157), calls=%async_computation.2 | async-start | bytes 50331648 | tf_op jit(solution)/shard_map/all_to_all | solution.py:248
  1039.5 696.3 %reduce-scatter.16.cloned.1.call-start = ((), (), s32[]{:S(2)}) async-start(), calls=%async_computation.11 | async-start | bytes 2654208 | tf_op jit(solution)/shard_map/reduce_scatter | solution.py:314
  1052.1 11.1 copy-start.13
  1052.2 11.1 copy-start.15
  1052.2 11.1 copy-start.48
  1052.2 11.1 copy-start.50
  1052.2 11.1 copy-start.53
  1063.2 3.7 copy-start.78
  1063.2 3.7 copy-start.33
  1063.2 3.7 copy-start.45
  1069.0 46.1 %copy-start.10 = (f32[512,768]{1,0:T(8,128)}, f32[512,768]{1,0:T(8,128)S(1)}, u32[]{:S(2)}) copy-start(f32[512,768]{1,0:T(8,128)S(1)} %get-tuple-element.115) | copy-start | bytes 4718596
  1071.7 664.2 %reduce-scatter.20.cloned.1.call-start = ((), (), s32[]{:S(2)}) async-start(), calls=%async_computation.13 | async-start | bytes 5308416 | tf_op jit(solution)/shard_map/reduce_scatter | solution.py:332
  1078.7 728.0 %reduce-scatter.18.cloned.1.call-start = ((), (), s32[]{:S(2)}) async-start(), calls=%async_computation.12 | async-start | bytes 5308416 | tf_op jit(solution)/shard_map/reduce_scatter | solution.py:326
  1086.8 14.9 copy-start.25
  1086.8 852.3 %reduce-scatter.14.cloned.1.call-start = ((), (), s32[]{:S(2)}) async-start(), calls=%async_computation.10 | async-start | bytes 7962624 | tf_op jit(solution)/shard_map/reduce_scatter | solution.py:311
  1112.7 5.3 copy-start.9
  1112.7 5.3 copy-start.23
  1112.7 5.3 copy-start.41
  1117.9 11.1 slice-start
  1118.0 11.0 slice-start.1
  1118.0 12.6 slice-start.2
  1130.6 7.3 copy-start.7
  1139.9 5.2 copy-start.38
  1141.1 4.0 copy-start.29
  1141.2 4.0 copy-start.74
  1145.1 3.8 copy-start.77
  1159.9 843.5 %reduce-scatter.26.cloned.1.call-start = ((), (), s32[]{:S(2)}) async-start(), calls=%async_computation.16 | async-start | bytes 221184
  1161.4 906.6 %reduce-scatter.24.cloned.1.call-start = ((), (), s32[]{:S(2)}) async-start(), calls=%async_computation.15 | async-start | bytes 221184
  1162.4 970.5 %reduce-scatter.22.cloned.1.call-start = ((), (), s32[]{:S(2)}) async-start(), calls=%async_computation.14 | async-start | bytes 221184
  1163.7 1128.4 %all-reduce.7.cloned.1.call-start = ((), (), s32[]{:S(2)}) async-start(), calls=%async_computation.17 | async-start | bytes 17301504 | tf_op jit(solution)/shard_map/psum | solution.py:341
  1939.1 22.7 copy-start.11
  1939.1 22.7 copy-start.30
  1939.1 22.7 copy-start.39
  2292.1 9.1 copy-start.18
  (33 other events, 56.8 us)
Sparse Core Ops, SparseCore 0:
  1071.8 497.1 reduce-scatter.15
  1572.7 135.0 reduce-scatter.19
  1711.4 95.2 reduce-scatter.17
  1810.2 128.7 reduce-scatter.13
  1942.2 61.1 reduce-scatter.25
  2007.0 60.9 reduce-scatter.23
  2071.9 61.0 reduce-scatter.21
  2135.9 156.1 all-reduce.6
where the time goes:
time: 2320 us; the launch traced here: 2310 us
  waiting for transfers between devices  1460 us (63%)
  local copies, waits for them, and re-layouts  330 us (14%)
  matrix products  255 us (11%)
  other arithmetic  199 us (9%)
  blocking collectives  39.7 us (2%)
    all_to_all x1, waiting for transfers between devices, fetch_rows(): lax.all_to_all(found_rows, 'store', split_axis=0, concat_axis=0, tiled=True)  496 us
    all_to_all x1, waiting for transfers between devices, body(): lax.all_to_all(grad_buffer, 'store', split_axis=0, concat_axis=0, tiled=T...  445 us
    unnamed x11, waiting for transfers between devices  164 us
    psum x1, waiting for transfers between devices, body(): lax.psum(shares[1].astype(jnp.bfloat16), 'dp').astype(jnp.float32)  150 us
    reduce_scatter x1, waiting for transfers between devices, body(): lax.psum_scatter(grad_proj.astype(jnp.bfloat16), 'store', scatter_dimensi...  132 us
    scatter-add x1, other arithmetic, body(): partial_store = jnp.zeros((rows_here, D), jnp.float32).at[asked_back.resh...  119 us
    gather x1, local copies, waits for them, and re-layouts, fetch_rows(): datastore[asked_rows.reshape(-1)]  76.6 us
    reduce_scatter x1, waiting for transfers between devices, body(): lax.psum_scatter(grad_inner_weight.astype(jnp.bfloat16), 'store', scatter...  70.8 us
  transfers between devices with their start and end apart: 10, of which 8 were waited for; matrix products, arithmetic and copies ran while one was open for 13% of the time, Pallas kernels for 0%

commit v1 on v0

--- a/solution.py
+++ b/solution.py
@@ -93,6 +93,78 @@
         * score_scale
     )
     return jnp.where(allowed[None], scores, -1e30)
+
+
+DENSE_LIMIT = 1 << 16
+
+
+def is_dense(owners, rows_here):
+    return owners * rows_here <= DENSE_LIMIT
+
+
+def gather_store(datastore):
+    copies = lax.axis_size("dp")
+    part = datastore.shape[0] // copies
+    mine = lax.dynamic_slice_in_dim(datastore, lax.axis_index("dp") * part, part, axis=0)
+    return lax.all_gather(mine, ("store", "dp"), axis=0, tiled=True)
+
+
+def reduce_store(indices, row_grad, rows):
+    partial = (
+        jnp.zeros((rows, D), jnp.float32)
+        .at[indices.reshape(-1)]
+        .add(row_grad.reshape(-1, D).astype(jnp.float32))
+    )
+    share = lax.psum_scatter(
+        partial.astype(jnp.bfloat16), ("store", "dp"), scatter_dimension=0, tiled=True
+    )
+    return lax.all_gather(share, "dp", axis=0, tiled=True).astype(jnp.float32)
+
+
+def reduce_weights(squares, inner, outer, features, inner_bias):
+    owners = lax.axis_size("store")
+    part = D // owners
+    wide = inner.shape[1] // D
+    low = [square.astype(jnp.bfloat16).reshape(owners, part, D) for square in squares]
+    low += [
+        inner[:, block * D : (block + 1) * D].astype(jnp.bfloat16).reshape(owners, part, D)
+        for block in range(wide)
+    ]
+    low.append(outer.astype(jnp.bfloat16).reshape(owners, wide * part, D))
+    small = jnp.concatenate(
+        [feature.astype(jnp.bfloat16).reshape(owners, part) for feature in features]
+        + [inner_bias.astype(jnp.bfloat16).reshape(owners, wide * part)],
+        axis=1,
+    )
+    small = jnp.pad(small, ((0, 0), (0, 64 * D - small.shape[1]))).reshape(owners, 64, D)
+    packed = jnp.concatenate(low + [small], axis=1)
+    share = lax.psum_scatter(
+        packed.reshape(-1, D), ("store", "dp"), scatter_dimension=0, tiled=True
+    )
+    total = lax.all_gather(share, "dp", axis=0, tiled=True).astype(jnp.float32)
+    count = len(squares)
+    blocks = total[: (count + 2 * wide) * part].reshape(count + 2 * wide, part, D)
+    grad_proj = jnp.transpose(blocks[:6], (1, 0, 2))
+    grad_out = jnp.transpose(blocks[6:8], (1, 0, 2))
+    grad_inner = jnp.transpose(blocks[8 : 8 + wide], (1, 0, 2)).reshape(part, wide * D)
+    grad_outer = blocks[8 + wide :].reshape(wide * part, D)
+    tail = total[(count + 2 * wide) * part :].reshape(-1)
+    table = tail[: len(features) * part].reshape(len(features), part)
+    grad_bias = jnp.transpose(table[0:6])
+    grad_gain = jnp.transpose(table[6:9])
+    grad_shift = jnp.transpose(table[9:12])
+    grad_inner_bias = tail[len(features) * part :][: wide * part]
+    return (
+        grad_proj,
+        grad_out,
+        grad_bias,
+        grad_gain,
+        grad_shift,
+        grad_inner,
+        grad_inner_bias,
+        grad_outer,
+        table[12],
+    )
 
 
 def body(
@@ -120,9 +192,14 @@
     length = lengths[0]
     allowed = (position[None, :] <= position[:, None]) & (position[None, :] < length)
     valid = (position < length)[:, None]
-    target, request = route_slots(indices, rows_here, owners, capacity)
-    returned, asked_here = fetch_rows(request, datastore)
-    fetched = returned.reshape(owners * capacity, D)[target].reshape(seq_len, K, D)
+    dense = is_dense(owners, rows_here)
+    if dense:
+        full_store = gather_store(datastore)
+        fetched = full_store[indices.reshape(-1)].reshape(seq_len, K, D)
+    else:
+        target, request = route_slots(indices, rows_here, owners, capacity)
+        returned, asked_here = fetch_rows(request, datastore)
+        fetched = returned.reshape(owners * capacity, D)[target].reshape(seq_len, K, D)
     self_bias = jnp.concatenate([proj_bias[:, 0], jnp.zeros((D,), jnp.float32), proj_bias[:, 1]])
     self_proj = proj_weight[:, 0:3, :].reshape(D, 3 * D)
     joined = (product(tokens, self_proj) + self_bias).astype(jnp.bfloat16)
@@ -210,8 +287,11 @@
     summary_low = jnp.einsum(
         "the,dhe->thd", mixed_heads, value_heads, preferred_element_type=jnp.float32
     ).astype(jnp.bfloat16)
-    returned_again, asked_back = fetch_again(request, datastore)
-    fetched_back = returned_again.reshape(owners * capacity, D)[target].reshape(seq_len, K, D)
+    if dense:
+        fetched_back = fetched
+    else:
+        returned_again, asked_back = fetch_again(request, datastore)
+        fetched_back = returned_again.reshape(owners * capacity, D)[target].reshape(seq_len, K, D)
     prob_grad = jnp.einsum(
         "thd,tkd->thk", summary_low, fetched_back, preferred_element_type=jnp.float32
     )
@@ -239,19 +319,22 @@
     )
     bias_three = column_sum(query_low)
     grad_cross_query = contract_rows(first_low, query_low)
-    grad_buffer = (
-        jnp.zeros((owners * capacity, D), jnp.bfloat16)
-        .at[target]
-        .set(row_grad.reshape(-1, D))
-        .reshape(owners, capacity, D)
-    )
-    arrived = lax.all_to_all(grad_buffer, "store", split_axis=0, concat_axis=0, tiled=True)
-    partial_store = (
-        jnp.zeros((rows_here, D), jnp.float32)
-        .at[asked_back.reshape(-1)]
-        .add(arrived.reshape(-1, D).astype(jnp.float32))
-    )
-    grad_store = lax.psum(partial_store.astype(jnp.bfloat16), "dp").astype(jnp.float32)
+    if dense:
+        grad_store = reduce_store(indices, row_grad, owners * rows_here)
+    else:
+        grad_buffer = (
+            jnp.zeros((owners * capacity, D), jnp.bfloat16)
+            .at[target]
+            .set(row_grad.reshape(-1, D))
+            .reshape(owners, capacity, D)
+        )
+        arrived = lax.all_to_all(grad_buffer, "store", split_axis=0, concat_axis=0, tiled=True)
+        partial_store = (
+            jnp.zeros((rows_here, D), jnp.float32)
+            .at[asked_back.reshape(-1)]
+            .add(arrived.reshape(-1, D).astype(jnp.float32))
+        )
+        grad_store = lax.psum(partial_store.astype(jnp.bfloat16), "dp").astype(jnp.float32)
     first_up = second_grad + product_back(query_low, proj_weight[:, 3, :])
     first_grad, gain_one, shift_one = norm_backward(
         first_up, first_normed, first_inverse, norm_gain[:, 0]
@@ -292,6 +375,28 @@
     bias_zero = column_sum(joined_low[:, :D])
     bias_one = column_sum(joined_low[:, 2 * D :])
     grad_tokens = (first_grad + product_back(joined_low, self_proj)).astype(jnp.bfloat16)
+    if dense:
+        squares = (
+            grad_self_proj[:, 0],
+            grad_self_proj[:, 1],
+            grad_self_proj[:, 2],
+            grad_cross_query,
+            grad_key_heads.reshape(D, D),
+            grad_value_heads.reshape(D, D),
+            grad_self_out,
+            grad_cross_out,
+        )
+        biases = (bias_zero, bias_one, bias_two, bias_three, bias_four, bias_five)
+        gains = (gain_one, gain_two, gain_three)
+        shifts = (shift_one, shift_two, shift_three)
+        shares = reduce_weights(
+            squares,
+            grad_inner_weight,
+            grad_outer_weight,
+            biases + gains + shifts + (grad_outer_bias,),
+            grad_inner_bias,
+        )
+        return (output, grad_tokens, grad_store) + shares
     grad_proj = jnp.stack(
         [
             grad_self_proj[:, 0],

time: 2320 us -> 1520 us (0.66)
  waiting for transfers between devices: 1460 us -> 717 us
  local copies, waits for them, and re-layouts: 330 us -> 246 us
  other arithmetic: 199 us -> 277 us
  blocking collectives: 39.7 us -> 0 us
    all_to_all x2 -> x0, waiting for transfers between devices: 941 us -> none  [the longest x1 496 us: fetch_rows(): lax.all_to_all(found_rows, 'store', split_axis=0, concat_axis=0, tiled=True)]
    all_gather x0 -> x3, waiting for transfers between devices: none -> 289 us  [the longest x1 231 us: gather_store(): return lax.all_gather(mine, ('store', 'dp'), axis=0, tiled=True)]
    reduce_scatter x4 -> x2, waiting for transfers between devices: 203 us -> 427 us  [the longest x1 427 us: reduce_store(): lax.psum_scatter(partial.astype(jnp.bfloat16), ('store', 'dp'), scatter_d...]
    unnamed x11 -> x5, waiting for transfers between devices: 164 us -> 0.56 us
    psum x1 -> x0, waiting for transfers between devices: 150 us -> none  [body(): lax.psum(shares[1].astype(jnp.bfloat16), 'dp').astype(jnp.float32)]
    scatter x3 -> x0, local copies, waits for them, and re-layouts: 111 us -> none  [the longest x1 50.4 us: body(): grad_buffer = jnp.zeros((owners * capacity, D), jnp.bfloat16).at[target]....]
    scatter-add x1 -> x3, other arithmetic: 119 us -> 168 us  [reduce_store(): partial = jnp.zeros((rows, D), jnp.float32).at[indices.reshape(-1)].add(r...]
    convert_element_type x10 -> x3, other arithmetic: 23.4 us -> 71.3 us  [the longest x1 48.4 us: reduce_store(): partial.astype(jnp.bfloat16)]
  transfers between devices with their start and end apart: 10 -> 5, of which waited for: 8 -> 4; matrix products, arithmetic and copies ran while one was open for 13% -> 22% of each run, Pallas kernels for 0% -> 0%
where the time goes in v1:
time: 1520 us; the launch traced here: 1510 us
  waiting for transfers between devices  717 us (47%)
  other arithmetic  277 us (18%)
  matrix products  257 us (17%)
  local copies, waits for them, and re-layouts  246 us (16%)
  between operations  15.8 us (1%)
    reduce_scatter x1, waiting for transfers between devices, reduce_store(): lax.psum_scatter(partial.astype(jnp.bfloat16), ('store', 'dp'), scatter_d...  427 us
    all_gather x1, waiting for transfers between devices, gather_store(): return lax.all_gather(mine, ('store', 'dp'), axis=0, tiled=True)  231 us
    scatter-add x3, other arithmetic, reduce_store(): partial = jnp.zeros((rows, D), jnp.float32).at[indices.reshape(-1)].add(r...  168 us
    gather x1, local copies, waits for them, and re-layouts, body(): fetched = full_store[indices.reshape(-1)].reshape(seq_len, K, D)  141 us
    convert_element_type x1, other arithmetic, reduce_store(): partial.astype(jnp.bfloat16)  48.4 us
    unnamed x198, local copies, waits for them, and re-layouts  40 us
    all_gather x1, waiting for transfers between devices, reduce_store(): return lax.all_gather(share, 'dp', axis=0, tiled=True).astype(jnp.float32)  38.3 us
    dot_general x6, matrix products, product(): return jnp.dot(matrix, factor, preferred_element_type=jnp.float32)  31 us
  transfers between devices with their start and end apart: 5, of which 4 were waited for; matrix products, arithmetic and copies ran while one was open for 22% of the time, Pallas kernels for 0%

profile of v1, /device:TPU:0, one launch (start us, length us, event | category | flops | bytes accessed | tf_op | source)
XLA Modules:
  0.0 1512.1 jit_solution(7419862620713482006)
XLA Ops:
  7.2 2.7 constant_dynamic-slice_fusion
  13.4 3.0 copy-done.2
  18.0 2.8 copy.101
  20.7 2.4 copy.105
  23.2 3.7 copy.131
  26.9 4.3 fusion.23
  33.2 2.1 fusion.14
  35.3 2.6 exponential_reduce_fusion
  39.8 3.4 convolution_convert_fusion.10
  43.2 4.7 fusion.72
  50.1 2.2 add_convert_fusion.3
  53.3 5.1 fusion.15
  58.4 230.6 %all-gather.4.cloned.1.call-done = bf16[32768,768]{1,0:T(8,128)(2,1)} async-done(((bf16[1024,768]{1,0:T(8,128)(2,1)}), bf16[32768,768]{1,0:T(8,128)(2,1)}) %all-gather.4.cloned.1.call-update) | async-done | bytes 50331664 | tf_op jit(solution)/shard_map/all_gather | solution.py:109
  289.0 141.3 %gather_fusion = bf16[8192,768]{1,0:T(8,128)(2,1)} fusion(bf16[32768,768]{1,0:T(8,128)(2,1)} %all-gather.4.cloned.1.call-done, s32[8192]{0:T(1024)S(1)} %broadcast_clamp_fusion.1), kind=kCustom, calls=%fused_computation | custom fusion | bytes 25198592 | tf_op jit(solution)/shard_map/gather | solution.py:198
  430.3 13.7 fusion.75
  444.0 14.1 exponential_reduce_fusion.1
  458.2 12.0 fusion.43
  470.3 11.2 fusion.28
  483.0 19.6 %multiply_convert_fusion.2 = (bf16[512,3072]{1,0:T(8,128)(2,1)S(1)}, f32[512,3072]{1,0:T(8,128)}, f32[512,3072]{1,0:T(8,128)}) fusion(f32[3072]{0:T(1024)S(1)} %copy-done.75, bf16[768,3072]{1,0:T(8,128)(2,1)} %param.23, f32[512,768]{1,0:T(8,128)S(1)} %get-tuple-element.74, f32[768]{0:T(1024)S(1)} %copy-done.68, f32[768]{0:T(1024)S(1)} %get-tuple-element.94, ...), kind=kOutput, calls=%fused_computation.31 | convolution fusion | flops 2521694208 | bytes 22042624 | tf_op jit(solution)/shard_map/dot_general | solution.py:16
  502.7 2.8 fusion.77
  505.9 2.3 multiply_reduce_fusion.2
  509.4 4.3 convolution_convert_fusion
  513.7 9.4 fusion.79
  523.1 5.9 multiply_reduce_fusion.3
  529.0 5.2 convolution_convert_fusion.1
  536.5 2.3 fusion.78
  540.2 11.0 fusion.32
  551.2 5.0 convert_bitcast_fusion
  556.2 15.5 %multiply_reduce_fusion.1 = (f32[512,12]{1,0:T(8,128)S(1)}, f32[512,12,16]{2,1,0:T(8,128)}) fusion(f32[512,12,16]{2,1,0:T(8,128)} %copy-done.1, f32[512,12]{1,0:T(8,128)S(1)} %log_add_fusion, bf16[512,16,768]{2,1,0:T(8,128)(2,1)} %bitcast.157, bf16[512,12,768]{2,0,1:T(8,128)(2,1)} %convert_bitcast_fusion), kind=kOutput, calls=%fused_computation.51 | convolution fusion | flops 151283712 | bytes 22855680 | tf_op jit(solution)/shard_map/thd,tkd->thk/dot_general | solution.py:295
  571.7 6.3 multiply_convert_fusion.3
  578.1 12.7 fusion.80
  590.8 11.5 bitcast_reduce_fusion.2
  602.3 11.8 fusion.33
  614.2 2.0 multiply_reduce_fusion.4
  616.2 2.1 convolution_convert_fusion.5
  623.8 8.1 bitcast_reduce_fusion
  631.9 9.6 multiply_reduce_fusion
  641.6 7.2 multiply_convert_fusion.1
  648.8 2.9 multiply_convert_fusion.5
  658.6 4.2 fusion.69
  664.2 3.5 convolution_convert_fusion.3
  667.6 4.0 convert_element_type.276
  671.6 2.9 copy.122
  679.1 4.0 convert_element_type.273
  683.1 2.8 copy.121
  687.4 3.8 convolution_convert_fusion.2
  693.1 2.4 copy.136
  695.5 2.4 copy.135
  697.9 2.4 copy.134
  700.2 2.4 constant_dynamic-update-slice_fusion.12
  705.0 2.5 constant_dynamic-update-slice_fusion.11
  707.5 2.5 constant_dynamic-update-slice_fusion.10
  720.1 2.6 constant_dynamic-update-slice_fusion
  724.5 5.9 sort
  730.4 18.6 %fusion.6 = f32[512,16,768]{2,1,0:T(8,128)} fusion(bf16[512,12,768]{2,0,1:T(8,128)(2,1)} %convert_bitcast_fusion, f32[512,12,16]{2,1,0:T(8,128)} %copy-done.1, f32[512,12]{1,0:T(8,128)S(1)} %log_add_fusion), kind=kOutput, calls=%fused_computation.10 | convolution fusion | flops 151191552 | bytes 35020800 | tf_op jit(solution)/shard_map/thk,thd->tkd/dot_general | solution.py:302
  749.1 22.3 %add_convert_fusion = bf16[512,16,768]{2,1,0:T(8,128)(2,1)} fusion(f32[512,16,768]{2,1,0:T(8,128)} %fusion.6, bf16[512,12,16]{2,1,0:T(8,128)(2,1)S(1)} %multiply_convert_fusion.3, bf16[512,12,768]{2,0,1:T(8,128)(2,1)} %fusion.15), kind=kOutput, calls=%fused_computation.6 | convolution fusion | flops 163577856 | bytes 47382528 | tf_op jit(solution)/shard_map/thk,thd->tkd/dot_general | solution.py:303
  771.3 14.3 bitcast_convert_fusion
  785.7 161.8 %scatter_custom_fusion = f32[32768,768]{1,0:T(8,128)} fusion(s32[8192]{0:T(1024)S(1)} %get-tuple-element.12, f32[]{:T(128)} %constant.42.clone.1, f32[8192,768]{1,0:T(8,128)} %bitcast_convert_fusion, s32[8192]{0:T(1024)S(1)} %broadcast_clamp_fusion), kind=kCustom, calls=%fused_computation.3 | custom fusion | flops 6291456 | bytes 100663808 | tf_op jit(solution)/shard_map/scatter-add | solution.py:116
  947.5 48.4 %convert_element_type.265 = bf16[32768,768]{1,0:T(8,128)(2,1)} convert(f32[32768,768]{1,0:T(8,128)} %scatter_custom_fusion) | non-fusion elementwise | flops 25165824 | bytes 150994944 | tf_op jit(solution)/shard_map/convert_element_type | solution.py:119
  996.6 427.3 %reduce-scatter.3.cloned.1.call-done = bf16[1024,768]{1,0:T(8,128)(2,1)} async-done(((bf16[32768,768]{1,0:T(8,128)(2,1)}), bf16[1024,768]{1,0:T(8,128)(2,1)}) %reduce-scatter.3.cloned.1.call-update) | async-done | bytes 1572880 | tf_op jit(solution)/shard_map/reduce_scatter | solution.py:118
  1423.9 5.2 add_convert_fusion.2
  1429.1 19.9 %all-gather.8.cloned.1.call-done = bf16[1600,768]{1,0:T(8,128)(2,1)} async-done(((bf16[400,768]{1,0:T(8,128)(2,1)}), bf16[1600,768]{1,0:T(8,128)(2,1)}) %all-gather.8.cloned.1.call-update) | async-done | bytes 2457616 | tf_op jit(solution)/shard_map/all_gather | solution.py:144
  1458.5 38.3 %all-gather.6.cloned.1.call-done = bf16[4096,768]{1,0:T(8,128)(2,1)} async-done(((bf16[1024,768]{1,0:T(8,128)(2,1)}), bf16[4096,768]{1,0:T(8,128)(2,1)}) %all-gather.6.cloned.1.call-update) | async-done | bytes 6291472 | tf_op jit(solution)/shard_map/all_gather | solution.py:121
  1496.8 8.6 convert_element_type.266
  (283 shorter events, 64.0 us)
Async XLA Ops:
  7.2 5.3 copy-start.48
  7.2 281.8 %all-gather.4.cloned.1.call-start = ((), (), s32[]{:S(2)}) async-start(), calls=%async_computation.2 | async-start | bytes 51904512 | tf_op jit(solution)/shard_map/all_gather | solution.py:109
  9.9 986.1 %reduce-scatter.5.cloned.1.call-start = ((), (), s32[]{:S(2)}) async-start(), calls=%async_computation.5 | async-start | bytes 20275200 | tf_op jit(solution)/shard_map/reduce_scatter | solution.py:141
  16.4 6.8 slice-start.5
  32.2 5.7 copy-start.28
  33.0 16.3 %copy-start.65 = (f32[768]{0:T(1024)}, f32[768]{0:T(1024)S(1)}, u32[]{:S(2)}) copy-start(f32[768]{0:T(1024)S(1)} %get-tuple-element.36) | copy-start | bytes 9220
  33.2 4.7 copy-start.9
  35.3 4.5 copy-start
  43.2 4.7 copy-start.38
  43.2 4.7 copy-start.71
  43.2 4.7 copy-start.74
  49.3 4.1 copy-start.23
  49.3 9.1 copy-start.51
  52.6 5.8 copy-start.30
  444.0 26.2 %copy-start.1 = (f32[512,12,16]{2,1,0:T(8,128)}, f32[512,12,16]{2,1,0:T(8,128)S(1)}, u32[]{:S(2)}) copy-start(f32[512,12,16]{2,1,0:T(8,128)S(1)} %get-tuple-element.70) | copy-start | bytes 1179652
  458.2 12.1 copy-start.25
  458.2 12.1 copy-start.56
  470.2 11.3 copy-start.16
  470.3 11.3 copy-start.35
  470.3 11.3 copy-start.52
  470.3 11.3 copy-start.66
  470.3 11.3 copy-start.69
  481.6 21.1 %slice-start.8 = ((s8[4718592]{0:T(1024)(128)(4,1)}), s8[4194304]{0:T(1024)(128)(4,1)S(1)}, s32[]{:S(2)}) async-start(s8[4718592]{0:T(1024)(128)(4,1)} %bitcast.210), calls=%async_computation.15 | async-start | bytes 8388608
  483.0 19.7 %slice-start.9 = ((s8[4718592]{0:T(1024)(128)(4,1)}), s8[524288]{0:T(1024)(128)(4,1)S(1)}, s32[]{:S(2)}) async-start(s8[4718592]{0:T(1024)(128)(4,1)} %bitcast.210), calls=%async_computation.16 | async-start | bytes 1048576
  483.0 19.7 %copy-start.76 = (f32[768]{0:T(1024)S(1)}, f32[768]{0:T(1024)}, u32[]{:S(2)}) copy-start(f32[768]{0:T(1024)} %param.26) | copy-start | bytes 9220
  509.4 13.7 slice-start.10
  513.7 9.4 slice-start.11
  523.1 5.9 copy-start.78
  578.1 12.7 copy-start.24
  590.8 23.4 %slice-start.3 = ((s8[7077888]{0:T(1024)(128)(4,1)}), s8[2883584]{0:T(1024)(128)(4,1)S(1)}, s32[]{:S(2)}) async-start(s8[7077888]{0:T(1024)(128)(4,1)} %bitcast.162), calls=%async_computation.10 | async-start | bytes 5767168
  602.3 11.8 slice-start.4
  602.3 11.8 copy-start.14
  602.3 11.9 copy-start.17
  602.3 11.9 copy-start.53
  602.3 11.9 copy-start.77
  618.9 4.9 copy-start.10
  618.9 4.9 copy-start.44
  623.8 8.1 copy-start.29
  623.8 17.7 %slice-start = ((s8[12582912]{0:T(1024)(128)(4,1)}), s8[4194304]{0:T(1024)(128)(4,1)S(1)}, s32[]{:S(2)}) async-start(s8[12582912]{0:T(1024)(128)(4,1)} %bitcast.159), calls=%async_computation.7 | async-start | bytes 8388608
  623.8 17.7 %slice-start.1 = ((s8[12582912]{0:T(1024)(128)(4,1)}), s8[4194304]{0:T(1024)(128)(4,1)S(1)}, s32[]{:S(2)}) async-start(s8[12582912]{0:T(1024)(128)(4,1)} %bitcast.159), calls=%async_computation.8 | async-start | bytes 8388608
  631.9 9.6 slice-start.2
  641.5 7.3 copy-start.8
  651.7 4.4 copy-start.58
  651.8 5.0 copy-start.72
  651.8 5.6 copy-start.54
  651.8 6.3 copy-start.73
  693.1 9.5 copy-start.57
  704.1 6.0 copy-start.37
  704.1 7.1 copy-start.27
  705.0 7.2 copy-start.26
  707.5 5.9 copy-start.21
  710.0 4.5 copy-start.22
  711.1 4.6 copy-start.20
  712.2 4.6 copy-start.19
  712.2 7.8 slice-start.6
  713.4 4.5 copy-start.18
  715.7 4.4 slice-start.7
  723.7 700.1 %reduce-scatter.3.cloned.1.call-start = ((), (), s32[]{:S(2)}) async-start(), calls=%async_computation.3 | async-start | bytes 51904512 | tf_op jit(solution)/shard_map/reduce_scatter | solution.py:118
  995.9 427.9 %copy-start.12 = (f32[512,768]{1,0:T(8,128)S(1)}, f32[512,768]{1,0:T(8,128)}, u32[]{:S(2)}) copy-start(f32[512,768]{1,0:T(8,128)} %copy-done.11) | copy-start | bytes 4718596
  995.9 428.0 %copy-start.32 = (bf16[12,64,512]{2,1,0:T(8,128)(2,1)S(1)}, bf16[12,64,512]{2,1,0:T(8,128)(2,1)}, u32[]{:S(2)}) copy-start(bf16[12,64,512]{2,1,0:T(8,128)(2,1)} %get-tuple-element.85) | copy-start | bytes 2359300
  995.9 428.0 %copy-start.40 = (bf16[12,64,512]{2,1,0:T(8,128)(2,1)S(1)}, bf16[12,64,512]{2,1,0:T(8,128)(2,1)}, u32[]{:S(2)}) copy-start(bf16[12,64,512]{2,1,0:T(8,128)(2,1)} %multiply_convert_fusion.5) | copy-start | bytes 2359300
  995.9 453.0 %all-gather.8.cloned.1.call-start = ((), (), s32[]{:S(2)}) async-start(), calls=%async_computation.6 | async-start | bytes 3072000 | tf_op jit(solution)/shard_map/all_gather | solution.py:144
  996.5 500.3 %all-gather.6.cloned.1.call-start = ((), (), s32[]{:S(2)}) async-start(), calls=%async_computation.4 | async-start | bytes 7864320 | tf_op jit(solution)/shard_map/all_gather | solution.py:121
  1449.0 4.7 copy-start.5
  (32 other events, 74.3 us)
Sparse Core Ops, SparseCore 0:
  11.5 277.5 all-gather.3
  723.8 209.5 reduce-scatter.4
  996.1 427.7 reduce-scatter.2
  1425.2 23.7 all-gather.7
  1450.4 46.3 all-gather.5

commit v2 on v1

--- a/solution.py
+++ b/solution.py
@@ -102,11 +102,32 @@
     return owners * rows_here <= DENSE_LIMIT
 
 
-def gather_store(datastore):
+STORE_PARTS = 2
+
+
+def fetch_dense(datastore, indices):
     copies = lax.axis_size("dp")
-    part = datastore.shape[0] // copies
-    mine = lax.dynamic_slice_in_dim(datastore, lax.axis_index("dp") * part, part, axis=0)
-    return lax.all_gather(mine, ("store", "dp"), axis=0, tiled=True)
+    rows_here = datastore.shape[0]
+    share = rows_here // copies
+    part = share // STORE_PARTS
+    flat = indices.reshape(-1)
+    which = (flat % share) // part
+    local = (flat // share) * part + flat % part
+    start = lax.axis_index("dp") * share
+    fetched = None
+    earlier = None
+    for index in range(STORE_PARTS):
+        mine = lax.dynamic_slice_in_dim(datastore, start + index * part, part, axis=0)
+        if earlier is not None:
+            mine, earlier = lax.optimization_barrier((mine, earlier))
+        table = lax.all_gather(mine, ("store", "dp"), axis=0, tiled=True)
+        earlier = mine
+        rows = table[local]
+        if fetched is None:
+            fetched = rows
+        else:
+            fetched = jnp.where((which == index)[:, None], rows, fetched)
+    return fetched
 
 
 def reduce_store(indices, row_grad, rows):
@@ -194,8 +215,7 @@
     valid = (position < length)[:, None]
     dense = is_dense(owners, rows_here)
     if dense:
-        full_store = gather_store(datastore)
-        fetched = full_store[indices.reshape(-1)].reshape(seq_len, K, D)
+        fetched = fetch_dense(datastore, indices).reshape(seq_len, K, D)
     else:
         target, request = route_slots(indices, rows_here, owners, capacity)
         returned, asked_here = fetch_rows(request, datastore)

time: 1520 us -> 1480 us (0.974)
  local copies, waits for them, and re-layouts: 246 us -> 202 us
    gather x1 -> x2, local copies, waits for them, and re-layouts: 141 us -> 97.3 us  [fetch_dense(): rows = table[local]]
    all_gather x1 -> x2, waiting for transfers between devices: 231 us -> 215 us  [fetch_dense(): table = lax.all_gather(mine, ('store', 'dp'), axis=0, tiled=True)]
    unnamed x198 -> x196, local copies, waits for them, and re-layouts: 40 us -> 39.4 us
  transfers between devices with their start and end apart: 5 -> 6, of which waited for: 4 -> 5; matrix products, arithmetic and copies ran while one was open for 22% -> 26% of each run, Pallas kernels for 0% -> 0%
where the time goes in v2:
time: 1480 us; the launch traced here: 1470 us
  waiting for transfers between devices  702 us (47%)
  other arithmetic  292 us (20%)
  matrix products  256 us (17%)
  local copies, waits for them, and re-layouts  202 us (14%)
  between operations  16.2 us (1%)
    reduce_scatter x1, waiting for transfers between devices, reduce_store(): lax.psum_scatter(partial.astype(jnp.bfloat16), ('store', 'dp'), scatter_d...  428 us
    all_gather x2, waiting for transfers between devices, fetch_dense(): table = lax.all_gather(mine, ('store', 'dp'), axis=0, tiled=True)  215 us
    scatter-add x3, other arithmetic, reduce_store(): partial = jnp.zeros((rows, D), jnp.float32).at[indices.reshape(-1)].add(r...  167 us
    gather x2, local copies, waits for them, and re-layouts, fetch_dense(): rows = table[local]  97.3 us
    convert_element_type x1, other arithmetic, reduce_store(): partial.astype(jnp.bfloat16)  48.3 us
    unnamed x196, local copies, waits for them, and re-layouts  39.4 us
    all_gather x1, waiting for transfers between devices, reduce_store(): return lax.all_gather(share, 'dp', axis=0, tiled=True).astype(jnp.float32)  38.3 us
    dot_general x6, matrix products, product(): return jnp.dot(matrix, factor, preferred_element_type=jnp.float32)  31.2 us
  transfers between devices with their start and end apart: 6, of which 5 were waited for; matrix products, arithmetic and copies ran while one was open for 26% of the time, Pallas kernels for 0%

profile of v2, /device:TPU:0, one launch (start us, length us, event | category | flops | bytes accessed | tf_op | source)
XLA Modules:
  0.0 1468.1 jit_solution(15763816677794895742)
XLA Ops:
  7.2 2.6 constant_dynamic-slice_fusion
  14.9 3.0 copy-done.2
  19.5 2.8 copy.103
  22.3 2.4 copy.108
  24.7 3.7 copy.134
  28.4 4.3 fusion.23
  36.9 2.6 exponential_reduce_fusion
  41.4 3.4 convolution_convert_fusion.10
  44.8 4.7 fusion.77
  51.7 2.2 add_convert_fusion.3
  55.1 5.1 fusion.15
  60.2 108.1 %all-gather.5.cloned.1.call-done = bf16[16384,768]{1,0:T(8,128)(2,1)} async-done(((bf16[512,768]{1,0:T(8,128)(2,1)}), bf16[16384,768]{1,0:T(8,128)(2,1)}) %all-gather.5.cloned.1.call-update) | async-done | bytes 25165840 | tf_op jit(solution)/shard_map/all_gather | solution.py:123
  168.3 48.8 %gather_fusion = bf16[8192,768]{1,0:T(8,128)(2,1)} fusion(bf16[16384,768]{1,0:T(8,128)(2,1)} %all-gather.5.cloned.1.call-done, s32[8192]{0:T(1024)S(1)} %broadcast_clamp_fusion.1), kind=kCustom, calls=%fused_computation | custom fusion | bytes 25198592 | tf_op jit(solution)/shard_map/gather | solution.py:125
  217.1 106.9 %all-gather.7.cloned.1.call-done = bf16[16384,768]{1,0:T(8,128)(2,1)} async-done(((bf16[512,768]{1,0:T(8,128)(2,1)}), bf16[16384,768]{1,0:T(8,128)(2,1)}) %all-gather.7.cloned.1.call-update) | async-done | bytes 25165840 | tf_op jit(solution)/shard_map/all_gather | solution.py:123
  324.0 48.5 %gather_fusion.1 = bf16[8192,768]{1,0:T(8,128)(2,1)} fusion(bf16[16384,768]{1,0:T(8,128)(2,1)} %all-gather.7.cloned.1.call-done, s32[8192]{0:T(1024)S(1)} %broadcast_clamp_fusion.1), kind=kCustom, calls=%fused_computation.1 | custom fusion | bytes 25198592 | tf_op jit(solution)/shard_map/gather | solution.py:125
  372.5 14.1 broadcast_select_fusion
  386.6 13.5 fusion.80
  400.1 14.1 exponential_reduce_fusion.1
  414.2 11.8 fusion.43
  426.1 11.2 fusion.28
  438.8 19.8 %multiply_convert_fusion.2 = (bf16[512,3072]{1,0:T(8,128)(2,1)S(1)}, f32[512,3072]{1,0:T(8,128)}, f32[512,3072]{1,0:T(8,128)}) fusion(f32[3072]{0:T(1024)S(1)} %copy-done.74, bf16[768,3072]{1,0:T(8,128)(2,1)} %param.23, f32[512,768]{1,0:T(8,128)S(1)} %get-tuple-element.80, f32[768]{0:T(1024)S(1)} %copy-done.67, f32[768]{0:T(1024)S(1)} %get-tuple-element.100, ...), kind=kOutput, calls=%fused_computation.33 | convolution fusion | flops 2521694208 | bytes 22042624 | tf_op jit(solution)/shard_map/dot_general | solution.py:16
  458.7 2.8 fusion.82
  461.9 2.3 multiply_reduce_fusion.2
  465.4 4.3 convolution_convert_fusion
  469.7 9.6 fusion.84
  479.3 5.9 multiply_reduce_fusion.3
  485.1 4.9 convolution_convert_fusion.1
  492.3 2.3 fusion.83
  496.0 11.0 fusion.32
  507.0 5.0 convert_bitcast_fusion
  512.0 15.5 %multiply_reduce_fusion.1 = (f32[512,12]{1,0:T(8,128)S(1)}, f32[512,12,16]{2,1,0:T(8,128)}) fusion(f32[512,12,16]{2,1,0:T(8,128)} %copy-done.1, f32[512,12]{1,0:T(8,128)S(1)} %log_add_fusion, bf16[512,16,768]{2,1,0:T(8,128)(2,1)} %broadcast_select_fusion, bf16[512,12,768]{2,0,1:T(8,128)(2,1)} %convert_bitcast_fusion), kind=kOutput, calls=%fused_computation.53 | convolution fusion | flops 151283712 | bytes 22855680 | tf_op jit(solution)/shard_map/thd,tkd->thk/dot_general | solution.py:315
  527.5 6.6 multiply_convert_fusion.3
  534.1 12.6 fusion.85
  546.7 11.5 bitcast_reduce_fusion.2
  558.3 11.6 fusion.33
  580.1 8.1 bitcast_reduce_fusion
  588.2 9.6 multiply_reduce_fusion
  597.8 7.5 multiply_convert_fusion.1
  605.3 2.9 multiply_convert_fusion.5
  615.1 4.2 fusion.74
  620.0 3.5 convolution_convert_fusion.3
  623.5 4.0 convert_element_type.276
  627.5 2.8 copy.125
  634.9 4.0 convert_element_type.273
  638.9 2.8 copy.124
  643.1 3.8 convolution_convert_fusion.2
  648.8 2.4 copy.139
  651.2 2.4 copy.138
  653.6 2.4 copy.137
  656.0 2.4 constant_dynamic-update-slice_fusion.12
  660.7 2.5 constant_dynamic-update-slice_fusion.11
  663.2 2.5 constant_dynamic-update-slice_fusion.10
  675.8 2.6 constant_dynamic-update-slice_fusion
  680.2 5.9 sort
  686.2 18.3 %fusion.6 = f32[512,16,768]{2,1,0:T(8,128)} fusion(bf16[512,12,768]{2,0,1:T(8,128)(2,1)} %convert_bitcast_fusion, f32[512,12,16]{2,1,0:T(8,128)} %copy-done.1, f32[512,12]{1,0:T(8,128)S(1)} %log_add_fusion), kind=kOutput, calls=%fused_computation.11 | convolution fusion | flops 151191552 | bytes 35020800 | tf_op jit(solution)/shard_map/thk,thd->tkd/dot_general | solution.py:322
  704.5 22.3 %add_convert_fusion = bf16[512,16,768]{2,1,0:T(8,128)(2,1)} fusion(f32[512,16,768]{2,1,0:T(8,128)} %fusion.6, bf16[512,12,16]{2,1,0:T(8,128)(2,1)S(1)} %multiply_convert_fusion.3, bf16[512,12,768]{2,0,1:T(8,128)(2,1)} %fusion.15), kind=kOutput, calls=%fused_computation.7 | convolution fusion | flops 163577856 | bytes 47382528 | tf_op jit(solution)/shard_map/thk,thd->tkd/dot_general | solution.py:323
  726.8 14.3 bitcast_convert_fusion
  741.1 161.4 %scatter_custom_fusion = f32[32768,768]{1,0:T(8,128)} fusion(s32[8192]{0:T(1024)S(1)} %get-tuple-element.14, f32[]{:T(128)} %constant.59.clone.1, f32[8192,768]{1,0:T(8,128)} %bitcast_convert_fusion, s32[8192]{0:T(1024)S(1)} %broadcast_clamp_fusion), kind=kCustom, calls=%fused_computation.4 | custom fusion | flops 6291456 | bytes 100663808 | tf_op jit(solution)/shard_map/scatter-add | solution.py:137
  902.5 48.3 %convert_element_type.265 = bf16[32768,768]{1,0:T(8,128)(2,1)} convert(f32[32768,768]{1,0:T(8,128)} %scatter_custom_fusion) | non-fusion elementwise | flops 25165824 | bytes 150994944 | tf_op jit(solution)/shard_map/convert_element_type | solution.py:140
  951.5 427.9 %reduce-scatter.3.cloned.1.call-done = bf16[1024,768]{1,0:T(8,128)(2,1)} async-done(((bf16[32768,768]{1,0:T(8,128)(2,1)}), bf16[1024,768]{1,0:T(8,128)(2,1)}) %reduce-scatter.3.cloned.1.call-update) | async-done | bytes 1572880 | tf_op jit(solution)/shard_map/reduce_scatter | solution.py:139
  1379.4 5.2 add_convert_fusion.2
  1384.6 19.9 %all-gather.11.cloned.1.call-done = bf16[1600,768]{1,0:T(8,128)(2,1)} async-done(((bf16[400,768]{1,0:T(8,128)(2,1)}), bf16[1600,768]{1,0:T(8,128)(2,1)}) %all-gather.11.cloned.1.call-update) | async-done | bytes 2457616 | tf_op jit(solution)/shard_map/all_gather | solution.py:165
  1414.0 38.3 %all-gather.9.cloned.1.call-done = bf16[4096,768]{1,0:T(8,128)(2,1)} async-done(((bf16[1024,768]{1,0:T(8,128)(2,1)}), bf16[4096,768]{1,0:T(8,128)(2,1)}) %all-gather.9.cloned.1.call-update) | async-done | bytes 6291472 | tf_op jit(solution)/shard_map/all_gather | solution.py:142
  1452.3 8.6 convert_element_type.266
  (288 shorter events, 71.8 us)
Async XLA Ops:
  7.2 6.0 copy-start.44
  7.2 161.1 %all-gather.5.cloned.1.call-start = ((), (), s32[]{:S(2)}) async-start(), calls=%async_computation.2 | async-start | bytes 25952256 | tf_op jit(solution)/shard_map/all_gather | solution.py:123
  9.9 314.1 %all-gather.7.cloned.1.call-start = ((), (), s32[]{:S(2)}) async-start(), calls=%async_computation.3 | async-start | bytes 25952256 | tf_op jit(solution)/shard_map/all_gather | solution.py:123
  10.6 940.3 %reduce-scatter.5.cloned.1.call-start = ((), (), s32[]{:S(2)}) async-start(), calls=%async_computation.6 | async-start | bytes 20275200 | tf_op jit(solution)/shard_map/reduce_scatter | solution.py:162
  18.0 6.8 slice-start.5
  33.8 5.7 copy-start.28
  34.6 16.3 %copy-start.64 = (f32[768]{0:T(1024)}, f32[768]{0:T(1024)S(1)}, u32[]{:S(2)}) copy-start(f32[768]{0:T(1024)S(1)} %get-tuple-element.38) | copy-start | bytes 9220
  34.8 4.7 copy-start.9
  36.9 4.5 copy-start
  44.8 4.8 copy-start.38
  44.8 4.7 copy-start.73
  50.8 4.2 copy-start.23
  54.2 6.0 copy-start.30
  217.1 155.4 %copy-start.43 = (pred[512,16]{1,0:T(8,128)(4,1)S(1)}, pred[512,16]{1,0:T(8,128)(4,1)}, u32[]{:S(2)}) copy-start(pred[512,16]{1,0:T(8,128)(4,1)} %copy.104) | copy-start | bytes 24580
  400.1 26.0 %copy-start.1 = (f32[512,12,16]{2,1,0:T(8,128)}, f32[512,12,16]{2,1,0:T(8,128)S(1)}, u32[]{:S(2)}) copy-start(f32[512,12,16]{2,1,0:T(8,128)S(1)} %get-tuple-element.76) | copy-start | bytes 1179652
  414.2 11.8 copy-start.25
  414.2 11.8 copy-start.55
  426.1 11.3 copy-start.16
  426.1 11.3 copy-start.35
  426.1 11.3 copy-start.65
  426.1 11.3 copy-start.68
  437.4 21.3 %slice-start.8 = ((s8[4718592]{0:T(1024)(128)(4,1)}), s8[4194304]{0:T(1024)(128)(4,1)S(1)}, s32[]{:S(2)}) async-start(s8[4718592]{0:T(1024)(128)(4,1)} %bitcast.210), calls=%async_computation.16 | async-start | bytes 8388608
  438.8 19.8 %slice-start.9 = ((s8[4718592]{0:T(1024)(128)(4,1)}), s8[524288]{0:T(1024)(128)(4,1)S(1)}, s32[]{:S(2)}) async-start(s8[4718592]{0:T(1024)(128)(4,1)} %bitcast.210), calls=%async_computation.17 | async-start | bytes 1048576
  438.8 19.8 %copy-start.75 = (f32[768]{0:T(1024)S(1)}, f32[768]{0:T(1024)}, u32[]{:S(2)}) copy-start(f32[768]{0:T(1024)} %param.26) | copy-start | bytes 9220
  465.4 13.9 slice-start.10
  469.7 9.6 slice-start.11
  479.2 5.9 copy-start.77
  534.1 12.6 copy-start.24
  546.7 23.1 %slice-start.3 = ((s8[7077888]{0:T(1024)(128)(4,1)}), s8[2883584]{0:T(1024)(128)(4,1)S(1)}, s32[]{:S(2)}) async-start(s8[7077888]{0:T(1024)(128)(4,1)} %bitcast.162), calls=%async_computation.11 | async-start | bytes 5767168
  558.3 11.6 slice-start.4
  558.3 11.6 copy-start.14
  558.3 11.6 copy-start.17
  558.3 11.6 copy-start.76
  575.1 4.9 copy-start.10
  575.1 4.9 copy-start.42
  580.0 8.1 copy-start.29
  580.0 17.7 %slice-start = ((s8[12582912]{0:T(1024)(128)(4,1)}), s8[4194304]{0:T(1024)(128)(4,1)S(1)}, s32[]{:S(2)}) async-start(s8[12582912]{0:T(1024)(128)(4,1)} %bitcast.157), calls=%async_computation.8 | async-start | bytes 8388608
  580.1 17.7 %slice-start.1 = ((s8[12582912]{0:T(1024)(128)(4,1)}), s8[4194304]{0:T(1024)(128)(4,1)S(1)}, s32[]{:S(2)}) async-start(s8[12582912]{0:T(1024)(128)(4,1)} %bitcast.157), calls=%async_computation.9 | async-start | bytes 8388608
  588.2 9.6 slice-start.2
  597.8 7.5 copy-start.8
  608.2 4.4 copy-start.57
  608.2 5.0 copy-start.71
  608.2 5.6 copy-start.52
  608.2 6.2 copy-start.72
  615.1 4.2 copy-start.70
  620.0 12.9 copy-start.53
  648.8 9.5 copy-start.56
  659.8 5.9 copy-start.37
  659.8 7.0 copy-start.27
  660.7 7.2 copy-start.26
  663.2 5.9 copy-start.21
  665.7 4.6 copy-start.22
  666.8 4.6 copy-start.20
  667.9 4.6 copy-start.19
  667.9 7.9 slice-start.6
  669.1 4.5 copy-start.18
  671.4 4.4 slice-start.7
  679.5 699.9 %reduce-scatter.3.cloned.1.call-start = ((), (), s32[]{:S(2)}) async-start(), calls=%async_computation.4 | async-start | bytes 51904512 | tf_op jit(solution)/shard_map/reduce_scatter | solution.py:139
  950.8 428.6 %copy-start.12 = (f32[512,768]{1,0:T(8,128)S(1)}, f32[512,768]{1,0:T(8,128)}, u32[]{:S(2)}) copy-start(f32[512,768]{1,0:T(8,128)} %copy-done.11) | copy-start | bytes 4718596
  950.8 428.6 %copy-start.32 = (bf16[12,64,512]{2,1,0:T(8,128)(2,1)S(1)}, bf16[12,64,512]{2,1,0:T(8,128)(2,1)}, u32[]{:S(2)}) copy-start(bf16[12,64,512]{2,1,0:T(8,128)(2,1)} %get-tuple-element.91) | copy-start | bytes 2359300
  950.8 428.6 %copy-start.40 = (bf16[12,64,512]{2,1,0:T(8,128)(2,1)S(1)}, bf16[12,64,512]{2,1,0:T(8,128)(2,1)}, u32[]{:S(2)}) copy-start(bf16[12,64,512]{2,1,0:T(8,128)(2,1)} %multiply_convert_fusion.5) | copy-start | bytes 2359300
  950.9 453.6 %all-gather.11.cloned.1.call-start = ((), (), s32[]{:S(2)}) async-start(), calls=%async_computation.7 | async-start | bytes 3072000 | tf_op jit(solution)/shard_map/all_gather | solution.py:165
  951.4 500.9 %all-gather.9.cloned.1.call-start = ((), (), s32[]{:S(2)}) async-start(), calls=%async_computation.5 | async-start | bytes 7864320 | tf_op jit(solution)/shard_map/all_gather | solution.py:142
  1404.5 4.7 copy-start.5
  (32 other events, 78.6 us)
Sparse Core Ops, SparseCore 0:
  11.5 156.7 all-gather.4
  171.7 152.2 all-gather.6
  679.6 209.8 reduce-scatter.4
  951.0 428.3 reduce-scatter.2
  1380.8 23.6 all-gather.10
  1405.9 46.3 all-gather.8

commit v3 on v2

--- a/solution.py
+++ b/solution.py
@@ -1,6 +1,10 @@
+import functools
+
 import jax
 import jax.numpy as jnp
 from jax import lax
+from jax.experimental import pallas as pl
+from jax.experimental.pallas import tpu as pltpu
 from jax.sharding import PartitionSpec as P
 
 D = 768
@@ -99,13 +103,14 @@
 
 
 def is_dense(owners, rows_here):
-    return owners * rows_here <= DENSE_LIMIT
+    fits = owners * rows_here <= DENSE_LIMIT and rows_here % (8 * CHUNK) == 0
+    return fits and owners == 8 and lax.axis_size("dp") == 4
 
 
 STORE_PARTS = 2
 
 
-def fetch_dense(datastore, indices):
+def fetch_dense(datastore, indices, plan):
     copies = lax.axis_size("dp")
     rows_here = datastore.shape[0]
     share = rows_here // copies
@@ -122,24 +127,269 @@
             mine, earlier = lax.optimization_barrier((mine, earlier))
         table = lax.all_gather(mine, ("store", "dp"), axis=0, tiled=True)
         earlier = mine
+        if index == STORE_PARTS - 1:
+            which, plan = lax.optimization_barrier((which, plan))
         rows = table[local]
         if fetched is None:
             fetched = rows
         else:
             fetched = jnp.where((which == index)[:, None], rows, fetched)
-    return fetched
-
-
-def reduce_store(indices, row_grad, rows):
-    partial = (
-        jnp.zeros((rows, D), jnp.float32)
-        .at[indices.reshape(-1)]
-        .add(row_grad.reshape(-1, D).astype(jnp.float32))
-    )
-    share = lax.psum_scatter(
-        partial.astype(jnp.bfloat16), ("store", "dp"), scatter_dimension=0, tiled=True
-    )
-    return lax.all_gather(share, "dp", axis=0, tiled=True).astype(jnp.float32)
+    return fetched, plan
+
+
+MESH_ID = pl.DeviceIdType.MESH
+VMEM_LIMIT = 67043328
+CHUNK = 64
+
+
+GROUP = 8
+
+
+def scatter_kernel(steps, block, out_rows, row_ref, from_ref, twice_ref, groups_ref, own_ref, other_ref, out_ref, total, wide):
+    step = pl.program_id(0)
+
+    @pl.when(step == 0)
+    def _():
+        def clear(i, carry):
+            total[pl.ds(i * 32, 32), :] = jnp.zeros((32, D), jnp.float32)
+            return carry
+        lax.fori_loop(0, total.shape[0] // 32, clear, 0)
+
+    @pl.when(step < steps // 2)
+    def _():
+        wide[...] = own_ref[...].astype(jnp.float32)
+
+    @pl.when((step >= steps // 2) & (step < steps))
+    def _():
+        wide[...] = other_ref[...].astype(jnp.float32)
+
+    @pl.when(step < steps)
+    def _():
+        def group(i, carry):
+            first = step * block + i * GROUP
+            rows = [row_ref[first + k] for k in range(GROUP)]
+            came = [from_ref[first + k] for k in range(GROUP)]
+            twice = twice_ref[step * (block // GROUP) + i]
+
+            @pl.when(twice == 0)
+            def _():
+                sums = [total[pl.ds(rows[k], 1), :] + wide[pl.ds(came[k], 1), :] for k in range(GROUP)]
+                for k in range(GROUP):
+                    total[pl.ds(rows[k], 1), :] = sums[k]
+
+            @pl.when(twice != 0)
+            def _():
+                for k in range(GROUP):
+                    total[pl.ds(rows[k], 1), :] = total[pl.ds(rows[k], 1), :] + wide[pl.ds(came[k], 1), :]
+            return carry
+        lax.fori_loop(0, groups_ref[step], group, 0)
+
+    @pl.when(step >= steps)
+    def _():
+        first = pl.multiple_of((step - steps) * out_rows, out_rows)
+        out_ref[...] = total[pl.ds(first, out_rows), :].astype(jnp.bfloat16)
+
+
+SCATTER_BLOCK = 256
+
+
+def scatter_plan(where, rows):
+    keys = jnp.arange(where.shape[0], dtype=jnp.int32).reshape(-1, SCATTER_BLOCK) % SCATTER_BLOCK
+    where = where.reshape(-1, SCATTER_BLOCK)
+    skipped = where >= rows
+    keys, where = lax.sort((jnp.where(skipped, keys + SCATTER_BLOCK, keys), where), dimension=1, num_keys=1)
+    count = jnp.sum((~skipped).astype(jnp.int32), axis=1)
+    groups = (count + GROUP - 1) // GROUP
+    where = jnp.where(keys >= SCATTER_BLOCK, rows + keys % GROUP, where)
+    spare = lax.broadcasted_iota(jnp.int32, where.shape, 1) % GROUP
+    where = jnp.where(keys >= SCATTER_BLOCK, rows + spare, where)
+    eights = where.reshape(-1, GROUP)
+    twice = jnp.zeros((eights.shape[0],), jnp.int32)
+    for shift in range(1, GROUP):
+        same = eights[:, shift:] == eights[:, :-shift]
+        twice = twice | jnp.any(same, axis=1).astype(jnp.int32)
+    return where.reshape(-1), (keys % SCATTER_BLOCK).reshape(-1), twice, groups
+
+
+def scatter_rows(plan, own, other, rows, out_rows=256):
+    block = SCATTER_BLOCK
+    half = own.shape[0] // block
+    steps = 2 * half
+    return pl.pallas_call(
+        functools.partial(scatter_kernel, steps, block, out_rows),
+        out_shape=jax.ShapeDtypeStruct((rows, D), jnp.bfloat16),
+        grid_spec=pltpu.PrefetchScalarGridSpec(
+            num_scalar_prefetch=4,
+            grid=(steps + rows // out_rows,),
+            in_specs=[
+                pl.BlockSpec((block, D), lambda i, *_: (jnp.minimum(i, half - 1), 0)),
+                pl.BlockSpec((block, D), lambda i, *_: (jnp.clip(i - half, 0, half - 1), 0)),
+            ],
+            out_specs=pl.BlockSpec((out_rows, D), lambda i, *_: (jnp.maximum(i - steps, 0), 0)),
+            scratch_shapes=[
+                pltpu.VMEM((rows + 32, D), jnp.float32),
+                pltpu.VMEM((block, D), jnp.float32),
+            ],
+        ),
+        compiler_params=pltpu.CompilerParams(vmem_limit_bytes=VMEM_LIMIT),
+        name="scatter_rows",
+    )(*plan, own, other)
+
+
+def reduce_kernel(chunks, part_ref, out_ref, keep_a, keep_b, one_a, one_b, two_a, two_b, layer, along, done,
+                  keep_sem, one_send, one_recv, two_send, two_recv, z_send, z_recv,
+                  own_sem, y_send, y_recv, core_send, core_recv, pass_send, pass_recv):
+    dp = lax.axis_index("dp")
+    store = lax.axis_index("store")
+    y, core = lax.div(dp, 2), lax.rem(dp, 2)
+    z, x = lax.div(store, 2), lax.rem(store, 2)
+    x_peer = (dp, z * 2 + (1 - x))
+    y_peer = ((1 - y) * 2 + core, store)
+    core_peer = (y * 2 + (1 - core), store)
+    z_of = [lax.rem(z + hop, 4) for hop in range(4)]
+    z_peer = [(dp, z_of[hop] * 2 + x) for hop in range(4)]
+
+    barrier = pltpu.get_barrier_semaphore()
+    for peer in (x_peer, y_peer, core_peer, z_peer[1], z_peer[2], z_peer[3]):
+        pl.semaphore_signal(barrier, inc=1, device_id=peer, device_id_type=MESH_ID)
+    pl.semaphore_wait(barrier, 6)
+
+    def remote(src, dst, send, recv, peer):
+        return pltpu.make_async_remote_copy(src_ref=src, dst_ref=dst, send_sem=send, recv_sem=recv,
+                                            device_id=peer, device_id_type=MESH_ID)
+
+    keeps = [(
+        pltpu.make_async_copy(part_ref.at[:, x, :, 0, q], keep_a.at[q], keep_sem.at[0, q]),
+        pltpu.make_async_copy(part_ref.at[:, :, y, 1, q], keep_b.at[q], keep_sem.at[1, q]),
+    ) for q in range(chunks)]
+    ones = [(
+        remote(part_ref.at[:, 1 - x, :, 0, q], one_a.at[q], one_send.at[0, q], one_recv.at[0, q], x_peer),
+        remote(part_ref.at[:, :, 1 - y, 1, q], one_b.at[q], one_send.at[1, q], one_recv.at[1, q], y_peer),
+    ) for q in range(chunks)]
+    twos = [(
+        remote(keep_a.at[q, :, 1 - y], two_a.at[q], two_send.at[0, q], two_recv.at[0, q], y_peer),
+        remote(keep_b.at[q, :, 1 - x], two_b.at[q], two_send.at[1, q], two_recv.at[1, q], x_peer),
+    ) for q in range(chunks)]
+    zs = [[
+        remote(layer.at[q, z_of[hop]], along.at[q, hop - 1], z_send.at[hop - 1, q], z_recv.at[hop - 1, q], z_peer[hop])
+        for hop in (1, 2, 3)] for q in range(chunks)]
+    own = [pltpu.make_async_copy(done.at[q], out_ref.at[core, y, :, q], own_sem.at[q]) for q in range(chunks)]
+    to_y = [remote(done.at[q], out_ref.at[core, y, :, q], y_send.at[q], y_recv.at[q], y_peer) for q in range(chunks)]
+    to_core = [remote(done.at[q], out_ref.at[core, y, :, q], core_send.at[q], core_recv.at[q], core_peer) for q in range(chunks)]
+    passed = [remote(out_ref.at[core, 1 - y, :, q], out_ref.at[core, 1 - y, :, q], pass_send.at[q], pass_recv.at[q], core_peer)
+              for q in range(chunks)]
+
+    def plus(first, second):
+        return (first.astype(jnp.float32) + second.astype(jnp.float32)).astype(jnp.bfloat16)
+
+    window = 2
+    for q in range(min(window, chunks)):
+        for copy in keeps[q] + ones[q]:
+            copy.start()
+    for step in range(chunks + 3):
+        q = step
+        if q < chunks:
+            for copy in keeps[q]:
+                copy.wait()
+            for copy in ones[q]:
+                copy.wait_recv()
+
+            def merge(i, carry, q=q):
+                for half in range(2):
+                    keep_a[q, i, half] = plus(keep_a[q, i, half], one_a[q, i, half])
+                    keep_b[q, i, half] = plus(keep_b[q, i, half], one_b[q, i, half])
+                return carry
+            lax.fori_loop(0, 4, merge, 0)
+            for copy in twos[q]:
+                copy.start()
+            if q + window < chunks:
+                for copy in keeps[q + window] + ones[q + window]:
+                    copy.start()
+        q = step - 1
+        if 0 <= q < chunks:
+            for copy in twos[q]:
+                copy.wait_recv()
+
+            def merge_two(i, carry, q=q):
+                layer[q, i, 0] = plus(keep_a[q, i, y], two_a[q, i])
+                layer[q, i, 1] = plus(keep_b[q, i, x], two_b[q, i])
+                return carry
+            lax.fori_loop(0, 4, merge_two, 0)
+            for copy in zs[q]:
+                copy.start()
+        q = step - 2
+        if 0 <= q < chunks:
+            for copy in zs[q]:
+                copy.wait_recv()
+
+            def finish(i, carry, q=q):
+                value = layer[q, z, i].astype(jnp.float32)
+                for hop in range(3):
+                    value = value + along[q, hop, i].astype(jnp.float32)
+                done[q, i] = value.astype(jnp.bfloat16)
+                return carry
+            lax.fori_loop(0, 2, finish, 0)
+            for copy in (own[q], to_y[q], to_core[q]):
+                copy.start()
+        q = step - 3
+        if 0 <= q < chunks:
+            to_y[q].wait_recv()
+            passed[q].start()
+    for q in range(chunks):
+        for copy in ones[q] + twos[q] + tuple(zs[q]):
+            copy.wait_send()
+        own[q].wait()
+        to_y[q].wait_send()
+        to_core[q].wait()
+        passed[q].wait()
+
+
+def reduce_rows(partial, collective_id=0):
+    rows = partial.shape[0] // 8
+    chunks = rows // (4 * CHUNK)
+    blocks = partial.reshape(4, 2, 2, 2, chunks, CHUNK, D)
+    dma = pltpu.SemaphoreType.DMA
+    vm = lambda *lead: pltpu.VMEM(lead + (CHUNK, D), jnp.bfloat16)
+    out = pl.pallas_call(
+        functools.partial(reduce_kernel, chunks),
+        out_shape=jax.ShapeDtypeStruct((2, 2, 2, chunks, CHUNK, D), jnp.bfloat16),
+        in_specs=[pl.BlockSpec(memory_space=pl.ANY)],
+        out_specs=pl.BlockSpec(memory_space=pl.ANY),
+        scratch_shapes=[
+            vm(chunks, 4, 2), vm(chunks, 4, 2), vm(chunks, 4, 2), vm(chunks, 4, 2),
+            vm(chunks, 4), vm(chunks, 4), vm(chunks, 4, 2), vm(chunks, 3, 2), vm(chunks, 2),
+            dma((2, chunks)), dma((2, chunks)), dma((2, chunks)), dma((2, chunks)), dma((2, chunks)),
+            dma((3, chunks)), dma((3, chunks)),
+            dma((chunks,)), dma((chunks,)), dma((chunks,)), dma((chunks,)), dma((chunks,)), dma((chunks,)), dma((chunks,)),
+        ],
+        compiler_params=pltpu.CompilerParams(collective_id=collective_id, has_side_effects=True, vmem_limit_bytes=VMEM_LIMIT),
+        name="reduce_rows",
+    )(blocks)
+    return out.reshape(2 * rows, D)
+
+PAIRS = ((0, 1), (1, 0), (2, 3), (3, 2))
+
+
+def own_rows(flat, rows_here):
+    half = rows_here // 2
+    core = lax.rem(lax.axis_index("dp"), 2)
+    local = flat % rows_here
+    rows = lax.axis_size("store") * half
+    return jnp.where(local // half == core, (flat // rows_here) * half + local % half, rows)
+
+
+def plan_store(indices, rows_here):
+    flat = indices.reshape(-1)
+    other = lax.ppermute(flat, "dp", PAIRS)
+    where = jnp.concatenate([own_rows(flat, rows_here), own_rows(other, rows_here)])
+    return scatter_plan(where, lax.axis_size("store") * rows_here // 2)
+
+
+def reduce_store(plan, row_grad, rows_here):
+    own = row_grad.reshape(-1, D)
+    other = lax.ppermute(own, "dp", PAIRS)
+    partial = scatter_rows(plan, own, other, lax.axis_size("store") * rows_here // 2)
+    return reduce_rows(partial).astype(jnp.float32)
 
 
 def reduce_weights(squares, inner, outer, features, inner_bias):
@@ -215,7 +465,9 @@
     valid = (position < length)[:, None]
     dense = is_dense(owners, rows_here)
     if dense:
-        fetched = fetch_dense(datastore, indices).reshape(seq_len, K, D)
+        plan = plan_store(indices, rows_here)
+        fetched, plan = fetch_dense(datastore, indices, plan)
+        fetched = fetched.reshape(seq_len, K, D)
     else:
         target, request = route_slots(indices, rows_here, owners, capacity)
         returned, asked_here = fetch_rows(request, datastore)
@@ -337,10 +589,12 @@
         .astype(jnp.bfloat16)
         .reshape(seq_len, D)
     )
+    if dense:
+        query_low, row_grad = lax.optimization_barrier((query_low, row_grad))
     bias_three = column_sum(query_low)
     grad_cross_query = contract_rows(first_low, query_low)
     if dense:
-        grad_store = reduce_store(indices, row_grad, owners * rows_here)
+        grad_store = reduce_store(plan, row_grad, rows_here)
     else:
         grad_buffer = (
             jnp.zeros((owners * capacity, D), jnp.bfloat16)

time: 1480 us -> 1330 us (0.90)
  Pallas kernels: 0 us -> 379 us
  waiting for transfers between devices: 702 us -> 417 us
  other arithmetic: 292 us -> 70 us
  local copies, waits for them, and re-layouts: 202 us -> 183 us
    reduce_scatter x1 -> x0, waiting for transfers between devices: 428 us -> none  [reduce_store(): lax.psum_scatter(partial.astype(jnp.bfloat16), ('store', 'dp'), scatter_d...]
    pallas_call x0 -> x2, Pallas kernels: none -> 379 us  [the longest x1 254 us: reduce_rows(): pl.pallas_call(functools.partial(reduce_kernel, chunks), out_shape=jax.Sh...]
    reduce_scatter x1, waiting for transfers between devices: 0.02 us -> 209 us  [reduce_weights(): lax.psum_scatter(packed.reshape(-1, D), ('store', 'dp'), scatter_dimensio...]
    scatter-add x3 -> x0, other arithmetic: 167 us -> none  [reduce_store(): partial = jnp.zeros((rows, D), jnp.float32).at[indices.reshape(-1)].add(r...]
    convert_element_type x3 -> x2, other arithmetic: 71.2 us -> 9.19 us  [the longest x1 8.55 us: reduce_store(): return reduce_rows(partial).astype(jnp.float32)]
    all_gather x1 -> x0, waiting for transfers between devices: 38.3 us -> none  [reduce_store(): return lax.all_gather(share, 'dp', axis=0, tiled=True).astype(jnp.float32)]
    all_gather x1, waiting for transfers between devices: 19.9 us -> 0.01 us  [reduce_weights(): total = lax.all_gather(share, 'dp', axis=0, tiled=True).astype(jnp.float32)]
    unnamed x196 -> x185, local copies, waits for them, and re-layouts: 39.4 us -> 38 us
  transfers between devices with their start and end apart: 6 -> 6, of which waited for: 5 -> 4; matrix products, arithmetic and copies ran while one was open for 26% -> 9% of each run, Pallas kernels for 0% -> 29%
where the time goes in v3:
time: 1330 us; the launch traced here: 1320 us
  waiting for transfers between devices  417 us (31%)
  Pallas kernels  379 us (28%)
  matrix products  252 us (19%)
  local copies, waits for them, and re-layouts  183 us (14%)
  other arithmetic  70 us (5%)
  between operations  18 us (1%)
    pallas_call x1, Pallas kernels, reduce_rows(): pl.pallas_call(functools.partial(reduce_kernel, chunks), out_shape=jax.Sh...  254 us
    reduce_scatter x1, waiting for transfers between devices, reduce_weights(): lax.psum_scatter(packed.reshape(-1, D), ('store', 'dp'), scatter_dimensio...  209 us
    all_gather x2, waiting for transfers between devices, fetch_dense(): table = lax.all_gather(mine, ('store', 'dp'), axis=0, tiled=True)  206 us
    pallas_call x1, Pallas kernels, scatter_rows(): pl.pallas_call(functools.partial(scatter_kernel, steps, block, out_rows),...  125 us
    gather x2, local copies, waits for them, and re-layouts, fetch_dense(): rows = table[local]  97 us
    unnamed x185, local copies, waits for them, and re-layouts  38 us
    dot_general x6, matrix products, product(): return jnp.dot(matrix, factor, preferred_element_type=jnp.float32)  31.7 us
  transfers between devices with their start and end apart: 6, of which 4 were waited for; matrix products, arithmetic and copies ran while one was open for 9% of the time, Pallas kernels for 29%

profile of v3, /device:TPU:0, one launch (start us, length us, event | category | flops | bytes accessed | tf_op | source)
XLA Modules:
  0.0 1319.7 jit_solution(11164644193698592766)
XLA Ops:
  12.6 2.6 constant_dynamic-slice_fusion
  18.5 3.0 copy-done.3
  23.1 2.7 copy.103
  25.8 2.4 copy.109
  28.3 3.7 copy.135
  32.0 4.3 fusion.17
  38.3 2.1 fusion.8
  40.4 2.6 exponential_reduce_fusion
  43.0 1.8 copy-done
  44.9 3.4 convolution_convert_fusion.10
  48.4 4.7 fusion.96
  54.5 2.7 add_convert_fusion.3
  57.9 6.7 fusion.9
  73.3 99.5 %all-gather.4.cloned.1.call-done = bf16[16384,768]{1,0:T(8,128)(2,1)} async-done(((bf16[512,768]{1,0:T(8,128)(2,1)}), bf16[16384,768]{1,0:T(8,128)(2,1)}) %all-gather.4.cloned.1.call-update) | async-done | bytes 25165840 | tf_op jit(solution)/shard_map/all_gather | solution.py:128
  172.8 48.4 %gather_fusion = bf16[8192,768]{1,0:T(8,128)(2,1)} fusion(bf16[16384,768]{1,0:T(8,128)(2,1)} %all-gather.4.cloned.1.call-done, s32[8192]{0:T(1024)S(1)} %broadcast_clamp_fusion), kind=kCustom, calls=%fused_computation | custom fusion | bytes 25198592 | tf_op jit(solution)/shard_map/gather | solution.py:132
  221.3 106.8 %all-gather.6.cloned.1.call-done = bf16[16384,768]{1,0:T(8,128)(2,1)} async-done(((bf16[512,768]{1,0:T(8,128)(2,1)}), bf16[16384,768]{1,0:T(8,128)(2,1)}) %all-gather.6.cloned.1.call-update) | async-done | bytes 25165840 | tf_op jit(solution)/shard_map/all_gather | solution.py:128
  328.0 48.6 %gather_fusion.1 = bf16[8192,768]{1,0:T(8,128)(2,1)} fusion(bf16[16384,768]{1,0:T(8,128)(2,1)} %all-gather.6.cloned.1.call-done, s32[8192]{0:T(1024)S(1)} %broadcast_clamp_fusion), kind=kCustom, calls=%fused_computation.1 | custom fusion | bytes 25198592 | tf_op jit(solution)/shard_map/gather | solution.py:132
  376.6 14.1 %broadcast_select_fusion = bf16[512,16,768]{2,1,0:T(8,128)(2,1)} fusion(bf16[512,16,768]{2,1,0:T(8,128)(2,1)} %bitcast.167, bf16[512,16,768]{2,1,0:T(8,128)(2,1)} %bitcast.168, pred[512,16]{1,0:T(8,128)(4,1)S(1)} %broadcast_in_dim.90), kind=kLoop, calls=%fused_computation.19 | loop fusion | flops 6291456 | bytes 37756928 | tf_op jit(solution)/shard_map/jit(_where)/select_n | solution.py:136
  390.8 13.5 %fusion.99 = (f32[512,12]{1,0:T(8,128)S(1)}, f32[512,12,16]{2,1,0:T(8,128)S(1)}) fusion(bf16[512,16,768]{2,1,0:T(8,128)(2,1)} %broadcast_select_fusion, bf16[512,12,768]{2,0,1:T(8,128)(2,1)} %fusion.9), kind=kOutput, calls=%fused_computation.287 | convolution fusion | flops 151087104 | bytes 22437888 | tf_op jit(solution)/shard_map/thd,tkd->thk/dot_general | solution.py:506
  404.2 14.1 %exponential_reduce_fusion.1 = f32[512,12]{1,0:T(8,128)S(1)} fusion(f32[512,12,16]{2,1,0:T(8,128)S(1)} %get-tuple-element.95, f32[512,12]{1,0:T(8,128)S(1)} %get-tuple-element.94), kind=kLoop, calls=%fused_computation.50 | loop fusion | flops 190464 | bytes 442368 | tf_op jit(solution)/shard_map/reduce_sum | solution.py:55
  418.4 11.8 fusion.43
  430.3 11.5 fusion.22
  443.2 19.9 %multiply_convert_fusion.2 = (bf16[512,3072]{1,0:T(8,128)(2,1)S(1)}, f32[512,3072]{1,0:T(8,128)}, f32[512,3072]{1,0:T(8,128)}) fusion(f32[3072]{0:T(1024)S(1)} %copy-done.72, bf16[768,3072]{1,0:T(8,128)(2,1)} %param.23, f32[512,768]{1,0:T(8,128)S(1)} %get-tuple-element.99, f32[768]{0:T(1024)S(1)} %get-tuple-element.55, f32[768]{0:T(1024)S(1)} %get-tuple-element.119, ...), kind=kOutput, calls=%fused_computation.28 | convolution fusion | flops 2521694208 | bytes 22042624 | tf_op jit(solution)/shard_map/dot_general | solution.py:20
  463.3 2.8 fusion.101
  466.5 2.3 multiply_reduce_fusion.2
  469.9 4.4 convolution_convert_fusion
  474.3 8.8 fusion.103
  483.1 6.6 multiply_reduce_fusion.3
  489.7 5.0 convolution_convert_fusion.1
  497.6 11.1 fusion.26
  508.7 5.0 convert_bitcast_fusion
  513.7 15.5 %multiply_reduce_fusion.1 = (f32[512,12]{1,0:T(8,128)S(1)}, f32[512,12,16]{2,1,0:T(8,128)}) fusion(f32[512,12,16]{2,1,0:T(8,128)} %copy-done.1, f32[512,12]{1,0:T(8,128)S(1)} %log_add_fusion, bf16[512,16,768]{2,1,0:T(8,128)(2,1)} %broadcast_select_fusion, bf16[512,12,768]{2,0,1:T(8,128)(2,1)} %convert_bitcast_fusion), kind=kOutput, calls=%fused_computation.48 | convolution fusion | flops 151283712 | bytes 22855680 | tf_op jit(solution)/shard_map/thd,tkd->thk/dot_general | solution.py:567
  529.2 6.4 multiply_convert_fusion.3
  535.6 12.6 fusion.104
  548.2 11.1 multiply_convert_fusion.7
  559.3 11.6 fusion.27
  570.9 15.8 %fusion = f32[512,16,768]{2,1,0:T(8,128)} fusion(bf16[512,12,768]{2,0,1:T(8,128)(2,1)} %convert_bitcast_fusion, f32[512,12,16]{2,1,0:T(8,128)S(1)} %copy-done.2, f32[512,12]{1,0:T(8,128)S(1)} %log_add_fusion), kind=kOutput, calls=%fused_computation.6 | convolution fusion | flops 151191552 | bytes 35020800 | tf_op jit(solution)/shard_map/thk,thd->tkd/dot_general | solution.py:574
  586.7 20.5 %add_convert_fusion = bf16[512,16,768]{2,1,0:T(8,128)(2,1)} fusion(f32[512,16,768]{2,1,0:T(8,128)} %fusion, bf16[512,12,16]{2,1,0:T(8,128)(2,1)S(1)} %multiply_convert_fusion.3, bf16[512,12,768]{2,0,1:T(8,128)(2,1)} %fusion.9), kind=kOutput, calls=%fused_computation.2 | convolution fusion | flops 163577856 | bytes 47382528 | tf_op jit(solution)/shard_map/thk,thd->tkd/dot_general | solution.py:575
  607.3 3.8 multiply_reduce_fusion.4
  611.1 2.1 convolution_convert_fusion.5
  614.6 1.8 convolution_convert_fusion.4
  616.7 7.5 bitcast_reduce_fusion
  624.2 9.6 multiply_reduce_fusion
  633.8 7.3 multiply_convert_fusion.1
  641.1 2.9 multiply_convert_fusion.5
  644.0 2.0 bitcast_reduce_fusion.1
  647.6 4.9 fusion.93
  652.6 2.9 convolution_convert_fusion.3
  655.5 3.1 convert_element_type.304
  658.6 1.8 copy.126
  660.4 3.1 convert_element_type.301
  663.5 1.8 copy.125
  668.2 3.8 convolution_convert_fusion.2
  672.1 1.6 fusion.94
  673.7 2.4 copy.140
  676.1 2.4 copy.139
  679.9 2.5 constant_dynamic-update-slice_fusion.12
  682.4 2.5 constant_dynamic-update-slice_fusion.11
  696.3 2.6 constant_dynamic-update-slice_fusion
  700.5 209.2 %reduce-scatter.2.cloned.1.call-done = bf16[400,768]{1,0:T(8,128)(2,1)} async-done(((bf16[12800,768]{1,0:T(8,128)(2,1)}), bf16[400,768]{1,0:T(8,128)(2,1)}) %reduce-scatter.2.cloned.1.call-update) | async-done | bytes 614416 | tf_op jit(solution)/shard_map/reduce_scatter | solution.py:412
  909.8 5.2 add_convert_fusion.2
  915.0 124.6 %scatter_rows.1 = bf16[16384,768]{1,0:T(8,128)(2,1)} custom-call(s32[16384]{0:T(1024)} %bitcast.218, s32[16384]{0:T(1024)} %bitcast.217, s32[2048]{0:T(1024)} %or_or_fusion.twice_ref, s32[64]{0:T(128)} %and_select_fusion.2.groups_ref, bf16[8192,768]{1,0:T(8,128)(2,1)} %bitcast.165, bf16[8192,768]{1,0:T(8,128)(2,1)} %collective-permute-done.1.other_ref), custom_call_target="tpu_custom_call" | custom-call | tf_op jit(solution)/shard_map/scatter_rows/pallas_call | solution.py:218
  1039.6 254.1 %reduce_rows.1 = bf16[2,2,2,8,64,768]{5,4,3,2,1,0:T(8,128)(2,1)} custom-call(bf16[4,2,2,2,8,64,768]{6,5,4,3,2,1,0:T(8,128)(2,1)} %bitcast.166), custom_call_target="tpu_custom_call" | custom-call | tf_op jit(solution)/shard_map/reduce_rows/pallas_call | solution.py:353
  1293.7 8.6 bitcast_convert_fusion
  (293 shorter events, 57.3 us)
Async XLA Ops:
  8.0 9.3 copy-start.55
  8.0 57.2 %sort.17.cloned.1.call-start = ((), (), s32[]{:S(2)}) async-start(), calls=%async_computation.5 | async-start | bytes 393248 | tf_op jit(solution)/shard_map/sort | solution.py:200
  9.1 8.9 copy-start.44
  9.1 1.4 collective-permute-start
  12.6 160.3 %all-gather.4.cloned.1.call-start = ((), (), s32[]{:S(2)}) async-start(), calls=%async_computation.1 | async-start | bytes 25952256 | tf_op jit(solution)/shard_map/all_gather | solution.py:128
  15.3 312.8 %all-gather.6.cloned.1.call-start = ((), (), s32[]{:S(2)}) async-start(), calls=%async_computation.2 | async-start | bytes 25952256 | tf_op jit(solution)/shard_map/all_gather | solution.py:128
  15.8 893.9 %reduce-scatter.2.cloned.1.call-start = ((), (), s32[]{:S(2)}) async-start(), calls=%async_computation.3 | async-start | bytes 20275200 | tf_op jit(solution)/shard_map/reduce_scatter | solution.py:412
  21.5 6.7 slice-start.3
  36.8 3.6 copy-start.4
  37.1 3.3 copy-start.8
  37.4 5.7 copy-start.26
  38.1 403.6 %copy-start.52 = (f32[768]{0:T(1024)}, f32[768]{0:T(1024)S(1)}, u32[]{:S(2)}) copy-start(f32[768]{0:T(1024)S(1)} %get-tuple-element.120) | copy-start | bytes 9220
  38.1 403.6 %copy-start.65 = (f32[768]{0:T(1024)}, f32[768]{0:T(1024)S(1)}, u32[]{:S(2)}) copy-start(f32[768]{0:T(1024)S(1)} %get-tuple-element.54) | copy-start | bytes 9220
  38.3 4.7 copy-start.10
  40.4 4.5 copy-start
  44.9 3.4 copy-start.7
  48.4 4.7 copy-start.38
  48.4 4.7 copy-start.69
  48.4 4.7 copy-start.71
  54.0 387.7 %copy-start.14 = (f32[512,768]{1,0:T(8,128)}, f32[512,768]{1,0:T(8,128)S(1)}, u32[]{:S(2)}) copy-start(f32[512,768]{1,0:T(8,128)S(1)} %get-tuple-element.93) | copy-start | bytes 4718596
  54.0 387.7 %copy-start.50 = (f32[512]{0:T(512)}, f32[512]{0:T(512)S(1)}, u32[]{:S(2)}) copy-start(f32[512]{0:T(512)S(1)} %broadcast_multiply_fusion.8) | copy-start | bytes 6148
  54.0 3.5 copy-start.45
  54.4 387.4 %copy-start.56 = (f32[512]{0:T(512)}, f32[512]{0:T(512)S(1)}, u32[]{:S(2)}) copy-start(f32[512]{0:T(512)S(1)} %add_rsqrt_fusion.2) | copy-start | bytes 6148
  57.5 7.1 copy-start.28
  57.9 6.7 copy-start.70
  404.2 26.0 %copy-start.1 = (f32[512,12,16]{2,1,0:T(8,128)}, f32[512,12,16]{2,1,0:T(8,128)S(1)}, u32[]{:S(2)}) copy-start(f32[512,12,16]{2,1,0:T(8,128)S(1)} %get-tuple-element.95) | copy-start | bytes 1179652
  430.2 11.5 copy-start.35
  430.2 11.5 copy-start.67
  441.8 21.4 %slice-start.6 = ((s8[4718592]{0:T(1024)(128)(4,1)}), s8[4194304]{0:T(1024)(128)(4,1)S(1)}, s32[]{:S(2)}) async-start(s8[4718592]{0:T(1024)(128)(4,1)} %bitcast.220), calls=%async_computation.13 | async-start | bytes 8388608
  443.2 20.0 %slice-start.7 = ((s8[4718592]{0:T(1024)(128)(4,1)}), s8[524288]{0:T(1024)(128)(4,1)S(1)}, s32[]{:S(2)}) async-start(s8[4718592]{0:T(1024)(128)(4,1)} %bitcast.220), calls=%async_computation.14 | async-start | bytes 1048576
  443.2 20.0 %copy-start.73 = (f32[768]{0:T(1024)S(1)}, f32[768]{0:T(1024)}, u32[]{:S(2)}) copy-start(f32[768]{0:T(1024)} %param.26) | copy-start | bytes 9220
  483.1 6.6 copy-start.74
  497.5 11.1 copy-start.23
  548.2 11.1 copy-start.29
  559.3 11.6 copy-start.2
  586.6 20.6 %copy-start.40 = (bf16[12,512,64]{1,2,0:T(8,128)(2,1)S(1)}, bf16[12,512,64]{1,2,0:T(8,128)(2,1)}, u32[]{:S(2)}) copy-start(bf16[12,512,64]{1,2,0:T(8,128)(2,1)} %multiply_convert_fusion.7) | copy-start | bytes 2359300
  586.6 20.6 %copy-start.51 = (f32[512]{0:T(512)S(1)}, f32[512]{0:T(512)}, u32[]{:S(2)}) copy-start(f32[512]{0:T(512)} %copy-done.50) | copy-start | bytes 6148
  586.7 20.6 %copy-start.53 = (f32[768]{0:T(1024)S(1)}, f32[768]{0:T(1024)}, u32[]{:S(2)}) copy-start(f32[768]{0:T(1024)} %copy-done.52) | copy-start | bytes 9220
  586.7 20.6 %copy-start.57 = (f32[512]{0:T(512)S(1)}, f32[512]{0:T(512)}, u32[]{:S(2)}) copy-start(f32[512]{0:T(512)} %copy-done.56) | copy-start | bytes 6148
  607.2 3.8 copy-start.15
  607.2 3.8 copy-start.66
  616.7 7.5 copy-start.27
  616.7 17.1 %slice-start = ((s8[12582912]{0:T(1024)(128)(4,1)}), s8[4194304]{0:T(1024)(128)(4,1)S(1)}, s32[]{:S(2)}) async-start(s8[12582912]{0:T(1024)(128)(4,1)} %bitcast.162), calls=%async_computation.7 | async-start | bytes 8388608
  616.7 17.1 %slice-start.1 = ((s8[12582912]{0:T(1024)(128)(4,1)}), s8[4194304]{0:T(1024)(128)(4,1)S(1)}, s32[]{:S(2)}) async-start(s8[12582912]{0:T(1024)(128)(4,1)} %bitcast.162), calls=%async_computation.8 | async-start | bytes 8388608
  624.2 9.6 slice-start.2
  633.8 7.3 copy-start.9
  647.6 5.0 copy-start.13
  679.9 5.1 copy-start.22
  679.9 6.2 copy-start.37
  679.9 7.3 copy-start.25
  682.4 6.0 copy-start.24
  684.9 4.6 copy-start.20
  686.1 4.5 copy-start.21
  687.2 4.5 copy-start.19
  688.4 4.5 copy-start.18
  688.4 7.9 slice-start.4
  689.5 4.5 copy-start.17
  690.6 4.5 copy-start.16
  691.8 4.5 slice-start.5
  699.9 209.9 %copy-start.32 = (bf16[12,64,512]{2,1,0:T(8,128)(2,1)S(1)}, bf16[12,64,512]{2,1,0:T(8,128)(2,1)}, u32[]{:S(2)}) copy-start(bf16[12,64,512]{2,1,0:T(8,128)(2,1)} %get-tuple-element.110) | copy-start | bytes 2359300
  699.9 209.9 %copy-start.41 = (bf16[12,64,512]{2,1,0:T(8,128)(2,1)S(1)}, bf16[12,64,512]{2,1,0:T(8,128)(2,1)}, u32[]{:S(2)}) copy-start(bf16[12,64,512]{2,1,0:T(8,128)(2,1)} %multiply_convert_fusion.5) | copy-start | bytes 2359300
  699.9 602.3 %all-gather.8.cloned.1.call-start = ((), (), s32[]{:S(2)}) async-start(), calls=%async_computation.4 | async-start | bytes 3072000 | tf_op jit(solution)/shard_map/all_gather | solution.py:415
  700.2 214.8 %collective-permute-start.1 = (bf16[8192,768]{1,0:T(8,128)(2,1)}, bf16[8192,768]{1,0:T(8,128)(2,1)}, u32[]{:S(2)}, u32[]{:S(2)}) collective-permute-start(bf16[8192,768]{1,0:T(8,128)(2,1)} %bitcast.164), channel_id=1, source_target_pairs={{0,8},{8,0},{16,24},{24,16},{1,9},{9,1},{17,25},{25,17},{2,10},{10... | collective-permute-start | bytes 37748744 | tf_op jit(solution)/shard_map/ppermute | solution.py:390
  1302.2 5.8 copy-start.6
  (26 other events, 61.3 us)
Sparse Core Ops, SparseCore 0:
  12.7 4.2 sort.19.cloned.1.call-done
  909.9 23.4 all-gather.7
  (1 shorter events, 0.0 us)
Sparse Core Ops, SparseCore 1:
  16.5 156.3 all-gather.3
  176.2 151.8 all-gather.5
  700.0 209.7 reduce-scatter.1

commit v4 on v3

--- a/solution.py
+++ b/solution.py
@@ -6,6 +6,7 @@
 from jax.experimental import pallas as pl
 from jax.experimental.pallas import tpu as pltpu
 from jax.sharding import PartitionSpec as P
+
 
 D = 768
 H = 12
@@ -145,23 +146,38 @@
 GROUP = 8
 
 
-def scatter_kernel(steps, block, out_rows, row_ref, from_ref, twice_ref, groups_ref, own_ref, other_ref, out_ref, total, wide):
+SPLIT = D // 128
+
+
+def scatter_kernel(steps, block, out_rows, row_ref, from_ref, twice_ref, groups_ref, own_ref, other_ref, *rest):
+    outs, (total, wide) = rest[:-2], rest[-2:]
     step = pl.program_id(0)
 
     @pl.when(step == 0)
     def _():
         def clear(i, carry):
-            total[pl.ds(i * 32, 32), :] = jnp.zeros((32, D), jnp.float32)
+            total[pl.ds(i * 192, 192), :] = jnp.zeros((192, 128), jnp.float32)
             return carry
-        lax.fori_loop(0, total.shape[0] // 32, clear, 0)
+
+        lax.fori_loop(0, total.shape[0] // 192, clear, 0)
+
+    def widen(ref):
+        def strip(i, carry):
+            first = pl.multiple_of(i * 32, 32)
+            value = ref[pl.ds(first, 32), :].astype(jnp.float32)
+            for part in range(SPLIT):
+                wide[pl.ds(first * SPLIT + part, 32, stride=SPLIT), :] = value[:, part * 128 : (part + 1) * 128]
+            return carry
+
+        lax.fori_loop(0, block // 32, strip, 0)
 
     @pl.when(step < steps // 2)
     def _():
-        wide[...] = own_ref[...].astype(jnp.float32)
+        widen(own_ref)
 
     @pl.when((step >= steps // 2) & (step < steps))
     def _():
-        wide[...] = other_ref[...].astype(jnp.float32)
+        widen(other_ref)
 
     @pl.when(step < steps)
     def _():
@@ -173,24 +189,39 @@
 
             @pl.when(twice == 0)
             def _():
-                sums = [total[pl.ds(rows[k], 1), :] + wide[pl.ds(came[k], 1), :] for k in range(GROUP)]
+                sums = [total[pl.ds(rows[k], SPLIT), :] + wide[pl.ds(came[k], SPLIT), :] for k in range(GROUP)]
                 for k in range(GROUP):
-                    total[pl.ds(rows[k], 1), :] = sums[k]
+                    total[pl.ds(rows[k], SPLIT), :] = sums[k]
 
             @pl.when(twice != 0)
             def _():
                 for k in range(GROUP):
-                    total[pl.ds(rows[k], 1), :] = total[pl.ds(rows[k], 1), :] + wide[pl.ds(came[k], 1), :]
+                    total[pl.ds(rows[k], SPLIT), :] = total[pl.ds(rows[k], SPLIT), :] + wide[pl.ds(came[k], SPLIT), :]
+
             return carry
+
         lax.fori_loop(0, groups_ref[step], group, 0)
 
-    @pl.when(step >= steps)
-    def _():
-        first = pl.multiple_of((step - steps) * out_rows, out_rows)
-        out_ref[...] = total[pl.ds(first, out_rows), :].astype(jnp.bfloat16)
-
-
-SCATTER_BLOCK = 256
+    def narrow(out_ref):
+        def strip(i, carry):
+            first = pl.multiple_of((step - steps) * out_rows * SPLIT + i * (32 * SPLIT), 32 * SPLIT)
+            for part in range(SPLIT):
+                value = total[pl.ds(first + part, 32, stride=SPLIT), :]
+                out_ref[pl.ds(pl.multiple_of(i * 32, 32), 32), part * 128 : (part + 1) * 128] = value.astype(jnp.bfloat16)
+            return carry
+
+        lax.fori_loop(0, out_rows // 32, strip, 0)
+
+    quarter = (total.shape[0] // SPLIT // 4) // out_rows
+    for index, out_ref in enumerate(outs):
+        last = quarter * (index + 1 if index < 2 else 4)
+
+        @pl.when((step >= steps + quarter * index) & (step < steps + last))
+        def _(out_ref=out_ref):
+            narrow(out_ref)
+
+
+SCATTER_BLOCK = 1024
 
 
 def scatter_plan(where, rows):
@@ -208,16 +239,25 @@
     for shift in range(1, GROUP):
         same = eights[:, shift:] == eights[:, :-shift]
         twice = twice | jnp.any(same, axis=1).astype(jnp.int32)
-    return where.reshape(-1), (keys % SCATTER_BLOCK).reshape(-1), twice, groups
-
-
-def scatter_rows(plan, own, other, rows, out_rows=256):
+    return SPLIT * where.reshape(-1), SPLIT * (keys % SCATTER_BLOCK).reshape(-1), twice, groups
+
+
+def scatter_rows(plan, own, other, rows, out_rows=512):
     block = SCATTER_BLOCK
     half = own.shape[0] // block
     steps = 2 * half
+    quarter = rows // 4 // out_rows
+
+    def part(first, count):
+        return pl.BlockSpec((out_rows, D), lambda i, *_: (jnp.clip(i - steps - first, 0, count - 1), 0))
+
     return pl.pallas_call(
         functools.partial(scatter_kernel, steps, block, out_rows),
-        out_shape=jax.ShapeDtypeStruct((rows, D), jnp.bfloat16),
+        out_shape=[
+            jax.ShapeDtypeStruct((rows // 4, D), jnp.bfloat16),
+            jax.ShapeDtypeStruct((rows // 4, D), jnp.bfloat16),
+            jax.ShapeDtypeStruct((rows // 2, D), jnp.bfloat16),
+        ],
         grid_spec=pltpu.PrefetchScalarGridSpec(
             num_scalar_prefetch=4,
             grid=(steps + rows // out_rows,),
@@ -225,19 +265,20 @@
                 pl.BlockSpec((block, D), lambda i, *_: (jnp.minimum(i, half - 1), 0)),
                 pl.BlockSpec((block, D), lambda i, *_: (jnp.clip(i - half, 0, half - 1), 0)),
             ],
-            out_specs=pl.BlockSpec((out_rows, D), lambda i, *_: (jnp.maximum(i - steps, 0), 0)),
+            out_specs=[part(0, quarter), part(quarter, quarter), part(2 * quarter, 2 * quarter)],
             scratch_shapes=[
-                pltpu.VMEM((rows + 32, D), jnp.float32),
-                pltpu.VMEM((block, D), jnp.float32),
+                pltpu.VMEM(((rows + 32) * SPLIT, 128), jnp.float32),
+                pltpu.VMEM((block * SPLIT, 128), jnp.float32),
             ],
         ),
         compiler_params=pltpu.CompilerParams(vmem_limit_bytes=VMEM_LIMIT),
+        cost_estimate=pl.CostEstimate(flops=0, transcendentals=0, bytes_accessed=220_000_000),
         name="scatter_rows",
     )(*plan, own, other)
 
 
-def reduce_kernel(chunks, part_ref, out_ref, keep_a, keep_b, one_a, one_b, two_a, two_b, layer, along, done,
-                  keep_sem, one_send, one_recv, two_send, two_recv, z_send, z_recv,
+def reduce_kernel(chunks, keep_ref, came_a, came_b, out_ref, keep_a, keep_b, one_a, one_b, two_a, two_b, layer, along, done,
+                  keep_sem, two_send, two_recv, z_send, z_recv,
                   own_sem, y_send, y_recv, core_send, core_recv, pass_send, pass_recv):
     dp = lax.axis_index("dp")
     store = lax.axis_index("store")
@@ -259,12 +300,10 @@
                                             device_id=peer, device_id_type=MESH_ID)
 
     keeps = [(
-        pltpu.make_async_copy(part_ref.at[:, x, :, 0, q], keep_a.at[q], keep_sem.at[0, q]),
-        pltpu.make_async_copy(part_ref.at[:, :, y, 1, q], keep_b.at[q], keep_sem.at[1, q]),
-    ) for q in range(chunks)]
-    ones = [(
-        remote(part_ref.at[:, 1 - x, :, 0, q], one_a.at[q], one_send.at[0, q], one_recv.at[0, q], x_peer),
-        remote(part_ref.at[:, :, 1 - y, 1, q], one_b.at[q], one_send.at[1, q], one_recv.at[1, q], y_peer),
+        pltpu.make_async_copy(keep_ref.at[0, :, :, q], keep_a.at[q], keep_sem.at[0, q]),
+        pltpu.make_async_copy(keep_ref.at[1, :, :, q], keep_b.at[q], keep_sem.at[1, q]),
+        pltpu.make_async_copy(came_a.at[:, :, q], one_a.at[q], keep_sem.at[2, q]),
+        pltpu.make_async_copy(came_b.at[:, :, q], one_b.at[q], keep_sem.at[3, q]),
     ) for q in range(chunks)]
     twos = [(
         remote(keep_a.at[q, :, 1 - y], two_a.at[q], two_send.at[0, q], two_recv.at[0, q], y_peer),
@@ -282,29 +321,24 @@
     def plus(first, second):
         return (first.astype(jnp.float32) + second.astype(jnp.float32)).astype(jnp.bfloat16)
 
-    window = 2
-    for q in range(min(window, chunks)):
-        for copy in keeps[q] + ones[q]:
+    for q in range(chunks):
+        for copy in keeps[q]:
             copy.start()
     for step in range(chunks + 3):
         q = step
         if q < chunks:
             for copy in keeps[q]:
                 copy.wait()
-            for copy in ones[q]:
-                copy.wait_recv()
 
             def merge(i, carry, q=q):
                 for half in range(2):
                     keep_a[q, i, half] = plus(keep_a[q, i, half], one_a[q, i, half])
                     keep_b[q, i, half] = plus(keep_b[q, i, half], one_b[q, i, half])
                 return carry
+
             lax.fori_loop(0, 4, merge, 0)
             for copy in twos[q]:
                 copy.start()
-            if q + window < chunks:
-                for copy in keeps[q + window] + ones[q + window]:
-                    copy.start()
         q = step - 1
         if 0 <= q < chunks:
             for copy in twos[q]:
@@ -314,6 +348,7 @@
                 layer[q, i, 0] = plus(keep_a[q, i, y], two_a[q, i])
                 layer[q, i, 1] = plus(keep_b[q, i, x], two_b[q, i])
                 return carry
+
             lax.fori_loop(0, 4, merge_two, 0)
             for copy in zs[q]:
                 copy.start()
@@ -328,6 +363,7 @@
                     value = value + along[q, hop, i].astype(jnp.float32)
                 done[q, i] = value.astype(jnp.bfloat16)
                 return carry
+
             lax.fori_loop(0, 2, finish, 0)
             for copy in (own[q], to_y[q], to_core[q]):
                 copy.start()
@@ -336,7 +372,7 @@
             to_y[q].wait_recv()
             passed[q].start()
     for q in range(chunks):
-        for copy in ones[q] + twos[q] + tuple(zs[q]):
+        for copy in twos[q] + tuple(zs[q]):
             copy.wait_send()
         own[q].wait()
         to_y[q].wait_send()
@@ -344,38 +380,52 @@
         passed[q].wait()
 
 
-def reduce_rows(partial, collective_id=0):
-    rows = partial.shape[0] // 8
+def reduce_rows(keep, came_a, came_b, collective_id=0):
+    rows = keep.shape[0] // 4
     chunks = rows // (4 * CHUNK)
-    blocks = partial.reshape(4, 2, 2, 2, chunks, CHUNK, D)
     dma = pltpu.SemaphoreType.DMA
     vm = lambda *lead: pltpu.VMEM(lead + (CHUNK, D), jnp.bfloat16)
     out = pl.pallas_call(
         functools.partial(reduce_kernel, chunks),
         out_shape=jax.ShapeDtypeStruct((2, 2, 2, chunks, CHUNK, D), jnp.bfloat16),
-        in_specs=[pl.BlockSpec(memory_space=pl.ANY)],
+        in_specs=[pl.BlockSpec(memory_space=pl.ANY)] * 3,
         out_specs=pl.BlockSpec(memory_space=pl.ANY),
         scratch_shapes=[
             vm(chunks, 4, 2), vm(chunks, 4, 2), vm(chunks, 4, 2), vm(chunks, 4, 2),
             vm(chunks, 4), vm(chunks, 4), vm(chunks, 4, 2), vm(chunks, 3, 2), vm(chunks, 2),
-            dma((2, chunks)), dma((2, chunks)), dma((2, chunks)), dma((2, chunks)), dma((2, chunks)),
+            dma((4, chunks)), dma((2, chunks)), dma((2, chunks)),
             dma((3, chunks)), dma((3, chunks)),
             dma((chunks,)), dma((chunks,)), dma((chunks,)), dma((chunks,)), dma((chunks,)), dma((chunks,)), dma((chunks,)),
         ],
         compiler_params=pltpu.CompilerParams(collective_id=collective_id, has_side_effects=True, vmem_limit_bytes=VMEM_LIMIT),
+        cost_estimate=pl.CostEstimate(flops=0, transcendentals=0, bytes_accessed=450_000_000),
         name="reduce_rows",
-    )(blocks)
+    )(
+        keep.reshape(2, 4, 2, chunks, CHUNK, D),
+        came_a.reshape(4, 2, chunks, CHUNK, D),
+        came_b.reshape(4, 2, chunks, CHUNK, D),
+    )
     return out.reshape(2 * rows, D)
+
 
 PAIRS = ((0, 1), (1, 0), (2, 3), (3, 2))
 
 
 def own_rows(flat, rows_here):
     half = rows_here // 2
-    core = lax.rem(lax.axis_index("dp"), 2)
-    local = flat % rows_here
-    rows = lax.axis_size("store") * half
-    return jnp.where(local // half == core, (flat // rows_here) * half + local % half, rows)
+    quarter = half // 4
+    dp = lax.axis_index("dp")
+    here_y, core = dp // 2, dp % 2
+    here_x = lax.axis_index("store") % 2
+    owner, local = flat // rows_here, flat % rows_here
+    z, x = owner // 2, owner % 2
+    y = (local % half) // (2 * quarter)
+    second = (local // quarter) % 2
+    stays = jnp.where(second == 0, x == here_x, y == here_y)
+    pair = jnp.where(second == 0, y, x)
+    rows = 8 * half
+    target = (2 * stays + second) * (rows // 4) + (2 * z + pair) * quarter + local % quarter
+    return jnp.where(local // half == core, target, rows)
 
 
 def plan_store(indices, rows_here):
@@ -385,56 +435,72 @@
     return scatter_plan(where, lax.axis_size("store") * rows_here // 2)
 
 
-def reduce_store(plan, row_grad, rows_here):
-    own = row_grad.reshape(-1, D)
-    other = lax.ppermute(own, "dp", PAIRS)
-    partial = scatter_rows(plan, own, other, lax.axis_size("store") * rows_here // 2)
-    return reduce_rows(partial).astype(jnp.float32)
-
-
-def reduce_weights(squares, inner, outer, features, inner_bias):
+def add_store(plan, own, other, rows_here):
+    return scatter_rows(plan, own, other, lax.axis_size("store") * rows_here // 2)
+
+
+def swap_store(send_a, send_b):
+    owners = lax.axis_size("store")
+    came_a = lax.ppermute(send_a, "store", [(i, i ^ 1) for i in range(owners)])
+    came_b = lax.ppermute(send_b, "dp", [(i, i ^ 2) for i in range(4)])
+    return came_a, came_b
+
+
+def by_owner(matrix):
+    owners = lax.axis_size("store")
+    return matrix.astype(jnp.bfloat16).reshape(owners, -1, D)
+
+
+def reduce_packed(packed):
+    return lax.psum_scatter(
+        packed.reshape(-1, D), ("store", "dp"), scatter_dimension=0, tiled=True
+    )
+
+
+def all_copies(first, second):
+    split = first.shape[0]
+    total = lax.all_gather(jnp.concatenate([first, second]), "dp", axis=0, tiled=False)
+    total = total.astype(jnp.float32)
+    return total[:, :split].reshape(-1, D), total[:, split:].reshape(-1, D)
+
+
+def pack_early(inner, outer, squares):
+    blocks = [inner[:, block * D : (block + 1) * D] for block in range(inner.shape[1] // D)]
+    return jnp.concatenate([by_owner(piece) for piece in blocks + [outer] + list(squares)], axis=1)
+
+
+def unpack_early(total, wide):
+    part = D // lax.axis_size("store")
+    inner_total = jnp.transpose(total[: wide * part].reshape(wide, part, D), (1, 0, 2))
+    rest = total[wide * part :]
+    return (
+        inner_total.reshape(part, wide * D),
+        rest[: wide * part],
+        rest[wide * part :].reshape(-1, part, D),
+    )
+
+
+def pack_late(squares, features, inner_bias):
     owners = lax.axis_size("store")
     part = D // owners
-    wide = inner.shape[1] // D
-    low = [square.astype(jnp.bfloat16).reshape(owners, part, D) for square in squares]
-    low += [
-        inner[:, block * D : (block + 1) * D].astype(jnp.bfloat16).reshape(owners, part, D)
-        for block in range(wide)
-    ]
-    low.append(outer.astype(jnp.bfloat16).reshape(owners, wide * part, D))
+    wide = inner_bias.shape[0] // D
     small = jnp.concatenate(
         [feature.astype(jnp.bfloat16).reshape(owners, part) for feature in features]
         + [inner_bias.astype(jnp.bfloat16).reshape(owners, wide * part)],
         axis=1,
     )
     small = jnp.pad(small, ((0, 0), (0, 64 * D - small.shape[1]))).reshape(owners, 64, D)
-    packed = jnp.concatenate(low + [small], axis=1)
-    share = lax.psum_scatter(
-        packed.reshape(-1, D), ("store", "dp"), scatter_dimension=0, tiled=True
-    )
-    total = lax.all_gather(share, "dp", axis=0, tiled=True).astype(jnp.float32)
-    count = len(squares)
-    blocks = total[: (count + 2 * wide) * part].reshape(count + 2 * wide, part, D)
-    grad_proj = jnp.transpose(blocks[:6], (1, 0, 2))
-    grad_out = jnp.transpose(blocks[6:8], (1, 0, 2))
-    grad_inner = jnp.transpose(blocks[8 : 8 + wide], (1, 0, 2)).reshape(part, wide * D)
-    grad_outer = blocks[8 + wide :].reshape(wide * part, D)
-    tail = total[(count + 2 * wide) * part :].reshape(-1)
-    table = tail[: len(features) * part].reshape(len(features), part)
-    grad_bias = jnp.transpose(table[0:6])
-    grad_gain = jnp.transpose(table[6:9])
-    grad_shift = jnp.transpose(table[9:12])
-    grad_inner_bias = tail[len(features) * part :][: wide * part]
+    return jnp.concatenate([by_owner(square) for square in squares] + [small], axis=1)
+
+
+def unpack_late(total, count, features, wide):
+    part = D // lax.axis_size("store")
+    tail = total[count * part :].reshape(-1)
+    table = tail[: features * part].reshape(features, part)
     return (
-        grad_proj,
-        grad_out,
-        grad_bias,
-        grad_gain,
-        grad_shift,
-        grad_inner,
-        grad_inner_bias,
-        grad_outer,
-        table[12],
+        total[: count * part].reshape(count, part, D),
+        table,
+        tail[features * part :][: wide * part],
     )
 
 
@@ -470,7 +536,7 @@
         fetched = fetched.reshape(seq_len, K, D)
     else:
         target, request = route_slots(indices, rows_here, owners, capacity)
-        returned, asked_here = fetch_rows(request, datastore)
+        returned, _ = fetch_rows(request, datastore)
         fetched = returned.reshape(owners * capacity, D)[target].reshape(seq_len, K, D)
     self_bias = jnp.concatenate([proj_bias[:, 0], jnp.zeros((D,), jnp.float32), proj_bias[:, 1]])
     self_proj = proj_weight[:, 0:3, :].reshape(D, 3 * D)
@@ -556,6 +622,14 @@
     grad_value_heads = jnp.einsum(
         "thd,the->dhe", summary, mixed_heads, preferred_element_type=jnp.float32
     )
+    if dense:
+        packed_early = pack_early(
+            grad_inner_weight,
+            grad_outer_weight,
+            (grad_value_heads.reshape(D, D), grad_cross_out),
+        )
+        mixed_heads, packed_early = lax.optimization_barrier((mixed_heads, packed_early))
+        share_early = reduce_packed(packed_early)
     summary_low = jnp.einsum(
         "the,dhe->thd", mixed_heads, value_heads, preferred_element_type=jnp.float32
     ).astype(jnp.bfloat16)
@@ -574,6 +648,10 @@
         jnp.einsum("thk,thd->tkd", cross_probs, summary_low, preferred_element_type=jnp.float32)
         + jnp.einsum("thk,thd->tkd", score_low, folded, preferred_element_type=jnp.float32)
     ).astype(jnp.bfloat16)
+    if dense:
+        score_low, row_grad = lax.optimization_barrier((score_low, row_grad))
+        own_grad = row_grad.reshape(-1, D)
+        other_grad = lax.ppermute(own_grad, "dp", PAIRS)
     folded_low = jnp.einsum(
         "thk,tkd->thd", score_low, fetched_back, preferred_element_type=jnp.float32
     ).astype(jnp.bfloat16)
@@ -590,12 +668,15 @@
         .reshape(seq_len, D)
     )
     if dense:
-        query_low, row_grad = lax.optimization_barrier((query_low, row_grad))
+        query_low, other_grad = lax.optimization_barrier((query_low, other_grad))
+        send_a, send_b, keep = add_store(plan, own_grad, other_grad, rows_here)
+        query_low, send_a, send_b, keep = lax.optimization_barrier(
+            (query_low, send_a, send_b, keep)
+        )
+        came_a, came_b = swap_store(send_a, send_b)
     bias_three = column_sum(query_low)
     grad_cross_query = contract_rows(first_low, query_low)
-    if dense:
-        grad_store = reduce_store(plan, row_grad, rows_here)
-    else:
+    if not dense:
         grad_buffer = (
             jnp.zeros((owners * capacity, D), jnp.bfloat16)
             .at[target]
@@ -650,27 +731,44 @@
     bias_one = column_sum(joined_low[:, 2 * D :])
     grad_tokens = (first_grad + product_back(joined_low, self_proj)).astype(jnp.bfloat16)
     if dense:
-        squares = (
-            grad_self_proj[:, 0],
-            grad_self_proj[:, 1],
-            grad_self_proj[:, 2],
-            grad_cross_query,
-            grad_key_heads.reshape(D, D),
-            grad_value_heads.reshape(D, D),
-            grad_self_out,
-            grad_cross_out,
-        )
-        biases = (bias_zero, bias_one, bias_two, bias_three, bias_four, bias_five)
-        gains = (gain_one, gain_two, gain_three)
-        shifts = (shift_one, shift_two, shift_three)
-        shares = reduce_weights(
-            squares,
-            grad_inner_weight,
-            grad_outer_weight,
-            biases + gains + shifts + (grad_outer_bias,),
+        packed_late = pack_late(
+            (
+                grad_self_proj[:, 0],
+                grad_self_proj[:, 1],
+                grad_self_proj[:, 2],
+                grad_cross_query,
+                grad_key_heads.reshape(D, D),
+                grad_self_out,
+            ),
+            (bias_zero, bias_one, bias_two, bias_three, bias_four, bias_five)
+            + (gain_one, gain_two, gain_three)
+            + (shift_one, shift_two, shift_three)
+            + (grad_outer_bias,),
             grad_inner_bias,
         )
-        return (output, grad_tokens, grad_store) + shares
+        share_late = reduce_packed(packed_late)
+        keep, came_a, came_b, share_early = lax.optimization_barrier(
+            (keep, came_a, came_b, share_early)
+        )
+        grad_store = reduce_rows(keep, came_a, came_b).astype(jnp.float32)
+        wide = grad_inner_bias.shape[0] // D
+        total_early, total_late = all_copies(share_early, share_late)
+        inner_total, outer_total, early = unpack_early(total_early, wide)
+        late, table, bias_inner = unpack_late(total_late, 6, 13, wide)
+        return (
+            output,
+            grad_tokens,
+            grad_store,
+            jnp.stack([late[0], late[1], late[2], late[3], late[4], early[0]], axis=1),
+            jnp.stack([late[5], early[1]], axis=1),
+            jnp.transpose(table[0:6]),
+            jnp.transpose(table[6:9]),
+            jnp.transpose(table[9:12]),
+            inner_total,
+            bias_inner,
+            outer_total,
+            table[12],
+        )
     grad_proj = jnp.stack(
         [
             grad_self_proj[:, 0],
@@ -773,4 +871,5 @@
         P("store", None),
         P("store"),
     )
+
     return jax.shard_map(body, mesh=mesh, in_specs=in_specs, out_specs=out_specs, check_vma=False)

time: 1330 us -> 1160 us (0.87)
  Pallas kernels: 379 us -> 239 us
  waiting for transfers between devices: 417 us -> 368 us
    reduce_scatter x1 -> x2, waiting for transfers between devices: 209 us -> 0.01 us  [reduce_packed(): lax.psum_scatter(packed.reshape(-1, D), ('store', 'dp'), scatter_dimensio...]
    ppermute x1 -> x3, waiting for transfers between devices: 0.01 us -> 160 us  [the longest x1 156 us: swap_store(): came_a = lax.ppermute(send_a, 'store', [(i, i ^ 1) for i in range(owners)])]
    pallas_call x1, Pallas kernels: 254 us -> 165 us  [reduce_rows(): pl.pallas_call(functools.partial(reduce_kernel, chunks), out_shape=jax.Sh...]
    pallas_call x1, Pallas kernels: 125 us -> 74.3 us  [scatter_rows(): pl.pallas_call(functools.partial(scatter_kernel, steps, block, out_rows),...]
    unnamed x185 -> x196, local copies, waits for them, and re-layouts: 38 us -> 45.4 us
  transfers between devices with their start and end apart: 6 -> 9, of which waited for: 4 -> 5; matrix products, arithmetic and copies ran while one was open for 9% -> 20% of each run, Pallas kernels for 29% -> 21%
where the time goes in v4:
time: 1160 us; the launch traced here: 1140 us
  waiting for transfers between devices  368 us (32%)
  matrix products  251 us (22%)
  Pallas kernels  239 us (21%)
  local copies, waits for them, and re-layouts  193 us (17%)
  other arithmetic  72.4 us (6%)
  between operations  18.2 us (2%)
    all_gather x2, waiting for transfers between devices, fetch_dense(): table = lax.all_gather(mine, ('store', 'dp'), axis=0, tiled=True)  207 us
    pallas_call x1, Pallas kernels, reduce_rows(): pl.pallas_call(functools.partial(reduce_kernel, chunks), out_shape=jax.Sh...  165 us
    ppermute x1, waiting for transfers between devices, swap_store(): came_a = lax.ppermute(send_a, 'store', [(i, i ^ 1) for i in range(owners)])  156 us
    gather x2, local copies, waits for them, and re-layouts, fetch_dense(): rows = table[local]  97.2 us
    pallas_call x1, Pallas kernels, scatter_rows(): pl.pallas_call(functools.partial(scatter_kernel, steps, block, out_rows),...  74.3 us
    unnamed x196, local copies, waits for them, and re-layouts  45.4 us
    dot_general x6, matrix products, product(): return jnp.dot(matrix, factor, preferred_element_type=jnp.float32)  31.7 us
    dot_general x6, matrix products, product_back(): jnp.einsum('tf,df->td', matrix, weight, preferred_element_type=jnp.float32)  29 us
  transfers between devices with their start and end apart: 9, of which 5 were waited for; matrix products, arithmetic and copies ran while one was open for 20% of the time, Pallas kernels for 21%

profile of v4, /device:TPU:0, one launch (start us, length us, event | category | flops | bytes accessed | tf_op | source)
XLA Modules:
  0.0 1144.0 jit_solution(5347399352754416598)
XLA Ops:
  12.7 2.6 constant_dynamic-slice_fusion
  18.6 2.5 copy-done.4
  22.7 2.5 copy.103
  25.3 2.4 copy.109
  27.6 3.7 copy.135
  31.3 4.3 fusion.17
  37.6 2.1 fusion.8
  39.8 2.6 exponential_reduce_fusion
  42.4 1.9 copy-done
  44.3 3.4 convolution_convert_fusion.10
  47.8 4.7 fusion.122
  53.9 2.6 add_convert_fusion.3
  57.2 6.8 fusion.9
  72.6 100.3 %all-gather.5.cloned.1.call-done = bf16[16384,768]{1,0:T(8,128)(2,1)} async-done(((bf16[512,768]{1,0:T(8,128)(2,1)}), bf16[16384,768]{1,0:T(8,128)(2,1)}) %all-gather.5.cloned.1.call-update) | async-done | bytes 25165840 | tf_op jit(solution)/shard_map/all_gather | solution.py:129
  172.9 48.4 %gather_fusion = bf16[8192,768]{1,0:T(8,128)(2,1)} fusion(bf16[16384,768]{1,0:T(8,128)(2,1)} %all-gather.5.cloned.1.call-done, s32[8192]{0:T(1024)S(1)} %broadcast_clamp_fusion), kind=kCustom, calls=%fused_computation | custom fusion | bytes 25198592 | tf_op jit(solution)/shard_map/gather | solution.py:133
  221.4 106.8 %all-gather.7.cloned.1.call-done = bf16[16384,768]{1,0:T(8,128)(2,1)} async-done(((bf16[512,768]{1,0:T(8,128)(2,1)}), bf16[16384,768]{1,0:T(8,128)(2,1)}) %all-gather.7.cloned.1.call-update) | async-done | bytes 25165840 | tf_op jit(solution)/shard_map/all_gather | solution.py:129
  328.2 48.8 %gather_fusion.1 = bf16[8192,768]{1,0:T(8,128)(2,1)} fusion(bf16[16384,768]{1,0:T(8,128)(2,1)} %all-gather.7.cloned.1.call-done, s32[8192]{0:T(1024)S(1)} %broadcast_clamp_fusion), kind=kCustom, calls=%fused_computation.1 | custom fusion | bytes 25198592 | tf_op jit(solution)/shard_map/gather | solution.py:133
  377.0 14.1 %broadcast_select_fusion = bf16[512,16,768]{2,1,0:T(8,128)(2,1)} fusion(bf16[512,16,768]{2,1,0:T(8,128)(2,1)} %bitcast.193, bf16[512,16,768]{2,1,0:T(8,128)(2,1)} %bitcast.194, pred[512,16]{1,0:T(8,128)(4,1)S(1)} %broadcast_in_dim.90), kind=kLoop, calls=%fused_computation.19 | loop fusion | flops 6291456 | bytes 37756928 | tf_op jit(solution)/shard_map/jit(_where)/select_n | solution.py:137
  391.1 13.5 %fusion.125 = (f32[512,12]{1,0:T(8,128)S(1)}, f32[512,12,16]{2,1,0:T(8,128)S(1)}) fusion(bf16[512,16,768]{2,1,0:T(8,128)(2,1)} %broadcast_select_fusion, bf16[512,12,768]{2,0,1:T(8,128)(2,1)} %fusion.9), kind=kOutput, calls=%fused_computation.358 | convolution fusion | flops 151087104 | bytes 22437888 | tf_op jit(solution)/shard_map/thd,tkd->thk/dot_general | solution.py:572
  404.6 14.1 %exponential_reduce_fusion.1 = f32[512,12]{1,0:T(8,128)S(1)} fusion(f32[512,12,16]{2,1,0:T(8,128)S(1)} %get-tuple-element.162, f32[512,12]{1,0:T(8,128)S(1)} %get-tuple-element.161), kind=kLoop, calls=%fused_computation.50 | loop fusion | flops 190464 | bytes 442368 | tf_op jit(solution)/shard_map/reduce_sum | solution.py:56
  418.8 11.8 %fusion.43 = bf16[512,12,768]{2,1,0:T(8,128)(2,1)} fusion(bf16[512,16,768]{2,1,0:T(8,128)(2,1)} %broadcast_select_fusion, f32[512,12,16]{2,1,0:T(8,128)S(1)} %get-tuple-element.162, f32[512,12]{1,0:T(8,128)S(1)} %log_add_fusion), kind=kOutput, calls=%fused_computation.132 | convolution fusion | flops 151191552 | bytes 22437888 | tf_op jit(solution)/shard_map/thk,tkd->thd/dot_general | solution.py:576
  430.6 10.3 fusion.22
  442.4 19.9 %multiply_convert_fusion.2 = (bf16[512,3072]{1,0:T(8,128)(2,1)S(1)}, f32[512,3072]{1,0:T(8,128)}, f32[512,3072]{1,0:T(8,128)}) fusion(f32[3072]{0:T(1024)S(1)} %copy-done.79, bf16[768,3072]{1,0:T(8,128)(2,1)} %param.23, f32[512,768]{1,0:T(8,128)S(1)} %get-tuple-element.166, f32[768]{0:T(1024)S(1)} %get-tuple-element.121, f32[768]{0:T(1024)S(1)} %get-tuple-element.186, ...), kind=kOutput, calls=%fused_computation.28 | convolution fusion | flops 2521694208 | bytes 22042624 | tf_op jit(solution)/shard_map/dot_general | solution.py:21
  462.4 2.8 fusion.127
  467.9 4.4 convolution_convert_fusion.1
  472.4 8.8 fusion.129
  481.2 6.6 multiply_reduce_fusion.3
  487.7 3.6 convolution_convert_fusion.2
  492.9 1.9 fusion.119
  497.8 11.0 fusion.26
  508.8 3.1 convert_element_type.287
  511.9 1.8 copy.112
  513.7 2.5 constant_dynamic-update-slice_fusion.6
  516.2 2.4 constant_dynamic-update-slice_fusion.5
  520.8 5.0 constant_dynamic-update-slice_fusion.2
  528.0 5.1 convert_bitcast_fusion
  533.1 16.5 %multiply_reduce_fusion.1 = (f32[512,12]{1,0:T(8,128)}, f32[512,12,16]{2,1,0:T(8,128)}) fusion(f32[512,12,16]{2,1,0:T(8,128)} %copy-done.1, f32[512,12]{1,0:T(8,128)S(1)} %log_add_fusion, bf16[512,16,768]{2,1,0:T(8,128)(2,1)} %broadcast_select_fusion, bf16[512,12,768]{2,0,1:T(8,128)(2,1)} %convert_bitcast_fusion), kind=kOutput, calls=%fused_computation.48 | convolution fusion | flops 151283712 | bytes 22855680 | tf_op jit(solution)/shard_map/thd,tkd->thk/dot_general | solution.py:641
  549.6 16.5 %fusion = f32[512,16,768]{2,1,0:T(8,128)} fusion(bf16[512,12,768]{2,0,1:T(8,128)(2,1)} %convert_bitcast_fusion, f32[512,12,16]{2,1,0:T(8,128)} %copy-done.1, f32[512,12]{1,0:T(8,128)S(1)} %log_add_fusion), kind=kOutput, calls=%fused_computation.6 | convolution fusion | flops 151191552 | bytes 35020800 | tf_op jit(solution)/shard_map/thk,thd->tkd/dot_general | solution.py:648
  566.1 6.7 multiply_convert_fusion.3
  572.9 20.7 %add_convert_fusion = bf16[512,16,768]{2,1,0:T(8,128)(2,1)} fusion(f32[512,16,768]{2,1,0:T(8,128)} %fusion, bf16[512,12,16]{2,1,0:T(8,128)(2,1)S(1)} %multiply_convert_fusion.3, bf16[512,12,768]{2,0,1:T(8,128)(2,1)} %fusion.9), kind=kOutput, calls=%fused_computation.2 | convolution fusion | flops 163577856 | bytes 47382528 | tf_op jit(solution)/shard_map/thk,thd->tkd/dot_general | solution.py:649
  599.1 13.7 %fusion.130 = bf16[512,12,768]{2,1,0:T(8,128)(2,1)} fusion(bf16[512,12,16]{2,1,0:T(8,128)(2,1)S(1)} %multiply_convert_fusion.3, bf16[512,16,768]{2,1,0:T(8,128)(2,1)} %broadcast_select_fusion), kind=kOutput, calls=%fused_computation.363 | convolution fusion | flops 150994944 | bytes 22216704 | tf_op jit(solution)/shard_map/thk,tkd->thd/dot_general | solution.py:655
  612.9 11.7 %fusion.27 = bf16[768,12,64]{0,2,1:T(8,128)(2,1)} fusion(bf16[512,12,64]{0,2,1:T(8,128)(2,1)S(1)} %bitcast.235, bf16[512,12,768]{2,1,0:T(8,128)(2,1)} %fusion.130), kind=kOutput, calls=%fused_computation.97 | convolution fusion | flops 605159424 | bytes 11403264 | tf_op jit(solution)/shard_map/thd,the->dhe/dot_general | solution.py:659
  624.5 3.4 convert_element_type.309
  628.0 1.8 copy.126
  629.8 11.5 %multiply_convert_fusion.7 = bf16[12,512,64]{1,2,0:T(8,128)(2,1)} fusion(bf16[768,12,64]{0,2,1:T(8,128)(2,1)S(1)} %bitcast.223, bf16[512,12,768]{2,1,0:T(8,128)(2,1)} %fusion.130), kind=kOutput, calls=%fused_computation.66 | convolution fusion | flops 604766208 | bytes 11403264 | tf_op jit(solution)/shard_map/thd,dhe->the/dot_general | solution.py:664
  641.2 74.3 %scatter_rows.1 = (bf16[4096,768]{1,0:T(8,128)(2,1)}, bf16[4096,768]{1,0:T(8,128)(2,1)}, bf16[8192,768]{1,0:T(8,128)(2,1)}) custom-call(s32[16384]{0:T(1024)} %bitcast.250, s32[16384]{0:T(1024)} %bitcast.251, s32[2048]{0:T(1024)} %or_or_fusion.twice_ref, s32[16]{0:T(128)} %and_select_fusion.2.groups_ref, bf16[8192,768]{1,0:T(8,128)(2,1)} %bitcast.192, ...), custom_call_target="tpu_custom_call" | custom-call | bytes 220000000 | tf_op jit(solution)/shard_map/scatter_rows/pallas_call | solution.py:254
  717.0 4.9 multiply_reduce_fusion.4
  722.0 2.4 convert_reduce_fusion.2
  724.5 2.7 convolution_convert_fusion.7
  728.5 9.0 bitcast_reduce_fusion
  737.5 7.5 multiply_reduce_fusion
  745.1 7.3 multiply_convert_fusion.1
  756.3 4.9 multiply_convert_fusion.5
  761.3 2.0 convolution_convert_fusion
  764.9 2.4 copy.140
  767.3 2.4 copy.139
  771.2 2.5 constant_dynamic-update-slice_fusion.12
  773.7 2.3 constant_dynamic-update-slice_fusion.11
  784.7 156.0 %collective-permute-done.2 = bf16[4096,768]{1,0:T(8,128)(2,1)} collective-permute-done((bf16[4096,768]{1,0:T(8,128)(2,1)}, bf16[4096,768]{1,0:T(8,128)(2,1)}, u32[]{:S(2)}, u32[]{:S(2)}) %collective-permute-start.2) | collective-permute-done | bytes 6291488 | tf_op jit(solution)/shard_map/ppermute | solution.py:444
  940.8 4.0 collective-permute-done.3
  944.8 2.0 pad_maximum_fusion.3
  946.8 5.2 add_convert_fusion.2
  952.0 164.5 %reduce_rows.1 = bf16[2,2,2,8,64,768]{5,4,3,2,1,0:T(8,128)(2,1)} custom-call(bf16[2,4,2,8,64,768]{5,4,3,2,1,0:T(8,128)(2,1)} %bitcast.195, bf16[4,2,8,64,768]{4,3,2,1,0:T(8,128)(2,1)} %bitcast.41.came_a, bf16[4,2,8,64,768]{4,3,2,1,0:T(8,128)(2,1)} %bitcast.42.came_b), custom_call_target="tpu_custom_call" | custom-call | bytes 450000000 | tf_op jit(solution)/shard_map/reduce_rows/pallas_call | solution.py:388
  1116.5 8.6 bitcast_convert_fusion
  (314 shorter events, 69.2 us)
Async XLA Ops:
  8.0 9.4 copy-start.57
  8.0 56.5 %sort.17.cloned.1.call-start = ((), (), s32[]{:S(2)}) async-start(), calls=%async_computation.7 | async-start | bytes 393248 | tf_op jit(solution)/shard_map/sort | solution.py:231
  9.1 9.0 copy-start.44
  9.1 1.4 collective-permute-start
  12.7 160.3 %all-gather.5.cloned.1.call-start = ((), (), s32[]{:S(2)}) async-start(), calls=%async_computation.2 | async-start | bytes 25952256 | tf_op jit(solution)/shard_map/all_gather | solution.py:129
  15.3 312.8 %all-gather.7.cloned.1.call-start = ((), (), s32[]{:S(2)}) async-start(), calls=%async_computation.3 | async-start | bytes 25952256 | tf_op jit(solution)/shard_map/all_gather | solution.py:129
  15.9 768.8 %reduce-scatter.3.cloned.1.call-start = ((), (), s32[]{:S(2)}) async-start(), calls=%async_computation.4 | async-start | bytes 12165120 | tf_op jit(solution)/shard_map/reduce_scatter | solution.py:455
  22.7 4.9 slice-start
  36.1 3.6 copy-start.5
  36.4 3.3 copy-start.11
  36.7 5.7 copy-start.25
  37.5 403.4 %copy-start.54 = (f32[768]{0:T(1024)}, f32[768]{0:T(1024)S(1)}, u32[]{:S(2)}) copy-start(f32[768]{0:T(1024)S(1)} %get-tuple-element.187) | copy-start | bytes 9220
  37.5 403.4 %copy-start.71 = (f32[768]{0:T(1024)}, f32[768]{0:T(1024)S(1)}, u32[]{:S(2)}) copy-start(f32[768]{0:T(1024)S(1)} %get-tuple-element.120) | copy-start | bytes 9220
  37.6 4.7 copy-start.13
  39.7 4.6 copy-start
  44.3 3.4 copy-start.8
  47.8 4.7 copy-start.37
  47.8 4.7 copy-start.75
  47.8 4.7 copy-start.77
  53.5 387.5 %copy-start.16 = (f32[512,768]{1,0:T(8,128)}, f32[512,768]{1,0:T(8,128)S(1)}, u32[]{:S(2)}) copy-start(f32[512,768]{1,0:T(8,128)S(1)} %get-tuple-element.160) | copy-start | bytes 4718596
  53.5 387.5 %copy-start.52 = (f32[512]{0:T(512)}, f32[512]{0:T(512)S(1)}, u32[]{:S(2)}) copy-start(f32[512]{0:T(512)S(1)} %broadcast_multiply_fusion.8) | copy-start | bytes 6148
  53.8 387.1 %copy-start.58 = (f32[512]{0:T(512)}, f32[512]{0:T(512)S(1)}, u32[]{:S(2)}) copy-start(f32[512]{0:T(512)S(1)} %add_rsqrt_fusion.2) | copy-start | bytes 6148
  56.8 7.1 copy-start.27
  57.2 6.8 copy-start.76
  404.6 25.9 %copy-start.1 = (f32[512,12,16]{2,1,0:T(8,128)}, f32[512,12,16]{2,1,0:T(8,128)S(1)}, u32[]{:S(2)}) copy-start(f32[512,12,16]{2,1,0:T(8,128)S(1)} %get-tuple-element.162) | copy-start | bytes 1179652
  430.5 10.4 copy-start.36
  430.5 10.4 copy-start.73
  441.0 21.4 %slice-start.1 = ((s8[4718592]{0:T(1024)(128)(4,1)}), s8[4194304]{0:T(1024)(128)(4,1)S(1)}, s32[]{:S(2)}) async-start(s8[4718592]{0:T(1024)(128)(4,1)} %bitcast.253), calls=%async_computation.10 | async-start | bytes 8388608
  442.4 19.9 %slice-start.2 = ((s8[4718592]{0:T(1024)(128)(4,1)}), s8[524288]{0:T(1024)(128)(4,1)S(1)}, s32[]{:S(2)}) async-start(s8[4718592]{0:T(1024)(128)(4,1)} %bitcast.253), calls=%async_computation.11 | async-start | bytes 1048576
  442.4 19.9 %copy-start.80 = (f32[768]{0:T(1024)S(1)}, f32[768]{0:T(1024)}, u32[]{:S(2)}) copy-start(f32[768]{0:T(1024)} %param.26) | copy-start | bytes 9220
  462.4 3.2 copy-start.32
  462.4 3.2 copy-start.48
  462.4 3.2 copy-start.56
  481.2 6.6 copy-start.82
  487.7 3.6 copy-start.50
  513.7 4.9 copy-start.18
  520.8 5.0 copy-start.24
  520.8 6.1 copy-start.19
  549.6 16.5 %copy-start.2 = (f32[512,12,16]{2,1,0:T(8,128)S(1)}, f32[512,12,16]{2,1,0:T(8,128)}, u32[]{:S(2)}) copy-start(f32[512,12,16]{2,1,0:T(8,128)} %copy-done.1) | copy-start | bytes 1179652
  593.6 47.6 %collective-permute-start.1 = (bf16[8192,768]{1,0:T(8,128)(2,1)}, bf16[8192,768]{1,0:T(8,128)(2,1)}, u32[]{:S(2)}, u32[]{:S(2)}) collective-permute-start(bf16[8192,768]{1,0:T(8,128)(2,1)} %bitcast.191), channel_id=1, source_target_pairs={{0,8},{8,0},{16,24},{24,16},{1,9},{9,1},{17,25},{25,17},{2,10},{10... | collective-permute-start | bytes 37748744 | tf_op jit(solution)/shard_map/ppermute | solution.py:654
  593.9 350.9 %reduce-scatter.5.cloned.1.call-start = ((), (), s32[]{:S(2)}) async-start(), calls=%async_computation.5 | async-start | bytes 8110080 | tf_op jit(solution)/shard_map/reduce_scatter | solution.py:455
  599.1 13.7 %copy-start.28 = (bf16[512,768]{0,1:T(8,128)(2,1)S(1)}, bf16[512,768]{0,1:T(8,128)(2,1)}, u32[]{:S(2)}) copy-start(bf16[512,768]{0,1:T(8,128)(2,1)} %copy-done.27) | copy-start | bytes 2359300
  624.5 5.2 copy-start.21
  717.0 5.0 copy-start.53
  717.0 5.0 copy-start.55
  717.0 5.0 copy-start.59
  724.4 4.1 copy-start.14
  724.4 4.1 copy-start.43
  728.5 9.1 copy-start.26
  745.1 7.3 copy-start.6
  752.5 3.8 copy-start.12
  755.1 6.1 copy-start.33
  756.3 4.9 copy-start.78
  756.3 4.9 copy-start.81
  771.1 4.9 copy-start.20
  771.1 6.0 copy-start.17
  771.2 6.0 copy-start.39
  771.2 6.0 copy-start.72
  783.6 163.2 %copy-start.34 = (bf16[12,64,512]{2,1,0:T(8,128)(2,1)S(1)}, bf16[12,64,512]{2,1,0:T(8,128)(2,1)}, u32[]{:S(2)}) copy-start(bf16[12,64,512]{2,1,0:T(8,128)(2,1)} %copy-done.33) | copy-start | bytes 2359300
  783.6 163.2 %copy-start.41 = (bf16[12,64,512]{2,1,0:T(8,128)(2,1)S(1)}, bf16[12,64,512]{2,1,0:T(8,128)(2,1)}, u32[]{:S(2)}) copy-start(bf16[12,64,512]{2,1,0:T(8,128)(2,1)} %copy-done.40) | copy-start | bytes 2359300
  783.6 341.5 %all-gather.9.cloned.1.call-start = ((), (), s32[]{:S(2)}) async-start(), calls=%async_computation.6 | async-start | bytes 3072000 | tf_op jit(solution)/shard_map/all_gather | solution.py:462
  783.6 157.1 %collective-permute-start.2 = (bf16[4096,768]{1,0:T(8,128)(2,1)}, bf16[4096,768]{1,0:T(8,128)(2,1)}, u32[]{:S(2)}, u32[]{:S(2)}) collective-permute-start(bf16[4096,768]{1,0:T(8,128)(2,1)} %get-tuple-element.55), channel_id=1, source_target_pairs={{0,1},{1,0},{2,3},{3,2},{4,5},{5,4},{6,7},{7,6},{8,9},{9,8},{10,11... | collective-permute-start | bytes 18874376 | tf_op jit(solution)/shard_map/ppermute | solution.py:444
  784.7 160.0 %collective-permute-start.3 = (bf16[4096,768]{1,0:T(8,128)(2,1)}, bf16[4096,768]{1,0:T(8,128)(2,1)}, u32[]{:S(2)}, u32[]{:S(2)}) collective-permute-start(bf16[4096,768]{1,0:T(8,128)(2,1)} %get-tuple-element.56), channel_id=1, source_target_pairs={{0,16},{8,24},{16,0},{24,8},{1,17},{9,25},{17,1},{25,9},{2,18},{10... | collective-permute-start | bytes 18874376 | tf_op jit(solution)/shard_map/ppermute | solution.py:445
  1125.1 6.3 copy-start.7
  (32 other events, 70.8 us)
Sparse Core Ops, SparseCore 0:
  12.8 5.5 sort.19.cloned.1.call-done
  946.9 32.6 all-gather.8
  (1 shorter events, 0.0 us)
Sparse Core Ops, SparseCore 1:
  16.6 156.3 all-gather.4
  176.3 151.8 all-gather.6
  594.0 146.6 reduce-scatter.2
  783.7 142.3 reduce-scatter.4

commit v5 on v4

--- a/solution.py
+++ b/solution.py
@@ -120,7 +120,7 @@
     which = (flat % share) // part
     local = (flat // share) * part + flat % part
     start = lax.axis_index("dp") * share
-    fetched = None
+    found = []
     earlier = None
     for index in range(STORE_PARTS):
         mine = lax.dynamic_slice_in_dim(datastore, start + index * part, part, axis=0)
@@ -130,12 +130,8 @@
         earlier = mine
         if index == STORE_PARTS - 1:
             which, plan = lax.optimization_barrier((which, plan))
-        rows = table[local]
-        if fetched is None:
-            fetched = rows
-        else:
-            fetched = jnp.where((which == index)[:, None], rows, fetched)
-    return fetched, plan
+        found.append(table[local])
+    return found[0], found[1], which[:, None], plan
 
 
 MESH_ID = pl.DeviceIdType.MESH
@@ -457,11 +453,8 @@
     )
 
 
-def all_copies(first, second):
-    split = first.shape[0]
-    total = lax.all_gather(jnp.concatenate([first, second]), "dp", axis=0, tiled=False)
-    total = total.astype(jnp.float32)
-    return total[:, :split].reshape(-1, D), total[:, split:].reshape(-1, D)
+def all_copies(share):
+    return lax.all_gather(share, "dp", axis=0, tiled=True).astype(jnp.float32)
 
 
 def pack_early(inner, outer, squares):
@@ -502,6 +495,98 @@
         table,
         tail[features * part :][: wide * part],
     )
+
+
+def cross_probs_of(folded, rows):
+    scores = lax.dot_general(folded, rows, (((1,), (1,)), ((), ())), preferred_element_type=jnp.float32)
+    token = lax.broadcasted_iota(jnp.int32, scores.shape, 0) % CROSS_TOKENS
+    owner = lax.broadcasted_iota(jnp.int32, scores.shape, 1) // K
+    scores = jnp.where(token == owner, scores, -1e30)
+    raised = jnp.exp(scores - jnp.max(scores, axis=1, keepdims=True))
+    return raised * (1.0 / jnp.sum(raised, axis=1, keepdims=True))
+
+
+def cross_tiles(ref):
+    tokens = ref.shape[1]
+    for first in range(0, tokens, CROSS_TOKENS):
+        yield pl.ds(first, CROSS_TOKENS), pl.ds(first * K, CROSS_TOKENS * K)
+
+
+def cross_forward_kernel(folded_ref, first_ref, second_ref, which_ref, rows_ref, summary_ref):
+    for some, slots in cross_tiles(folded_ref):
+        which = which_ref[slots, :] != 0
+        rows = jnp.where(
+            which, second_ref[slots, :].astype(jnp.float32), first_ref[slots, :].astype(jnp.float32)
+        ).astype(jnp.bfloat16)
+        rows_ref[slots, :] = rows
+        probs = cross_probs_of(folded_ref[:, some, :].reshape(H * CROSS_TOKENS, D), rows)
+        summary = jnp.dot(probs.astype(jnp.bfloat16), rows, preferred_element_type=jnp.float32)
+        summary_ref[:, some, :] = summary.astype(jnp.bfloat16).reshape(H, CROSS_TOKENS, D)
+
+
+def cross_backward_kernel(folded_ref, grad_ref, rows_ref, row_grad_ref, folded_grad_ref):
+    for some, slots in cross_tiles(folded_ref):
+        rows = rows_ref[slots, :]
+        folded = folded_ref[:, some, :].reshape(H * CROSS_TOKENS, D)
+        grad = grad_ref[:, some, :].reshape(H * CROSS_TOKENS, D)
+        probs = cross_probs_of(folded, rows)
+        prob_grad = lax.dot_general(
+            grad, rows, (((1,), (1,)), ((), ())), preferred_element_type=jnp.float32
+        )
+        total = jnp.sum(probs * prob_grad, axis=1, keepdims=True)
+        score_low = (probs * (prob_grad - total)).astype(jnp.bfloat16)
+        turned = (((0,), (0,)), ((), ()))
+        row_grad = lax.dot_general(
+            probs.astype(jnp.bfloat16), grad, turned, preferred_element_type=jnp.float32
+        )
+        row_grad += lax.dot_general(score_low, folded, turned, preferred_element_type=jnp.float32)
+        row_grad_ref[slots, :] = row_grad.astype(jnp.bfloat16)
+        folded_grad = jnp.dot(score_low, rows, preferred_element_type=jnp.float32)
+        folded_grad_ref[:, some, :] = folded_grad.astype(jnp.bfloat16).reshape(H, CROSS_TOKENS, D)
+
+
+CROSS_TOKENS = 16
+CROSS_STEP = 64
+
+
+def cross_specs():
+    heads = pl.BlockSpec((H, CROSS_STEP, D), lambda i: (0, i, 0))
+    rows = pl.BlockSpec((CROSS_STEP * K, D), lambda i: (i, 0))
+    return heads, rows
+
+
+def cross_forward(folded, first, second, which):
+    heads, rows = cross_specs()
+    tokens = folded.shape[1]
+    return pl.pallas_call(
+        cross_forward_kernel,
+        out_shape=[
+            jax.ShapeDtypeStruct((tokens * K, D), jnp.bfloat16),
+            jax.ShapeDtypeStruct((H, tokens, D), jnp.bfloat16),
+        ],
+        grid=(tokens // CROSS_STEP,),
+        in_specs=[heads, rows, rows, pl.BlockSpec((CROSS_STEP * K, 1), lambda i: (i, 0))],
+        out_specs=[rows, heads],
+        cost_estimate=pl.CostEstimate(flops=0, transcendentals=0, bytes_accessed=65_000_000),
+        name="cross_forward",
+    )(folded, first, second, which)
+
+
+def cross_backward(folded, grad, fetched):
+    heads, rows = cross_specs()
+    tokens = folded.shape[1]
+    return pl.pallas_call(
+        cross_backward_kernel,
+        out_shape=[
+            jax.ShapeDtypeStruct((tokens * K, D), jnp.bfloat16),
+            jax.ShapeDtypeStruct((H, tokens, D), jnp.bfloat16),
+        ],
+        grid=(tokens // CROSS_STEP,),
+        in_specs=[heads, heads, rows],
+        out_specs=[rows, heads],
+        cost_estimate=pl.CostEstimate(flops=0, transcendentals=0, bytes_accessed=100_000_000),
+        name="cross_backward",
+    )(folded, grad, fetched)
 
 
 def body(
@@ -532,8 +617,7 @@
     dense = is_dense(owners, rows_here)
     if dense:
         plan = plan_store(indices, rows_here)
-        fetched, plan = fetch_dense(datastore, indices, plan)
-        fetched = fetched.reshape(seq_len, K, D)
+        found_first, found_second, which_half, plan = fetch_dense(datastore, indices, plan)
     else:
         target, request = route_slots(indices, rows_here, owners, capacity)
         returned, _ = fetch_rows(request, datastore)
@@ -569,13 +653,18 @@
         jnp.einsum("the,dhe->thd", cross_query, key_heads, preferred_element_type=jnp.float32)
         * score_scale
     ).astype(jnp.bfloat16)
-    cross_scores = jnp.einsum("thd,tkd->thk", folded, fetched, preferred_element_type=jnp.float32)
-    cross_lse = log_total(cross_scores)
-    cross_full = jnp.exp(cross_scores - cross_lse)
-    cross_probs = cross_full.astype(jnp.bfloat16)
-    summary = jnp.einsum(
-        "thk,tkd->thd", cross_probs, fetched, preferred_element_type=jnp.float32
-    ).astype(jnp.bfloat16)
+    if dense:
+        folded_heads = jnp.transpose(folded, (1, 0, 2))
+        fetched, summary = cross_forward(folded_heads, found_first, found_second, which_half)
+        summary = jnp.transpose(summary, (1, 0, 2))
+    else:
+        cross_scores = jnp.einsum("thd,tkd->thk", folded, fetched, preferred_element_type=jnp.float32)
+        cross_lse = log_total(cross_scores)
+        cross_full = jnp.exp(cross_scores - cross_lse)
+        cross_probs = cross_full.astype(jnp.bfloat16)
+        summary = jnp.einsum(
+            "thk,tkd->thd", cross_probs, fetched, preferred_element_type=jnp.float32
+        ).astype(jnp.bfloat16)
     value_heads = proj_weight[:, 5, :].reshape(D, H, HD)
     cross_mixed = (
         jnp.einsum(
@@ -623,38 +712,34 @@
         "thd,the->dhe", summary, mixed_heads, preferred_element_type=jnp.float32
     )
     if dense:
-        packed_early = pack_early(
-            grad_inner_weight,
-            grad_outer_weight,
-            (grad_value_heads.reshape(D, D), grad_cross_out),
-        )
+        packed_early = pack_early(grad_inner_weight, grad_outer_weight, (grad_cross_out,))
         mixed_heads, packed_early = lax.optimization_barrier((mixed_heads, packed_early))
         share_early = reduce_packed(packed_early)
     summary_low = jnp.einsum(
         "the,dhe->thd", mixed_heads, value_heads, preferred_element_type=jnp.float32
     ).astype(jnp.bfloat16)
     if dense:
-        fetched_back = fetched
+        own_grad, folded_low = cross_backward(
+            folded_heads, jnp.transpose(summary_low, (1, 0, 2)), fetched
+        )
+        folded_low = jnp.transpose(folded_low, (1, 0, 2))
+        other_grad = lax.ppermute(own_grad, "dp", PAIRS)
     else:
         returned_again, asked_back = fetch_again(request, datastore)
         fetched_back = returned_again.reshape(owners * capacity, D)[target].reshape(seq_len, K, D)
-    prob_grad = jnp.einsum(
-        "thd,tkd->thk", summary_low, fetched_back, preferred_element_type=jnp.float32
-    )
-    score_low = (
-        cross_full * (prob_grad - jnp.sum(cross_full * prob_grad, axis=-1, keepdims=True))
-    ).astype(jnp.bfloat16)
-    row_grad = (
-        jnp.einsum("thk,thd->tkd", cross_probs, summary_low, preferred_element_type=jnp.float32)
-        + jnp.einsum("thk,thd->tkd", score_low, folded, preferred_element_type=jnp.float32)
-    ).astype(jnp.bfloat16)
-    if dense:
-        score_low, row_grad = lax.optimization_barrier((score_low, row_grad))
-        own_grad = row_grad.reshape(-1, D)
-        other_grad = lax.ppermute(own_grad, "dp", PAIRS)
-    folded_low = jnp.einsum(
-        "thk,tkd->thd", score_low, fetched_back, preferred_element_type=jnp.float32
-    ).astype(jnp.bfloat16)
+        prob_grad = jnp.einsum(
+            "thd,tkd->thk", summary_low, fetched_back, preferred_element_type=jnp.float32
+        )
+        score_low = (
+            cross_full * (prob_grad - jnp.sum(cross_full * prob_grad, axis=-1, keepdims=True))
+        ).astype(jnp.bfloat16)
+        row_grad = (
+            jnp.einsum("thk,thd->tkd", cross_probs, summary_low, preferred_element_type=jnp.float32)
+            + jnp.einsum("thk,thd->tkd", score_low, folded, preferred_element_type=jnp.float32)
+        ).astype(jnp.bfloat16)
+        folded_low = jnp.einsum(
+            "thk,tkd->thd", score_low, fetched_back, preferred_element_type=jnp.float32
+        ).astype(jnp.bfloat16)
     grad_key_heads = (
         jnp.einsum("thd,the->dhe", folded_low, cross_query, preferred_element_type=jnp.float32)
         * score_scale
@@ -670,8 +755,11 @@
     if dense:
         query_low, other_grad = lax.optimization_barrier((query_low, other_grad))
         send_a, send_b, keep = add_store(plan, own_grad, other_grad, rows_here)
-        query_low, send_a, send_b, keep = lax.optimization_barrier(
-            (query_low, send_a, send_b, keep)
+        query_low, mixed_heads, send_a, send_b, keep = lax.optimization_barrier(
+            (query_low, mixed_heads, send_a, send_b, keep)
+        )
+        grad_value_heads = jnp.einsum(
+            "thd,the->dhe", summary, mixed_heads, preferred_element_type=jnp.float32
         )
         came_a, came_b = swap_store(send_a, send_b)
     bias_three = column_sum(query_low)
@@ -738,6 +826,7 @@
                 grad_self_proj[:, 2],
                 grad_cross_query,
                 grad_key_heads.reshape(D, D),
+                grad_value_heads.reshape(D, D),
                 grad_self_out,
             ),
             (bias_zero, bias_one, bias_two, bias_three, bias_four, bias_five)
@@ -750,17 +839,18 @@
         keep, came_a, came_b, share_early = lax.optimization_barrier(
             (keep, came_a, came_b, share_early)
         )
-        grad_store = reduce_rows(keep, came_a, came_b).astype(jnp.float32)
         wide = grad_inner_bias.shape[0] // D
-        total_early, total_late = all_copies(share_early, share_late)
-        inner_total, outer_total, early = unpack_early(total_early, wide)
-        late, table, bias_inner = unpack_late(total_late, 6, 13, wide)
+        inner_total, outer_total, early = unpack_early(all_copies(share_early), wide)
+        grad_store = reduce_rows(keep, came_a, came_b)
+        grad_store, share_late = lax.optimization_barrier((grad_store, share_late))
+        grad_store = grad_store.astype(jnp.float32)
+        late, table, bias_inner = unpack_late(all_copies(share_late), 7, 13, wide)
         return (
             output,
             grad_tokens,
             grad_store,
-            jnp.stack([late[0], late[1], late[2], late[3], late[4], early[0]], axis=1),
-            jnp.stack([late[5], early[1]], axis=1),
+            jnp.stack([late[0], late[1], late[2], late[3], late[4], late[5]], axis=1),
+            jnp.stack([late[6], early[0]], axis=1),
             jnp.transpose(table[0:6]),
             jnp.transpose(table[6:9]),
             jnp.transpose(table[9:12]),

time: 1160 us -> 1060 us (0.914)
  matrix products: 251 us -> 141 us
  Pallas kernels: 239 us -> 296 us
  other arithmetic: 72.4 us -> 33.6 us
    dot_general x6 -> x0, matrix products: 92.7 us -> none  [the longest x1 20.7 us: body(): jnp.einsum('thk,thd->tkd', score_low, folded, preferred_element_type=jnp....]
    pallas_call x0 -> x2, Pallas kernels: none -> 59.8 us  [the longest x1 34.5 us: cross_backward(): pl.pallas_call(cross_backward_kernel, out_shape=[jax.ShapeDtypeStruct((to...]
    select_n x2 -> x1, other arithmetic: 14.4 us -> 0.26 us  [fetch_dense(): found.append(table[local])]
    reduce_sum x2 -> x1, other arithmetic: 16.7 us -> 2.57 us  [log_total(): jnp.sum(jnp.exp(scores - highest), axis=-1, keepdims=True)]
    unnamed x196 -> x208, local copies, waits for them, and re-layouts: 45.4 us -> 43.1 us
  transfers between devices with their start and end apart: 9 -> 10, of which waited for: 5 -> 6; matrix products, arithmetic and copies ran while one was open for 20% -> 21% of each run, Pallas kernels for 21% -> 22%
where the time goes in v5:
time: 1060 us; the launch traced here: 1050 us
  waiting for transfers between devices  369 us (35%)
  Pallas kernels  296 us (28%)
  local copies, waits for them, and re-layouts  194 us (18%)
  matrix products  141 us (13%)
  other arithmetic  33.6 us (3%)
  between operations  18 us (2%)
    all_gather x2, waiting for transfers between devices, fetch_dense(): table = lax.all_gather(mine, ('store', 'dp'), axis=0, tiled=True)  204 us
    pallas_call x1, Pallas kernels, reduce_rows(): pl.pallas_call(functools.partial(reduce_kernel, chunks), out_shape=jax.Sh...  162 us
    ppermute x1, waiting for transfers between devices, swap_store(): came_a = lax.ppermute(send_a, 'store', [(i, i ^ 1) for i in range(owners)])  158 us
    gather x2, local copies, waits for them, and re-layouts, fetch_dense(): found.append(table[local])  96.9 us
    pallas_call x1, Pallas kernels, scatter_rows(): pl.pallas_call(functools.partial(scatter_kernel, steps, block, out_rows),...  73.9 us
    unnamed x208, local copies, waits for them, and re-layouts  43.1 us
    pallas_call x1, Pallas kernels, cross_backward(): pl.pallas_call(cross_backward_kernel, out_shape=[jax.ShapeDtypeStruct((to...  34.5 us
    dot_general x6, matrix products, product_back(): jnp.einsum('tf,df->td', matrix, weight, preferred_element_type=jnp.float32)  31.2 us
  transfers between devices with their start and end apart: 10, of which 6 were waited for; matrix products, arithmetic and copies ran while one was open for 21% of the time, Pallas kernels for 22%

profile of v5, /device:TPU:0, one launch (start us, length us, event | category | flops | bytes accessed | tf_op | source)
XLA Modules:
  0.0 1054.6 jit_solution(13216346116114186652)
XLA Ops:
  12.7 2.6 constant_dynamic-slice_fusion
  18.6 2.5 copy-done.3
  21.2 1.6 fusion.121
  22.7 2.5 copy.58
  25.2 2.4 copy.63
  27.6 3.8 copy.81
  31.4 4.3 fusion.16
  37.7 2.1 fusion
  39.8 2.6 exponential_reduce_fusion
  42.4 1.8 copy-done
  44.3 3.4 convolution_convert_fusion.10
  47.7 4.8 fusion.124
  54.3 2.5 add_convert_fusion.2
  57.5 6.3 multiply_convert_fusion.folded_ref
  72.3 3.1 copy.62.which_ref
  75.4 97.4 %all-gather.7.cloned.1.call-done = bf16[16384,768]{1,0:T(8,128)(2,1)} async-done(((bf16[512,768]{1,0:T(8,128)(2,1)}), bf16[16384,768]{1,0:T(8,128)(2,1)}) %all-gather.7.cloned.1.call-update) | async-done | bytes 25165840 | tf_op jit(solution)/shard_map/all_gather | solution.py:129
  172.9 48.5 %gather_fusion.1 = bf16[8192,768]{1,0:T(8,128)(2,1)} fusion(bf16[16384,768]{1,0:T(8,128)(2,1)} %all-gather.7.cloned.1.call-done, s32[8192]{0:T(1024)S(1)} %broadcast_clamp_fusion), kind=kCustom, calls=%fused_computation.1 | custom fusion | bytes 25198592 | tf_op jit(solution)/shard_map/gather | solution.py:133
  221.4 106.7 %all-gather.5.cloned.1.call-done = bf16[16384,768]{1,0:T(8,128)(2,1)} async-done(((bf16[512,768]{1,0:T(8,128)(2,1)}), bf16[16384,768]{1,0:T(8,128)(2,1)}) %all-gather.5.cloned.1.call-update) | async-done | bytes 25165840 | tf_op jit(solution)/shard_map/all_gather | solution.py:129
  328.1 48.4 %gather_fusion = bf16[8192,768]{1,0:T(8,128)(2,1)} fusion(bf16[16384,768]{1,0:T(8,128)(2,1)} %all-gather.5.cloned.1.call-done, s32[8192]{0:T(1024)S(1)} %broadcast_clamp_fusion), kind=kCustom, calls=%fused_computation | custom fusion | bytes 25198592 | tf_op jit(solution)/shard_map/gather | solution.py:133
  376.5 25.3 %cross_forward.1 = (bf16[8192,768]{1,0:T(8,128)(2,1)}, bf16[12,512,768]{2,1,0:T(8,128)(2,1)}) custom-call(bf16[12,512,768]{2,1,0:T(8,128)(2,1)} %multiply_convert_fusion.folded_ref, bf16[8192,768]{1,0:T(8,128)(2,1)} %gather_fusion, bf16[8192,768]{1,0:T(8,128)(2,1)} %gather_fusion.1, s32[8192,1]{1,0:T(8,128)} %copy.62.which_ref), custom_call_target="tpu_custom_call" | custom-call | bytes 65000000 | tf_op jit(solution)/shard_map/cross_forward/pallas_call | solution.py:561
  401.9 6.8 fusion.18
  410.3 19.5 %multiply_convert_fusion.2 = (bf16[512,3072]{1,0:T(8,128)(2,1)S(1)}, f32[512,3072]{1,0:T(8,128)}, f32[512,3072]{1,0:T(8,128)}) fusion(f32[3072]{0:T(1024)S(1)} %copy-done.85, bf16[768,3072]{1,0:T(8,128)(2,1)} %param.23, f32[512,768]{1,0:T(8,128)S(1)} %get-tuple-element.162, f32[768]{0:T(1024)S(1)} %copy-done.78, f32[768]{0:T(1024)S(1)} %copy-done.55, ...), kind=kOutput, calls=%fused_computation.22 | convolution fusion | flops 2521694208 | bytes 22042624 | tf_op jit(solution)/shard_map/dot_general | solution.py:21
  429.8 2.8 fusion.129
  433.0 1.7 multiply_reduce_fusion.1
  435.3 4.7 convolution_convert_fusion.2
  440.0 8.7 fusion.131
  448.8 6.5 multiply_reduce_fusion.2
  455.3 3.4 convolution_convert_fusion.3
  459.4 1.7 fusion.130
  461.1 1.9 fusion.122
  463.0 1.8 convolution_convert_fusion.6
  466.3 2.8 constant_dynamic-update-slice_fusion.5
  472.4 4.8 constant_dynamic-update-slice_fusion.1
  478.4 5.2 convolution_convert_fusion.grad_ref
  483.6 34.5 %cross_backward.1 = (bf16[8192,768]{1,0:T(8,128)(2,1)}, bf16[12,512,768]{2,1,0:T(8,128)(2,1)}) custom-call(bf16[12,512,768]{2,1,0:T(8,128)(2,1)} %multiply_convert_fusion.folded_ref, bf16[12,512,768]{2,1,0:T(8,128)(2,1)} %convolution_convert_fusion.grad_ref, bf16[8192,768]{1,0:T(8,128)(2,1)} %get-tuple-element.48.rows_ref), custom_call_target="tpu_custom_call" | custom-call | bytes 100000000 | tf_op jit(solution)/shard_map/cross_backward/pallas_call | solution.py:578
  523.7 5.9 fusion.29
  529.6 1.7 convert_element_type.278
  531.3 1.8 copy.73
  533.1 8.0 multiply_convert_fusion.6
  541.7 73.9 %scatter_rows.1 = (bf16[4096,768]{1,0:T(8,128)(2,1)}, bf16[4096,768]{1,0:T(8,128)(2,1)}, bf16[8192,768]{1,0:T(8,128)(2,1)}) custom-call(s32[16384]{0:T(1024)} %bitcast.240, s32[16384]{0:T(1024)} %bitcast.241, s32[2048]{0:T(1024)} %or_or_fusion.twice_ref, s32[16]{0:T(128)} %and_select_fusion.2.groups_ref, bf16[8192,768]{1,0:T(8,128)(2,1)} %get-tuple-element.50.own_ref, ...), custom_call_target="tpu_custom_call" | custom-call | bytes 220000000 | tf_op jit(solution)/shard_map/scatter_rows/pallas_call | solution.py:250
  617.0 5.5 multiply_reduce_fusion.3
  623.2 1.9 convert_reduce_fusion.2
  625.9 2.6 convolution_convert_fusion.7
  630.3 5.6 fusion.32
  635.9 2.6 convert_element_type.281
  638.5 2.9 copy.74
  641.5 7.7 bitcast_reduce_fusion
  649.3 7.0 multiply_reduce_fusion
  656.3 7.1 multiply_convert_fusion.1
  663.5 2.6 bitcast_reduce_fusion.1
  666.7 4.9 multiply_convert_fusion.4
  671.7 2.0 convolution_convert_fusion.1
  673.7 1.6 fusion.123
  675.3 2.4 copy.86
  677.7 2.4 copy.85
  681.6 2.5 constant_dynamic-update-slice_fusion.12
  694.2 1.7 collective-permute-start.2
  696.0 158.4 %collective-permute-done.2 = bf16[4096,768]{1,0:T(8,128)(2,1)} collective-permute-done((bf16[4096,768]{1,0:T(8,128)(2,1)}, bf16[4096,768]{1,0:T(8,128)(2,1)}, u32[]{:S(2)}, u32[]{:S(2)}) %collective-permute-start.2) | collective-permute-done | bytes 6291488 | tf_op jit(solution)/shard_map/ppermute | solution.py:440
  854.4 4.9 collective-permute-done.3
  859.4 162.2 %reduce_rows.1 = bf16[2,2,2,8,64,768]{5,4,3,2,1,0:T(8,128)(2,1)} custom-call(bf16[2,4,2,8,64,768]{5,4,3,2,1,0:T(8,128)(2,1)} %bitcast.196, bf16[4,2,8,64,768]{4,3,2,1,0:T(8,128)(2,1)} %bitcast.38.came_a, bf16[4,2,8,64,768]{4,3,2,1,0:T(8,128)(2,1)} %bitcast.39.came_b), custom_call_target="tpu_custom_call" | custom-call | bytes 450000000 | tf_op jit(solution)/shard_map/reduce_rows/pallas_call | solution.py:384
  1021.6 6.1 add_convert_fusion.1
  1027.7 2.5 fusion.126
  1031.6 1.9 copy-done.2
  1033.5 5.8 convert_element_type.295
  (319 shorter events, 61.0 us)
Async XLA Ops:
  8.0 56.4 %sort.17.cloned.1.call-start = ((), (), s32[]{:S(2)}) async-start(), calls=%async_computation.8 | async-start | bytes 393248 | tf_op jit(solution)/shard_map/sort | solution.py:227
  9.1 6.3 copy-start.43
  9.1 1.4 collective-permute-start
  12.6 4.8 copy-start.57
  12.6 160.3 %all-gather.7.cloned.1.call-start = ((), (), s32[]{:S(2)}) async-start(), calls=%async_computation.3 | async-start | bytes 25952256 | tf_op jit(solution)/shard_map/all_gather | solution.py:129
  15.3 312.8 %all-gather.5.cloned.1.call-start = ((), (), s32[]{:S(2)}) async-start(), calls=%async_computation.2 | async-start | bytes 25952256 | tf_op jit(solution)/shard_map/all_gather | solution.py:129
  15.9 680.0 %reduce-scatter.3.cloned.1.call-start = ((), (), s32[]{:S(2)}) async-start(), calls=%async_computation.4 | async-start | bytes 10948608 | tf_op jit(solution)/shard_map/reduce_scatter | solution.py:451
  18.1 3.1 copy-start.3
  22.7 4.9 slice-start
  36.1 3.6 copy-start.4
  36.4 3.3 copy-start.13
  36.7 5.7 copy-start.30
  37.5 371.2 %copy-start.53 = (f32[768]{0:T(1024)}, f32[768]{0:T(1024)S(1)}, u32[]{:S(2)}) copy-start(f32[768]{0:T(1024)S(1)} %get-tuple-element.179) | copy-start | bytes 9220
  37.7 4.7 copy-start.15
  39.8 4.5 copy-start
  44.3 3.4 copy-start.12
  47.7 4.8 copy-start.37
  47.7 4.8 copy-start.81
  47.7 4.8 copy-start.83
  53.9 354.8 %copy-start.19 = (f32[512,768]{1,0:T(8,128)}, f32[512,768]{1,0:T(8,128)S(1)}, u32[]{:S(2)}) copy-start(f32[512,768]{1,0:T(8,128)S(1)} %get-tuple-element.158) | copy-start | bytes 4718596
  54.0 354.8 %copy-start.51 = (f32[512]{0:T(512)}, f32[512]{0:T(512)S(1)}, u32[]{:S(2)}) copy-start(f32[512]{0:T(512)S(1)} %broadcast_multiply_fusion.8) | copy-start | bytes 6148
  57.1 6.7 copy-start.8
  57.5 6.4 copy-start.82
  376.5 25.3 %copy-start.6 = (bf16[768,1,768]{0,2,1:T(8,128)(2,1)S(1)}, bf16[768,1,768]{0,2,1:T(8,128)(2,1)}, u32[]{:S(2)}) copy-start(bf16[768,1,768]{0,2,1:T(8,128)(2,1)} %copy.63) | copy-start | bytes 3538948
  401.9 6.8 copy-start.36
  401.9 6.8 copy-start.59
  401.9 6.8 copy-start.76
  401.9 6.8 copy-start.79
  408.8 21.0 %slice-start.1 = ((s8[4718592]{0:T(1024)(128)(4,1)}), s8[4194304]{0:T(1024)(128)(4,1)S(1)}, s32[]{:S(2)}) async-start(s8[4718592]{0:T(1024)(128)(4,1)} %bitcast.244), calls=%async_computation.11 | async-start | bytes 8388608
  410.2 19.5 %slice-start.2 = ((s8[4718592]{0:T(1024)(128)(4,1)}), s8[524288]{0:T(1024)(128)(4,1)S(1)}, s32[]{:S(2)}) async-start(s8[4718592]{0:T(1024)(128)(4,1)} %bitcast.244), calls=%async_computation.12 | async-start | bytes 1048576
  410.3 19.5 %copy-start.86 = (f32[768]{0:T(1024)S(1)}, f32[768]{0:T(1024)}, u32[]{:S(2)}) copy-start(f32[768]{0:T(1024)} %param.26) | copy-start | bytes 9220
  429.8 3.2 copy-start.33
  429.8 3.2 copy-start.47
  429.8 3.2 copy-start.56
  429.8 3.2 copy-start.74
  448.8 6.5 copy-start.88
  455.3 3.4 copy-start.49
  459.4 3.6 copy-start.18
  466.3 12.1 %copy-start.10 = (bf16[512,768]{0,1:T(8,128)(2,1)}, bf16[512,768]{0,1:T(8,128)(2,1)S(1)}, u32[]{:S(2)}) copy-start(bf16[512,768]{0,1:T(8,128)(2,1)S(1)} %copy.65) | copy-start | bytes 2359300
  466.3 3.9 copy-start.22
  472.4 4.8 copy-start.24
  518.1 23.6 %collective-permute-start.1 = (bf16[8192,768]{1,0:T(8,128)(2,1)}, bf16[8192,768]{1,0:T(8,128)(2,1)}, u32[]{:S(2)}, u32[]{:S(2)}) collective-permute-start(bf16[8192,768]{1,0:T(8,128)(2,1)} %get-tuple-element.50.own_ref), channel_id=1, source_target_pairs={{0,8},{8,0},{16,24},{24,16},{1,9},{9,1},{17,25},{25,17},{2,10},{10... | collective-permute-start | bytes 37748744 | tf_op jit(solution)/shard_map/ppermute | solution.py:726
  518.4 5.3 copy-start.9
  518.4 503.2 %reduce-scatter.5.cloned.1.call-start = ((), (), s32[]{:S(2)}) async-start(), calls=%async_computation.5 | async-start | bytes 9326592 | tf_op jit(solution)/shard_map/reduce_scatter | solution.py:451
  617.0 6.2 copy-start.20
  617.0 6.2 copy-start.52
  617.0 6.2 copy-start.54
  617.0 6.2 copy-start.60
  625.1 66.1 %copy-start.17 = (f32[512,768]{1,0:T(8,128)}, f32[512,768]{1,0:T(8,128)S(1)}, u32[]{:S(2)}) copy-start(f32[512,768]{1,0:T(8,128)S(1)} %get-tuple-element.125) | copy-start | bytes 4718596
  625.9 4.4 copy-start.11
  635.9 5.6 copy-start.16
  641.5 7.8 copy-start.31
  656.3 7.1 copy-start.5
  663.5 3.1 copy-start.14
  666.7 5.0 copy-start.34
  666.7 5.0 copy-start.84
  666.7 5.0 copy-start.87
  681.5 3.6 copy-start.25
  694.2 333.5 %all-gather.11.cloned.1.call-start = ((), (), s32[]{:S(2)}) async-start(), calls=%async_computation.7 | async-start | bytes 1658880 | tf_op jit(solution)/shard_map/all_gather | solution.py:457
  694.2 160.1 %collective-permute-start.2 = (bf16[4096,768]{1,0:T(8,128)(2,1)}, bf16[4096,768]{1,0:T(8,128)(2,1)}, u32[]{:S(2)}, u32[]{:S(2)}) collective-permute-start(bf16[4096,768]{1,0:T(8,128)(2,1)} %get-tuple-element.62), channel_id=1, source_target_pairs={{0,1},{1,0},{2,3},{3,2},{4,5},{5,4},{6,7},{7,6},{8,9},{9,8},{10,11... | collective-permute-start | bytes 18874376 | tf_op jit(solution)/shard_map/ppermute | solution.py:440
  696.0 163.3 %collective-permute-start.3 = (bf16[4096,768]{1,0:T(8,128)(2,1)}, bf16[4096,768]{1,0:T(8,128)(2,1)}, u32[]{:S(2)}, u32[]{:S(2)}) collective-permute-start(bf16[4096,768]{1,0:T(8,128)(2,1)} %get-tuple-element.63), channel_id=1, source_target_pairs={{0,16},{8,24},{16,0},{24,8},{1,17},{9,25},{17,1},{25,9},{2,18},{10... | collective-permute-start | bytes 18874376 | tf_op jit(solution)/shard_map/ppermute | solution.py:441
  859.3 180.0 %all-gather.9.cloned.1.call-start = ((), (), s32[]{:S(2)}) async-start(), calls=%async_computation.6 | async-start | bytes 1413120 | tf_op jit(solution)/shard_map/all_gather | solution.py:457
  1027.7 3.7 copy-start.7
  1030.3 3.2 copy-start.2
  (39 other events, 90.3 us)
Sparse Core Ops, SparseCore 0:
  12.8 5.5 sort.19.cloned.1.call-done
  859.4 23.3 all-gather.10
  1021.7 16.0 all-gather.8
  (1 shorter events, 0.0 us)
Sparse Core Ops, SparseCore 1:
  16.6 156.2 all-gather.6
  176.2 151.8 all-gather.4
  518.5 140.5 reduce-scatter.2
  694.3 154.7 reduce-scatter.4

commit v6 on v5

--- a/solution.py
+++ b/solution.py
@@ -273,135 +273,269 @@
     )(*plan, own, other)
 
 
-def reduce_kernel(chunks, keep_ref, came_a, came_b, out_ref, keep_a, keep_b, one_a, one_b, two_a, two_b, layer, along, done,
-                  keep_sem, two_send, two_recv, z_send, z_recv,
-                  own_sem, y_send, y_recv, core_send, core_recv, pass_send, pass_recv):
+SIGNALS = 26
+
+
+def plus(first, second):
+    return (first.astype(jnp.float32) + second.astype(jnp.float32)).astype(jnp.bfloat16)
+
+
+class Unit:
+    def __init__(self, place, signals, spare, out):
+        self.x, self.y, self.z, self.core, self.inner, self.peers = place
+        self.signals = signals
+        self.keep_a, self.keep_b, self.one_a, self.one_b, self.two_a, self.two_b = spare[:6]
+        self.layer, self.three, self.merged, self.near, self.far, self.done = spare[6:]
+        self.out = out
+
+    def remote(self, src, dst, send, recv, peer):
+        return pltpu.make_async_remote_copy(
+            src_ref=src, dst_ref=dst, send_sem=self.signals(send), recv_sem=self.signals(recv),
+            device_id=peer, device_id_type=MESH_ID,
+        )
+
+    def loads(self, sources):
+        places = (self.keep_a, self.keep_b, self.one_a, self.one_b)
+        return [
+            pltpu.make_async_copy(source, place, self.signals(index))
+            for index, (source, place) in enumerate(zip(sources, places))
+        ]
+
+    def firsts(self, send_a, send_b):
+        return [
+            self.remote(send_a, self.one_a, 22, 24, self.peers["x"]),
+            self.remote(send_b, self.one_b, 23, 25, self.peers["y"]),
+        ]
+
+    def seconds(self):
+        return [
+            self.remote(self.keep_a.at[:, 1 - self.y], self.two_a, 4, 6, self.peers["y"]),
+            self.remote(self.keep_b.at[:, 1 - self.x], self.two_b, 5, 7, self.peers["x"]),
+        ]
+
+    def merge_first(self):
+        def body(i, carry):
+            for half in range(2):
+                self.keep_a[i, half] = plus(self.keep_a[i, half], self.one_a[i, half])
+                self.keep_b[i, half] = plus(self.keep_b[i, half], self.one_b[i, half])
+            return carry
+
+        lax.fori_loop(0, 4, body, 0)
+        for copy in self.seconds():
+            copy.start()
+
+    def from_end(self):
+        first = 1 - lax.div(self.z, 3)
+        return self.remote(self.layer.at[pl.ds(first, 3)], self.three, 8, 9, self.peers["beside"])
+
+    def to_end(self):
+        return self.remote(self.layer.at[self.peers["end_z"]], self.near, 10, 11, self.peers["beside"])
+
+    def across_inner(self):
+        return self.remote(self.merged.at[0], self.far, 12, 14, self.peers["other_inner"])
+
+    def across_end(self):
+        return self.remote(self.merged.at[1], self.far, 13, 14, self.peers["far_end"])
+
+    def merge_second(self):
+        for copy in self.seconds():
+            copy.wait_recv()
+
+        def body(i, carry):
+            self.layer[i, 0] = plus(self.keep_a[i, self.y], self.two_a[i])
+            self.layer[i, 1] = plus(self.keep_b[i, self.x], self.two_b[i])
+            return carry
+
+        lax.fori_loop(0, 4, body, 0)
+
+        @pl.when(self.inner)
+        def _():
+            self.to_end().start()
+
+        @pl.when(jnp.logical_not(self.inner))
+        def _():
+            self.from_end().start()
+
+    def merge_third(self):
+        @pl.when(self.inner)
+        def _():
+            self.from_end().wait_recv()
+
+            def body(i, carry):
+                self.merged[0, i] = plus(self.layer[3 - self.z, i], self.three[1, i])
+                self.merged[1, i] = plus(self.layer[6 - 3 * self.z, i], self.three[4 - 2 * self.z, i])
+                return carry
+
+            lax.fori_loop(0, 2, body, 0)
+            self.across_inner().start()
+            self.across_end().start()
+
+    def own(self):
+        return pltpu.make_async_copy(self.done, self.out(self.core, self.y), self.signals(15))
+
+    def to_y(self):
+        return self.remote(self.done, self.out(self.core, self.y), 16, 17, self.peers["y"])
+
+    def to_core(self):
+        return self.remote(self.done, self.out(self.core, self.y), 18, 19, self.peers["core"])
+
+    def passed(self):
+        place = self.out(self.core, 1 - self.y)
+        return self.remote(place, place, 20, 21, self.peers["core"])
+
+    def finish(self):
+        self.across_inner().wait_recv()
+
+        @pl.when(self.inner)
+        def _():
+            def body(i, carry):
+                total = self.layer[self.z, i].astype(jnp.float32) + self.far[i].astype(jnp.float32)
+                total = total + self.three[2 * self.z - 2, i].astype(jnp.float32)
+                self.done[i] = total.astype(jnp.bfloat16)
+                return carry
+
+            lax.fori_loop(0, 2, body, 0)
+
+        @pl.when(jnp.logical_not(self.inner))
+        def _():
+            self.to_end().wait_recv()
+
+            def body(i, carry):
+                total = self.layer[self.z, i].astype(jnp.float32) + self.far[i].astype(jnp.float32)
+                total = total + self.near[i].astype(jnp.float32)
+                self.done[i] = total.astype(jnp.bfloat16)
+                return carry
+
+            lax.fori_loop(0, 2, body, 0)
+
+        self.own().start()
+        self.to_y().start()
+        self.to_core().start()
+
+    def hand_on(self):
+        self.to_y().wait_recv()
+        self.passed().start()
+
+    def drain(self):
+        for copy in self.seconds():
+            copy.wait_send()
+
+        @pl.when(self.inner)
+        def _():
+            self.to_end().wait_send()
+            self.across_inner().wait_send()
+            self.across_end().wait_send()
+
+        @pl.when(jnp.logical_not(self.inner))
+        def _():
+            self.from_end().wait_send()
+
+        self.own().wait()
+        self.to_y().wait_send()
+        self.to_core().wait()
+        self.passed().wait()
+
+
+def reduce_kernel(chunks, keep_ref, came_a, came_b, weight_ref, out_ref, weight_out, *scratch):
+    rows, weights, signals = scratch[:12], scratch[12:24], scratch[24]
     dp = lax.axis_index("dp")
     store = lax.axis_index("store")
     y, core = lax.div(dp, 2), lax.rem(dp, 2)
     z, x = lax.div(store, 2), lax.rem(store, 2)
-    x_peer = (dp, z * 2 + (1 - x))
-    y_peer = ((1 - y) * 2 + core, store)
-    core_peer = (y * 2 + (1 - core), store)
-    z_of = [lax.rem(z + hop, 4) for hop in range(4)]
-    z_peer = [(dp, z_of[hop] * 2 + x) for hop in range(4)]
+    inner = (z == 1) | (z == 2)
+    beside = z + 1 - 2 * lax.rem(z, 2)
+    along = lambda to: (dp, to * 2 + x)
+    peers = {
+        "x": (dp, z * 2 + (1 - x)),
+        "y": ((1 - y) * 2 + core, store),
+        "core": (y * 2 + (1 - core), store),
+        "beside": along(beside),
+        "end_z": 3 * lax.div(z, 2),
+        "other_inner": along(3 - z),
+        "far_end": along(3 - 3 * lax.div(z, 2)),
+    }
+    place = (x, y, z, core, inner, peers)
 
     barrier = pltpu.get_barrier_semaphore()
-    for peer in (x_peer, y_peer, core_peer, z_peer[1], z_peer[2], z_peer[3]):
+    for peer in (peers["x"], peers["y"], peers["core"]) + tuple(along(lax.rem(z + hop, 4)) for hop in (1, 2, 3)):
         pl.semaphore_signal(barrier, inc=1, device_id=peer, device_id_type=MESH_ID)
     pl.semaphore_wait(barrier, 6)
 
-    def remote(src, dst, send, recv, peer):
-        return pltpu.make_async_remote_copy(src_ref=src, dst_ref=dst, send_sem=send, recv_sem=recv,
-                                            device_id=peer, device_id_type=MESH_ID)
-
-    keeps = [(
-        pltpu.make_async_copy(keep_ref.at[0, :, :, q], keep_a.at[q], keep_sem.at[0, q]),
-        pltpu.make_async_copy(keep_ref.at[1, :, :, q], keep_b.at[q], keep_sem.at[1, q]),
-        pltpu.make_async_copy(came_a.at[:, :, q], one_a.at[q], keep_sem.at[2, q]),
-        pltpu.make_async_copy(came_b.at[:, :, q], one_b.at[q], keep_sem.at[3, q]),
-    ) for q in range(chunks)]
-    twos = [(
-        remote(keep_a.at[q, :, 1 - y], two_a.at[q], two_send.at[0, q], two_recv.at[0, q], y_peer),
-        remote(keep_b.at[q, :, 1 - x], two_b.at[q], two_send.at[1, q], two_recv.at[1, q], x_peer),
-    ) for q in range(chunks)]
-    zs = [[
-        remote(layer.at[q, z_of[hop]], along.at[q, hop - 1], z_send.at[hop - 1, q], z_recv.at[hop - 1, q], z_peer[hop])
-        for hop in (1, 2, 3)] for q in range(chunks)]
-    own = [pltpu.make_async_copy(done.at[q], out_ref.at[core, y, :, q], own_sem.at[q]) for q in range(chunks)]
-    to_y = [remote(done.at[q], out_ref.at[core, y, :, q], y_send.at[q], y_recv.at[q], y_peer) for q in range(chunks)]
-    to_core = [remote(done.at[q], out_ref.at[core, y, :, q], core_send.at[q], core_recv.at[q], core_peer) for q in range(chunks)]
-    passed = [remote(out_ref.at[core, 1 - y, :, q], out_ref.at[core, 1 - y, :, q], pass_send.at[q], pass_recv.at[q], core_peer)
-              for q in range(chunks)]
-
-    def plus(first, second):
-        return (first.astype(jnp.float32) + second.astype(jnp.float32)).astype(jnp.bfloat16)
-
-    for q in range(chunks):
-        for copy in keeps[q]:
+    units = [
+        Unit(
+            place, lambda kind, q=q: signals.at[kind, q], [ref.at[q] for ref in rows],
+            lambda c, h, q=q: out_ref.at[c, h, :, q],
+        )
+        for q in range(chunks)
+    ]
+    extra = Unit(
+        place, lambda kind: signals.at[kind, chunks], weights, lambda c, h: weight_out.at[c, h]
+    )
+    extra_first = extra.firsts(weight_ref.at[:, 1 - x, :, 0], weight_ref.at[:, :, 1 - y, 1])
+    extra_loads = extra.loads((weight_ref.at[:, x, :, 0], weight_ref.at[:, :, y, 1]))
+    loads = [
+        unit.loads((keep_ref.at[0, :, :, q], keep_ref.at[1, :, :, q], came_a.at[:, :, q], came_b.at[:, :, q]))
+        for q, unit in enumerate(units)
+    ]
+    for copy in loads[0] + extra_first + extra_loads:
+        copy.start()
+    for some in loads[1:]:
+        for copy in some:
             copy.start()
-    for step in range(chunks + 3):
-        q = step
-        if q < chunks:
-            for copy in keeps[q]:
+    for step in range(chunks + 4):
+        if step < chunks:
+            for copy in loads[step]:
                 copy.wait()
-
-            def merge(i, carry, q=q):
-                for half in range(2):
-                    keep_a[q, i, half] = plus(keep_a[q, i, half], one_a[q, i, half])
-                    keep_b[q, i, half] = plus(keep_b[q, i, half], one_b[q, i, half])
-                return carry
-
-            lax.fori_loop(0, 4, merge, 0)
-            for copy in twos[q]:
-                copy.start()
-        q = step - 1
-        if 0 <= q < chunks:
-            for copy in twos[q]:
+            units[step].merge_first()
+        if step == 2:
+            for copy in extra_loads:
+                copy.wait()
+            for copy in extra_first:
                 copy.wait_recv()
-
-            def merge_two(i, carry, q=q):
-                layer[q, i, 0] = plus(keep_a[q, i, y], two_a[q, i])
-                layer[q, i, 1] = plus(keep_b[q, i, x], two_b[q, i])
-                return carry
-
-            lax.fori_loop(0, 4, merge_two, 0)
-            for copy in zs[q]:
-                copy.start()
-        q = step - 2
-        if 0 <= q < chunks:
-            for copy in zs[q]:
-                copy.wait_recv()
-
-            def finish(i, carry, q=q):
-                value = layer[q, z, i].astype(jnp.float32)
-                for hop in range(3):
-                    value = value + along[q, hop, i].astype(jnp.float32)
-                done[q, i] = value.astype(jnp.bfloat16)
-                return carry
-
-            lax.fori_loop(0, 2, finish, 0)
-            for copy in (own[q], to_y[q], to_core[q]):
-                copy.start()
-        q = step - 3
-        if 0 <= q < chunks:
-            to_y[q].wait_recv()
-            passed[q].start()
-    for q in range(chunks):
-        for copy in twos[q] + tuple(zs[q]):
-            copy.wait_send()
-        own[q].wait()
-        to_y[q].wait_send()
-        to_core[q].wait()
-        passed[q].wait()
-
-
-def reduce_rows(keep, came_a, came_b, collective_id=0):
+            extra.merge_first()
+        for stage, name in enumerate(("merge_second", "merge_third", "finish", "hand_on")):
+            if 0 <= step - 1 - stage < chunks:
+                getattr(units[step - 1 - stage], name)()
+            if step == 4 + stage:
+                getattr(extra, name)()
+    for copy in extra_first:
+        copy.wait_send()
+    for unit in units + [extra]:
+        unit.drain()
+
+
+def reduce_rows(keep, came_a, came_b, weights, collective_id=0):
     rows = keep.shape[0] // 4
     chunks = rows // (4 * CHUNK)
-    dma = pltpu.SemaphoreType.DMA
-    vm = lambda *lead: pltpu.VMEM(lead + (CHUNK, D), jnp.bfloat16)
-    out = pl.pallas_call(
+    high = weights.shape[0] // 32
+
+    def spare(high, *lead):
+        return [
+            pltpu.VMEM(lead + part + (high, D), jnp.bfloat16)
+            for part in ((4, 2),) * 4 + ((4,), (4,), (4, 2), (3, 2), (2, 2), (2,), (2,), (2,))
+        ]
+
+    out, weights = pl.pallas_call(
         functools.partial(reduce_kernel, chunks),
-        out_shape=jax.ShapeDtypeStruct((2, 2, 2, chunks, CHUNK, D), jnp.bfloat16),
-        in_specs=[pl.BlockSpec(memory_space=pl.ANY)] * 3,
-        out_specs=pl.BlockSpec(memory_space=pl.ANY),
-        scratch_shapes=[
-            vm(chunks, 4, 2), vm(chunks, 4, 2), vm(chunks, 4, 2), vm(chunks, 4, 2),
-            vm(chunks, 4), vm(chunks, 4), vm(chunks, 4, 2), vm(chunks, 3, 2), vm(chunks, 2),
-            dma((4, chunks)), dma((2, chunks)), dma((2, chunks)),
-            dma((3, chunks)), dma((3, chunks)),
-            dma((chunks,)), dma((chunks,)), dma((chunks,)), dma((chunks,)), dma((chunks,)), dma((chunks,)), dma((chunks,)),
+        out_shape=[
+            jax.ShapeDtypeStruct((2, 2, 2, chunks, CHUNK, D), jnp.bfloat16),
+            jax.ShapeDtypeStruct((2, 2, 2, high, D), jnp.bfloat16),
         ],
-        compiler_params=pltpu.CompilerParams(collective_id=collective_id, has_side_effects=True, vmem_limit_bytes=VMEM_LIMIT),
+        in_specs=[pl.BlockSpec(memory_space=pl.ANY)] * 4,
+        out_specs=[pl.BlockSpec(memory_space=pl.ANY)] * 2,
+        scratch_shapes=spare(CHUNK, chunks) + spare(high) + [pltpu.SemaphoreType.DMA((SIGNALS, chunks + 1))],
+        compiler_params=pltpu.CompilerParams(
+            collective_id=collective_id, has_side_effects=True, vmem_limit_bytes=VMEM_LIMIT
+        ),
         cost_estimate=pl.CostEstimate(flops=0, transcendentals=0, bytes_accessed=450_000_000),
         name="reduce_rows",
     )(
         keep.reshape(2, 4, 2, chunks, CHUNK, D),
         came_a.reshape(4, 2, chunks, CHUNK, D),
         came_b.reshape(4, 2, chunks, CHUNK, D),
-    )
-    return out.reshape(2 * rows, D)
+        weights.reshape(4, 2, 2, 2, high, D),
+    )
+    return out.reshape(2 * rows, D), weights.reshape(8 * high, D)
 
 
 PAIRS = ((0, 1), (1, 0), (2, 3), (3, 2))
@@ -448,9 +582,7 @@
 
 
 def reduce_packed(packed):
-    return lax.psum_scatter(
-        packed.reshape(-1, D), ("store", "dp"), scatter_dimension=0, tiled=True
-    )
+    return lax.psum_scatter(packed.reshape(-1, D), ("store", "dp"), scatter_dimension=0, tiled=True)
 
 
 def all_copies(share):
@@ -482,8 +614,17 @@
         + [inner_bias.astype(jnp.bfloat16).reshape(owners, wide * part)],
         axis=1,
     )
-    small = jnp.pad(small, ((0, 0), (0, 64 * D - small.shape[1]))).reshape(owners, 64, D)
+    small = jnp.pad(small, ((0, 0), (0, part * D - small.shape[1]))).reshape(owners, part, D)
     return jnp.concatenate([by_owner(square) for square in squares] + [small], axis=1)
+
+
+def add_cores(packed):
+    core = lax.axis_index("dp") % 2
+    halves = packed.reshape(packed.shape[0], 2, -1, D)
+    mine = lax.dynamic_index_in_dim(halves, core, axis=1, keepdims=False)
+    other = lax.dynamic_index_in_dim(halves, 1 - core, axis=1, keepdims=False)
+    other = lax.ppermute(other, "dp", PAIRS)
+    return plus(mine, other).reshape(-1, D)
 
 
 def unpack_late(total, count, features, wide):
@@ -835,16 +976,15 @@
             + (grad_outer_bias,),
             grad_inner_bias,
         )
-        share_late = reduce_packed(packed_late)
-        keep, came_a, came_b, share_early = lax.optimization_barrier(
-            (keep, came_a, came_b, share_early)
-        )
         wide = grad_inner_bias.shape[0] // D
-        inner_total, outer_total, early = unpack_early(all_copies(share_early), wide)
-        grad_store = reduce_rows(keep, came_a, came_b)
-        grad_store, share_late = lax.optimization_barrier((grad_store, share_late))
+        early_totals = unpack_early(all_copies(share_early), wide)
+        keep, came_a, came_b, output, grad_tokens, early_totals = lax.optimization_barrier(
+            (keep, came_a, came_b, output, grad_tokens, early_totals)
+        )
+        inner_total, outer_total, early = early_totals
+        grad_store, total_late = reduce_rows(keep, came_a, came_b, add_cores(packed_late))
         grad_store = grad_store.astype(jnp.float32)
-        late, table, bias_inner = unpack_late(all_copies(share_late), 7, 13, wide)
+        late, table, bias_inner = unpack_late(total_late.astype(jnp.float32), 7, 13, wide)
         return (
             output,
             grad_tokens,

time: 1060 us -> 1000 us (0.943)
  waiting for transfers between devices: 369 us -> 287 us
  Pallas kernels: 296 us -> 307 us
    ppermute x1, waiting for transfers between devices: 158 us -> 54 us  [swap_store(): came_a = lax.ppermute(send_a, 'store', [(i, i ^ 1) for i in range(owners)])]
    all_gather x2 -> x1, waiting for transfers between devices: 0.01 us -> 18.9 us  [all_copies(): return lax.all_gather(share, 'dp', axis=0, tiled=True).astype(jnp.float32)]
    pallas_call x1, Pallas kernels: 162 us -> 174 us  [reduce_rows(): pl.pallas_call(functools.partial(reduce_kernel, chunks), out_shape=[jax.S...]
    unnamed x208 -> x212, local copies, waits for them, and re-layouts: 43.1 us -> 39.7 us
  transfers between devices with their start and end apart: 10 -> 9, of which waited for: 6 -> 7; matrix products, arithmetic and copies ran while one was open for 21% -> 21% of each run, Pallas kernels for 22% -> 7%
where the time goes in v6:
time: 1000 us; the launch traced here: 994 us
  Pallas kernels  307 us (31%)
  waiting for transfers between devices  287 us (29%)
  local copies, waits for them, and re-layouts  195 us (20%)
  matrix products  139 us (14%)
  other arithmetic  44.1 us (4%)
  between operations  18 us (2%)
    all_gather x2, waiting for transfers between devices, fetch_dense(): table = lax.all_gather(mine, ('store', 'dp'), axis=0, tiled=True)  204 us
    pallas_call x1, Pallas kernels, reduce_rows(): pl.pallas_call(functools.partial(reduce_kernel, chunks), out_shape=[jax.S...  174 us
    gather x2, local copies, waits for them, and re-layouts, fetch_dense(): found.append(table[local])  96.9 us
    pallas_call x1, Pallas kernels, scatter_rows(): pl.pallas_call(functools.partial(scatter_kernel, steps, block, out_rows),...  73.9 us
    ppermute x1, waiting for transfers between devices, swap_store(): came_a = lax.ppermute(send_a, 'store', [(i, i ^ 1) for i in range(owners)])  54 us
    unnamed x212, local copies, waits for them, and re-layouts  39.7 us
    pallas_call x1, Pallas kernels, cross_backward(): pl.pallas_call(cross_backward_kernel, out_shape=[jax.ShapeDtypeStruct((to...  34.5 us
    dot_general x6, matrix products, product(): return jnp.dot(matrix, factor, preferred_element_type=jnp.float32)  31 us
  transfers between devices with their start and end apart: 9, of which 7 were waited for; matrix products, arithmetic and copies ran while one was open for 21% of the time, Pallas kernels for 7%

profile of v6, /device:TPU:0, one launch (start us, length us, event | category | flops | bytes accessed | tf_op | source)
XLA Modules:
  0.0 993.9 jit_solution(13629081415972228907)
XLA Ops:
  12.7 2.6 constant_dynamic-slice_fusion
  18.6 2.5 copy-done.2
  22.7 2.5 copy.63
  25.2 2.4 copy.58
  27.6 3.8 copy.81
  31.4 4.3 fusion.17
  37.7 2.1 fusion
  39.8 2.6 exponential_reduce_fusion
  42.4 1.8 copy-done
  44.3 3.7 convolution_convert_fusion.10
  48.0 4.8 fusion.126
  54.6 2.5 add_convert_fusion.2
  57.7 6.3 multiply_convert_fusion.folded_ref
  72.5 2.9 copy.62.which_ref
  75.4 97.5 %all-gather.6.cloned.1.call-done = bf16[16384,768]{1,0:T(8,128)(2,1)} async-done(((bf16[512,768]{1,0:T(8,128)(2,1)}), bf16[16384,768]{1,0:T(8,128)(2,1)}) %all-gather.6.cloned.1.call-update) | async-done | bytes 25165840 | tf_op jit(solution)/shard_map/all_gather | solution.py:129
  172.9 48.5 %gather_fusion.1 = bf16[8192,768]{1,0:T(8,128)(2,1)} fusion(bf16[16384,768]{1,0:T(8,128)(2,1)} %all-gather.6.cloned.1.call-done, s32[8192]{0:T(1024)S(1)} %broadcast_clamp_fusion), kind=kCustom, calls=%fused_computation.1 | custom fusion | bytes 25198592 | tf_op jit(solution)/shard_map/gather | solution.py:133
  221.4 106.7 %all-gather.4.cloned.1.call-done = bf16[16384,768]{1,0:T(8,128)(2,1)} async-done(((bf16[512,768]{1,0:T(8,128)(2,1)}), bf16[16384,768]{1,0:T(8,128)(2,1)}) %all-gather.4.cloned.1.call-update) | async-done | bytes 25165840 | tf_op jit(solution)/shard_map/all_gather | solution.py:129
  328.1 48.4 %gather_fusion = bf16[8192,768]{1,0:T(8,128)(2,1)} fusion(bf16[16384,768]{1,0:T(8,128)(2,1)} %all-gather.4.cloned.1.call-done, s32[8192]{0:T(1024)S(1)} %broadcast_clamp_fusion), kind=kCustom, calls=%fused_computation | custom fusion | bytes 25198592 | tf_op jit(solution)/shard_map/gather | solution.py:133
  376.5 25.4 %cross_forward.1 = (bf16[8192,768]{1,0:T(8,128)(2,1)}, bf16[12,512,768]{2,1,0:T(8,128)(2,1)}) custom-call(bf16[12,512,768]{2,1,0:T(8,128)(2,1)} %multiply_convert_fusion.folded_ref, bf16[8192,768]{1,0:T(8,128)(2,1)} %gather_fusion, bf16[8192,768]{1,0:T(8,128)(2,1)} %gather_fusion.1, s32[8192,1]{1,0:T(8,128)} %copy.62.which_ref), custom_call_target="tpu_custom_call" | custom-call | bytes 65000000 | tf_op jit(solution)/shard_map/cross_forward/pallas_call | solution.py:702
  402.0 6.8 fusion.19
  410.3 19.5 %multiply_convert_fusion.2 = (bf16[512,3072]{1,0:T(8,128)(2,1)S(1)}, f32[512,3072]{1,0:T(8,128)}, f32[512,3072]{1,0:T(8,128)}) fusion(f32[3072]{0:T(1024)S(1)} %copy-done.87, bf16[768,3072]{1,0:T(8,128)(2,1)} %param.23, f32[512,768]{1,0:T(8,128)S(1)} %get-tuple-element.172, f32[768]{0:T(1024)S(1)} %copy-done.80, f32[768]{0:T(1024)S(1)} %copy-done.56, ...), kind=kOutput, calls=%fused_computation.25 | convolution fusion | flops 2521694208 | bytes 22042624 | tf_op jit(solution)/shard_map/dot_general | solution.py:21
  429.9 2.8 fusion.131
  433.0 1.7 multiply_reduce_fusion.1
  435.3 4.8 convolution_convert_fusion.2
  440.1 8.7 fusion.133
  448.9 6.5 multiply_reduce_fusion.2
  455.4 3.4 convolution_convert_fusion.3
  459.5 1.7 fusion.132
  461.2 1.9 fusion.123
  463.1 1.8 convolution_convert_fusion.6
  466.4 2.8 constant_dynamic-update-slice_fusion.5
  472.5 4.8 constant_dynamic-update-slice_fusion.1
  478.5 5.2 convolution_convert_fusion.grad_ref
  483.7 34.5 %cross_backward.1 = (bf16[8192,768]{1,0:T(8,128)(2,1)}, bf16[12,512,768]{2,1,0:T(8,128)(2,1)}) custom-call(bf16[12,512,768]{2,1,0:T(8,128)(2,1)} %multiply_convert_fusion.folded_ref, bf16[12,512,768]{2,1,0:T(8,128)(2,1)} %convolution_convert_fusion.grad_ref, bf16[8192,768]{1,0:T(8,128)(2,1)} %get-tuple-element.52.rows_ref), custom_call_target="tpu_custom_call" | custom-call | bytes 100000000 | tf_op jit(solution)/shard_map/cross_backward/pallas_call | solution.py:719
  523.8 5.9 fusion.30
  529.6 1.7 convert_element_type.297
  531.4 1.8 copy.74
  533.2 8.0 multiply_convert_fusion.6
  541.7 73.9 %scatter_rows.1 = (bf16[4096,768]{1,0:T(8,128)(2,1)}, bf16[4096,768]{1,0:T(8,128)(2,1)}, bf16[8192,768]{1,0:T(8,128)(2,1)}) custom-call(s32[16384]{0:T(1024)} %bitcast.255, s32[16384]{0:T(1024)} %bitcast.256, s32[2048]{0:T(1024)} %or_or_fusion.twice_ref, s32[16]{0:T(128)} %and_select_fusion.2.groups_ref, bf16[8192,768]{1,0:T(8,128)(2,1)} %get-tuple-element.54.own_ref, ...), custom_call_target="tpu_custom_call" | custom-call | bytes 220000000 | tf_op jit(solution)/shard_map/scatter_rows/pallas_call | solution.py:250
  617.6 5.1 multiply_reduce_fusion.3
  623.4 1.9 convert_reduce_fusion.2
  626.0 2.5 convolution_convert_fusion.7
  630.4 5.6 fusion.33
  636.0 2.6 convert_element_type.300
  638.6 3.0 copy.75
  641.6 7.6 bitcast_reduce_fusion
  649.3 1.8 collective-permute-start.2
  651.2 7.0 multiply_reduce_fusion
  658.2 7.1 multiply_convert_fusion.1
  669.5 4.9 multiply_convert_fusion.4
  674.4 2.0 convolution_convert_fusion.1
  678.0 2.4 copy.86
  680.4 2.4 copy.85
  682.8 1.8 copy.84
  692.0 2.5 dynamic-slice_bitcast_fusion
  694.5 2.7 copy-done.3
  697.6 5.2 add_convert_fusion.1
  702.8 18.9 %all-gather.8.cloned.1.call-done = bf16[864,768]{1,0:T(8,128)(2,1)} async-done(((bf16[216,768]{1,0:T(8,128)(2,1)}), bf16[864,768]{1,0:T(8,128)(2,1)}) %all-gather.8.cloned.1.call-update) | async-done | bytes 1327120 | tf_op jit(solution)/shard_map/all_gather | solution.py:589
  721.7 2.5 fusion.128
  726.3 7.0 fusion.1
  733.3 54.0 %collective-permute-done.2 = bf16[4096,768]{1,0:T(8,128)(2,1)} collective-permute-done((bf16[4096,768]{1,0:T(8,128)(2,1)}, bf16[4096,768]{1,0:T(8,128)(2,1)}, u32[]{:S(2)}, u32[]{:S(2)}) %collective-permute-start.2) | collective-permute-done | bytes 6291488 | tf_op jit(solution)/shard_map/ppermute | solution.py:574
  787.3 8.2 collective-permute-done.3
  795.5 173.6 %reduce_rows.1 = (bf16[2,2,2,8,64,768]{5,4,3,2,1,0:T(8,128)(2,1)}, bf16[2,2,2,96,768]{4,3,2,1,0:T(8,128)(2,1)}) custom-call(bf16[2,4,2,8,64,768]{5,4,3,2,1,0:T(8,128)(2,1)} %bitcast.208, bf16[4,2,8,64,768]{4,3,2,1,0:T(8,128)(2,1)} %bitcast.41.came_a, bf16[4,2,8,64,768]{4,3,2,1,0:T(8,128)(2,1)} %bitcast.42.came_b, bf16[4,2,2,2,96,768]{5,4,3,2,1,0:T(8,128)(2,1)} %bitcast.207), custom_call_target="tpu_custom_call" | custom-call | bytes 450000000 | tf_op jit(solution)/shard_map/reduce_rows/pallas_call | solution.py:518
  976.9 9.2 bitcast_convert_fusion
  (320 shorter events, 65.1 us)
Async XLA Ops:
  8.0 56.6 %sort.17.cloned.1.call-start = ((), (), s32[]{:S(2)}) async-start(), calls=%async_computation.5 | async-start | bytes 393248 | tf_op jit(solution)/shard_map/sort | solution.py:227
  9.1 6.8 copy-start.44
  9.1 1.4 collective-permute-start
  11.9 5.4 copy-start.58
  12.6 160.3 %all-gather.6.cloned.1.call-start = ((), (), s32[]{:S(2)}) async-start(), calls=%async_computation.2 | async-start | bytes 25952256 | tf_op jit(solution)/shard_map/all_gather | solution.py:129
  15.3 312.8 %all-gather.4.cloned.1.call-start = ((), (), s32[]{:S(2)}) async-start(), calls=%async_computation.1 | async-start | bytes 25952256 | tf_op jit(solution)/shard_map/all_gather | solution.py:129
  15.9 681.7 %reduce-scatter.2.cloned.1.call-start = ((), (), s32[]{:S(2)}) async-start(), calls=%async_computation.3 | async-start | bytes 10948608 | tf_op jit(solution)/shard_map/reduce_scatter | solution.py:585
  18.1 3.0 copy-start.2
  22.7 4.9 slice-start
  36.1 3.6 copy-start.4
  36.4 3.3 copy-start.13
  36.7 5.7 copy-start.30
  36.8 3.0 copy-start.75
  37.5 371.2 %copy-start.54 = (f32[768]{0:T(1024)}, f32[768]{0:T(1024)S(1)}, u32[]{:S(2)}) copy-start(f32[768]{0:T(1024)S(1)} %get-tuple-element.189) | copy-start | bytes 9220
  37.6 4.7 copy-start.15
  39.8 4.5 copy-start
  44.3 3.7 copy-start.12
  48.0 4.8 copy-start.37
  48.0 4.8 copy-start.83
  48.0 4.8 copy-start.85
  54.2 354.5 %copy-start.18 = (f32[512,768]{1,0:T(8,128)}, f32[512,768]{1,0:T(8,128)S(1)}, u32[]{:S(2)}) copy-start(f32[512,768]{1,0:T(8,128)S(1)} %get-tuple-element.168) | copy-start | bytes 4718596
  54.2 354.5 %copy-start.52 = (f32[512]{0:T(512)}, f32[512]{0:T(512)S(1)}, u32[]{:S(2)}) copy-start(f32[512]{0:T(512)S(1)} %broadcast_multiply_fusion.8) | copy-start | bytes 6148
  57.4 6.7 copy-start.8
  57.7 6.4 copy-start.84
  376.5 25.4 %copy-start.6 = (bf16[768,1,768]{0,2,1:T(8,128)(2,1)S(1)}, bf16[768,1,768]{0,2,1:T(8,128)(2,1)}, u32[]{:S(2)}) copy-start(bf16[768,1,768]{0,2,1:T(8,128)(2,1)} %copy.63) | copy-start | bytes 3538948
  401.9 6.8 copy-start.35
  401.9 6.8 copy-start.60
  401.9 6.8 copy-start.78
  402.0 6.8 copy-start.81
  408.8 21.0 %slice-start.1 = ((s8[4718592]{0:T(1024)(128)(4,1)}), s8[4194304]{0:T(1024)(128)(4,1)S(1)}, s32[]{:S(2)}) async-start(s8[4718592]{0:T(1024)(128)(4,1)} %bitcast.259), calls=%async_computation.8 | async-start | bytes 8388608
  410.3 19.5 %slice-start.2 = ((s8[4718592]{0:T(1024)(128)(4,1)}), s8[524288]{0:T(1024)(128)(4,1)S(1)}, s32[]{:S(2)}) async-start(s8[4718592]{0:T(1024)(128)(4,1)} %bitcast.259), calls=%async_computation.9 | async-start | bytes 1048576
  410.3 19.5 %copy-start.88 = (f32[768]{0:T(1024)S(1)}, f32[768]{0:T(1024)}, u32[]{:S(2)}) copy-start(f32[768]{0:T(1024)} %param.26) | copy-start | bytes 9220
  429.8 3.2 copy-start.33
  429.8 3.2 copy-start.48
  429.8 3.2 copy-start.57
  429.8 3.2 copy-start.76
  448.9 6.5 copy-start.90
  455.4 3.4 copy-start.50
  459.5 3.6 copy-start.17
  466.4 12.1 %copy-start.10 = (bf16[512,768]{0,1:T(8,128)(2,1)}, bf16[512,768]{0,1:T(8,128)(2,1)S(1)}, u32[]{:S(2)}) copy-start(bf16[512,768]{0,1:T(8,128)(2,1)S(1)} %copy.65) | copy-start | bytes 2359300
  466.4 3.9 copy-start.21
  472.5 4.8 copy-start.23
  518.2 23.6 %collective-permute-start.1 = (bf16[8192,768]{1,0:T(8,128)(2,1)}, bf16[8192,768]{1,0:T(8,128)(2,1)}, u32[]{:S(2)}, u32[]{:S(2)}) collective-permute-start(bf16[8192,768]{1,0:T(8,128)(2,1)} %get-tuple-element.54.own_ref), channel_id=1, source_target_pairs={{0,8},{8,0},{16,24},{24,16},{1,9},{9,1},{17,25},{25,17},{2,10},{10... | collective-permute-start | bytes 37748744 | tf_op jit(solution)/shard_map/ppermute | solution.py:867
  518.4 5.4 copy-start.9
  518.4 203.3 %all-gather.8.cloned.1.call-start = ((), (), s32[]{:S(2)}) async-start(), calls=%async_computation.4 | async-start | bytes 1658880 | tf_op jit(solution)/shard_map/all_gather | solution.py:589
  617.6 5.8 copy-start.19
  617.6 5.8 copy-start.53
  617.6 5.8 copy-start.55
  617.6 5.8 copy-start.61
  625.4 5.0 copy-start.11
  636.0 5.6 copy-start.16
  641.6 9.6 copy-start.31
  649.3 138.0 %collective-permute-start.2 = (bf16[4096,768]{1,0:T(8,128)(2,1)}, bf16[4096,768]{1,0:T(8,128)(2,1)}, u32[]{:S(2)}, u32[]{:S(2)}) collective-permute-start(bf16[4096,768]{1,0:T(8,128)(2,1)} %get-tuple-element.65), channel_id=1, source_target_pairs={{0,1},{1,0},{2,3},{3,2},{4,5},{5,4},{6,7},{7,6},{8,9},{9,8},{10,11... | collective-permute-start | bytes 18874376 | tf_op jit(solution)/shard_map/ppermute | solution.py:574
  651.1 144.3 %collective-permute-start.3 = (bf16[4096,768]{1,0:T(8,128)(2,1)}, bf16[4096,768]{1,0:T(8,128)(2,1)}, u32[]{:S(2)}, u32[]{:S(2)}) collective-permute-start(bf16[4096,768]{1,0:T(8,128)(2,1)} %get-tuple-element.66), channel_id=1, source_target_pairs={{0,16},{8,24},{16,0},{24,8},{1,17},{9,25},{17,1},{25,9},{2,18},{10... | collective-permute-start | bytes 18874376 | tf_op jit(solution)/shard_map/ppermute | solution.py:575
  658.2 7.1 copy-start.5
  665.4 4.0 copy-start.14
  669.5 4.9 copy-start.86
  669.5 4.9 copy-start.89
  692.0 5.2 copy-start.3
  692.0 5.7 copy-start.41
  697.1 29.2 %collective-permute-start.4 = (bf16[8,384,768]{2,1,0:T(8,128)(2,1)}, bf16[8,384,768]{2,1,0:T(8,128)(2,1)}, u32[]{:S(2)}, u32[]{:S(2)}) collective-permute-start(bf16[8,384,768]{2,1,0:T(8,128)(2,1)} %dynamic-slice_bitcast_fusion), channel_id=1, source_target_pairs={{0,8},{8,0},{16,24},{24,16},{1,9},{9,1},{17,25},{25,17},{2,10},{10... | collective-permute-start | bytes 14155784 | tf_op jit(solution)/shard_map/ppermute | solution.py:626
  721.7 3.6 copy-start.7
  969.1 6.3 copy-start.36
  976.9 9.2 copy-start.47
  (40 other events, 83.9 us)
Sparse Core Ops, SparseCore 0:
  12.8 5.5 sort.19.cloned.1.call-done
  697.8 23.9 all-gather.7
  (1 shorter events, 0.0 us)
Sparse Core Ops, SparseCore 1:
  16.6 156.3 all-gather.5
  176.2 151.8 all-gather.3
  518.5 140.4 reduce-scatter.1

commit v7 on v6

--- a/solution.py
+++ b/solution.py
@@ -136,10 +136,10 @@
 
 MESH_ID = pl.DeviceIdType.MESH
 VMEM_LIMIT = 67043328
-CHUNK = 64
-
-
-GROUP = 8
+CHUNK = 32
+
+
+GROUP = 16
 
 
 SPLIT = D // 128
@@ -155,7 +155,7 @@
             total[pl.ds(i * 192, 192), :] = jnp.zeros((192, 128), jnp.float32)
             return carry
 
-        lax.fori_loop(0, total.shape[0] // 192, clear, 0)
+        lax.fori_loop(0, total.shape[0] // 192, clear, 0, unroll=4)
 
     def widen(ref):
         def strip(i, carry):
@@ -165,7 +165,7 @@
                 wide[pl.ds(first * SPLIT + part, 32, stride=SPLIT), :] = value[:, part * 128 : (part + 1) * 128]
             return carry
 
-        lax.fori_loop(0, block // 32, strip, 0)
+        lax.fori_loop(0, block // 32, strip, 0, unroll=4)
 
     @pl.when(step < steps // 2)
     def _():
@@ -206,7 +206,7 @@
                 out_ref[pl.ds(pl.multiple_of(i * 32, 32), 32), part * 128 : (part + 1) * 128] = value.astype(jnp.bfloat16)
             return carry
 
-        lax.fori_loop(0, out_rows // 32, strip, 0)
+        lax.fori_loop(0, out_rows // 32, strip, 0, unroll=4)
 
     quarter = (total.shape[0] // SPLIT // 4) // out_rows
     for index, out_ref in enumerate(outs):
@@ -487,7 +487,7 @@
             for copy in loads[step]:
                 copy.wait()
             units[step].merge_first()
-        if step == 2:
+        if step == 4:
             for copy in extra_loads:
                 copy.wait()
             for copy in extra_first:
@@ -496,7 +496,7 @@
         for stage, name in enumerate(("merge_second", "merge_third", "finish", "hand_on")):
             if 0 <= step - 1 - stage < chunks:
                 getattr(units[step - 1 - stage], name)()
-            if step == 4 + stage:
+            if step == 6 + 2 * stage:
                 getattr(extra, name)()
     for copy in extra_first:
         copy.wait_send()

time: 1000 us -> 1010 us (1.010)
  no operation moved by 1% of the time
where the time goes in v7:
time: 1010 us; the launch traced here: 998 us
  Pallas kernels  311 us (31%)
  waiting for transfers between devices  286 us (28%)
  local copies, waits for them, and re-layouts  195 us (19%)
  matrix products  139 us (14%)
  other arithmetic  45.2 us (4%)
  between operations  18.4 us (2%)
    all_gather x2, waiting for transfers between devices, fetch_dense(): table = lax.all_gather(mine, ('store', 'dp'), axis=0, tiled=True)  203 us
    pallas_call x1, Pallas kernels, reduce_rows(): pl.pallas_call(functools.partial(reduce_kernel, chunks), out_shape=[jax.S...  178 us
    gather x2, local copies, waits for them, and re-layouts, fetch_dense(): found.append(table[local])  97.1 us
    pallas_call x1, Pallas kernels, scatter_rows(): pl.pallas_call(functools.partial(scatter_kernel, steps, block, out_rows),...  73.2 us
    ppermute x1, waiting for transfers between devices, swap_store(): came_a = lax.ppermute(send_a, 'store', [(i, i ^ 1) for i in range(owners)])  55.4 us
    unnamed x212, local copies, waits for them, and re-layouts  39.5 us
    pallas_call x1, Pallas kernels, cross_backward(): pl.pallas_call(cross_backward_kernel, out_shape=[jax.ShapeDtypeStruct((to...  34.5 us
    dot_general x6, matrix products, product(): return jnp.dot(matrix, factor, preferred_element_type=jnp.float32)  31.2 us
  transfers between devices with their start and end apart: 9, of which 7 were waited for; matrix products, arithmetic and copies ran while one was open for 21% of the time, Pallas kernels for 7%

profile of v7, /device:TPU:0, one launch (start us, length us, event | category | flops | bytes accessed | tf_op | source)
XLA Modules:
  0.0 998.0 jit_solution(3382159638539347927)
XLA Ops:
  12.7 2.6 constant_dynamic-slice_fusion
  18.6 2.5 copy-done.2
  22.7 2.5 copy.63
  25.2 2.4 copy.58
  27.6 3.8 copy.81
  31.4 4.3 fusion.17
  37.7 2.1 fusion
  39.8 2.6 exponential_reduce_fusion
  42.4 1.8 copy-done
  44.3 3.4 convolution_convert_fusion.10
  47.7 4.8 fusion.134
  54.3 2.5 add_convert_fusion.2
  57.5 6.7 multiply_convert_fusion.folded_ref
  73.4 2.7 copy.62.which_ref
  76.1 96.8 %all-gather.6.cloned.1.call-done = bf16[16384,768]{1,0:T(8,128)(2,1)} async-done(((bf16[512,768]{1,0:T(8,128)(2,1)}), bf16[16384,768]{1,0:T(8,128)(2,1)}) %all-gather.6.cloned.1.call-update) | async-done | bytes 25165840 | tf_op jit(solution)/shard_map/all_gather | solution.py:129
  172.9 48.7 %gather_fusion.1 = bf16[8192,768]{1,0:T(8,128)(2,1)} fusion(bf16[16384,768]{1,0:T(8,128)(2,1)} %all-gather.6.cloned.1.call-done, s32[8192]{0:T(1024)S(1)} %broadcast_clamp_fusion), kind=kCustom, calls=%fused_computation.1 | custom fusion | bytes 25198592 | tf_op jit(solution)/shard_map/gather | solution.py:133
  221.6 106.5 %all-gather.4.cloned.1.call-done = bf16[16384,768]{1,0:T(8,128)(2,1)} async-done(((bf16[512,768]{1,0:T(8,128)(2,1)}), bf16[16384,768]{1,0:T(8,128)(2,1)}) %all-gather.4.cloned.1.call-update) | async-done | bytes 25165840 | tf_op jit(solution)/shard_map/all_gather | solution.py:129
  328.1 48.4 %gather_fusion = bf16[8192,768]{1,0:T(8,128)(2,1)} fusion(bf16[16384,768]{1,0:T(8,128)(2,1)} %all-gather.4.cloned.1.call-done, s32[8192]{0:T(1024)S(1)} %broadcast_clamp_fusion), kind=kCustom, calls=%fused_computation | custom fusion | bytes 25198592 | tf_op jit(solution)/shard_map/gather | solution.py:133
  376.5 25.2 %cross_forward.1 = (bf16[8192,768]{1,0:T(8,128)(2,1)}, bf16[12,512,768]{2,1,0:T(8,128)(2,1)}) custom-call(bf16[12,512,768]{2,1,0:T(8,128)(2,1)} %multiply_convert_fusion.folded_ref, bf16[8192,768]{1,0:T(8,128)(2,1)} %gather_fusion, bf16[8192,768]{1,0:T(8,128)(2,1)} %gather_fusion.1, s32[8192,1]{1,0:T(8,128)} %copy.62.which_ref), custom_call_target="tpu_custom_call" | custom-call | bytes 65000000 | tf_op jit(solution)/shard_map/cross_forward/pallas_call | solution.py:702
  401.7 6.8 fusion.19
  410.1 19.6 %multiply_convert_fusion.2 = (bf16[512,3072]{1,0:T(8,128)(2,1)S(1)}, f32[512,3072]{1,0:T(8,128)}, f32[512,3072]{1,0:T(8,128)}) fusion(f32[3072]{0:T(1024)S(1)} %copy-done.87, bf16[768,3072]{1,0:T(8,128)(2,1)} %param.23, f32[512,768]{1,0:T(8,128)S(1)} %get-tuple-element.172, f32[768]{0:T(1024)S(1)} %copy-done.80, f32[768]{0:T(1024)S(1)} %copy-done.56, ...), kind=kOutput, calls=%fused_computation.25 | convolution fusion | flops 2521694208 | bytes 22042624 | tf_op jit(solution)/shard_map/dot_general | solution.py:21
  429.8 2.8 fusion.139
  433.0 1.7 multiply_reduce_fusion.1
  435.3 4.3 convolution_convert_fusion.2
  439.6 9.1 fusion.141
  448.7 6.5 multiply_reduce_fusion.2
  455.3 3.4 convolution_convert_fusion.3
  459.4 1.7 fusion.140
  461.1 1.9 fusion.131
  463.0 1.8 convolution_convert_fusion.6
  466.3 2.8 constant_dynamic-update-slice_fusion.5
  472.3 4.8 constant_dynamic-update-slice_fusion.1
  478.4 5.0 convolution_convert_fusion.grad_ref
  483.4 34.5 %cross_backward.1 = (bf16[8192,768]{1,0:T(8,128)(2,1)}, bf16[12,512,768]{2,1,0:T(8,128)(2,1)}) custom-call(bf16[12,512,768]{2,1,0:T(8,128)(2,1)} %multiply_convert_fusion.folded_ref, bf16[12,512,768]{2,1,0:T(8,128)(2,1)} %convolution_convert_fusion.grad_ref, bf16[8192,768]{1,0:T(8,128)(2,1)} %get-tuple-element.52.rows_ref), custom_call_target="tpu_custom_call" | custom-call | bytes 100000000 | tf_op jit(solution)/shard_map/cross_backward/pallas_call | solution.py:719
  523.6 5.9 fusion.30
  529.5 1.7 convert_element_type.329
  531.3 1.8 copy.74
  533.1 8.0 multiply_convert_fusion.6
  541.4 73.2 %scatter_rows.1 = (bf16[4096,768]{1,0:T(8,128)(2,1)}, bf16[4096,768]{1,0:T(8,128)(2,1)}, bf16[8192,768]{1,0:T(8,128)(2,1)}) custom-call(s32[16384]{0:T(1024)} %bitcast.255, s32[16384]{0:T(1024)} %bitcast.256, s32[1024]{0:T(1024)} %or_or_fusion.twice_ref, s32[16]{0:T(128)} %and_select_fusion.2.groups_ref, bf16[8192,768]{1,0:T(8,128)(2,1)} %get-tuple-element.54.own_ref, ...), custom_call_target="tpu_custom_call" | custom-call | bytes 220000000 | tf_op jit(solution)/shard_map/scatter_rows/pallas_call | solution.py:250
  616.6 5.5 multiply_reduce_fusion.3
  622.8 1.9 convert_reduce_fusion.2
  625.4 2.5 convolution_convert_fusion.7
  629.7 5.6 fusion.33
  635.3 2.6 convert_element_type.332
  637.9 3.0 copy.75
  640.9 7.6 bitcast_reduce_fusion
  648.6 1.8 collective-permute-start.2
  650.4 7.0 multiply_reduce_fusion
  657.4 7.1 multiply_convert_fusion.1
  668.7 4.9 multiply_convert_fusion.4
  673.6 2.0 convolution_convert_fusion.1
  677.3 2.4 copy.86
  679.6 2.4 copy.85
  682.0 1.7 copy.84
  691.1 2.5 dynamic-slice_bitcast_fusion
  693.5 2.7 copy-done.3
  696.7 5.2 add_convert_fusion.1
  701.8 17.9 %all-gather.8.cloned.1.call-done = bf16[864,768]{1,0:T(8,128)(2,1)} async-done(((bf16[216,768]{1,0:T(8,128)(2,1)}), bf16[864,768]{1,0:T(8,128)(2,1)}) %all-gather.8.cloned.1.call-update) | async-done | bytes 1327120 | tf_op jit(solution)/shard_map/all_gather | solution.py:589
  719.8 2.5 fusion.136
  724.3 7.0 fusion.1
  731.4 55.4 %collective-permute-done.2 = bf16[4096,768]{1,0:T(8,128)(2,1)} collective-permute-done((bf16[4096,768]{1,0:T(8,128)(2,1)}, bf16[4096,768]{1,0:T(8,128)(2,1)}, u32[]{:S(2)}, u32[]{:S(2)}) %collective-permute-start.2) | collective-permute-done | bytes 6291488 | tf_op jit(solution)/shard_map/ppermute | solution.py:574
  786.8 8.0 collective-permute-done.3
  794.8 178.1 %reduce_rows.1 = (bf16[2,2,2,16,32,768]{5,4,3,2,1,0:T(8,128)(2,1)}, bf16[2,2,2,96,768]{4,3,2,1,0:T(8,128)(2,1)}) custom-call(bf16[2,4,2,16,32,768]{5,4,3,2,1,0:T(8,128)(2,1)} %bitcast.208, bf16[4,2,16,32,768]{4,3,2,1,0:T(8,128)(2,1)} %bitcast.41.came_a, bf16[4,2,16,32,768]{4,3,2,1,0:T(8,128)(2,1)} %bitcast.42.came_b, bf16[4,2,2,2,96,768]{5,4,3,2,1,0:T(8,128)(2,1)} %bitcast.207), custom_call_target="tpu_custom_call" | custom-call | bytes 450000000 | tf_op jit(solution)/shard_map/reduce_rows/pallas_call | solution.py:518
  980.7 9.2 bitcast_convert_fusion
  (328 shorter events, 65.7 us)
Async XLA Ops:
  8.0 56.8 %sort.17.cloned.1.call-start = ((), (), s32[]{:S(2)}) async-start(), calls=%async_computation.5 | async-start | bytes 393248 | tf_op jit(solution)/shard_map/sort | solution.py:227
  9.1 6.8 copy-start.44
  9.1 1.4 collective-permute-start
  11.9 5.4 copy-start.58
  12.6 160.3 %all-gather.6.cloned.1.call-start = ((), (), s32[]{:S(2)}) async-start(), calls=%async_computation.2 | async-start | bytes 25952256 | tf_op jit(solution)/shard_map/all_gather | solution.py:129
  15.3 312.8 %all-gather.4.cloned.1.call-start = ((), (), s32[]{:S(2)}) async-start(), calls=%async_computation.1 | async-start | bytes 25952256 | tf_op jit(solution)/shard_map/all_gather | solution.py:129
  15.9 680.7 %reduce-scatter.2.cloned.1.call-start = ((), (), s32[]{:S(2)}) async-start(), calls=%async_computation.3 | async-start | bytes 10948608 | tf_op jit(solution)/shard_map/reduce_scatter | solution.py:585
  18.1 3.0 copy-start.2
  22.7 4.9 slice-start
  36.1 3.6 copy-start.4
  36.4 3.3 copy-start.13
  36.7 5.7 copy-start.30
  36.8 3.0 copy-start.75
  37.5 371.0 %copy-start.54 = (f32[768]{0:T(1024)}, f32[768]{0:T(1024)S(1)}, u32[]{:S(2)}) copy-start(f32[768]{0:T(1024)S(1)} %get-tuple-element.189) | copy-start | bytes 9220
  37.6 4.7 copy-start.15
  39.8 4.5 copy-start
  44.3 3.4 copy-start.12
  47.7 4.8 copy-start.37
  47.7 4.8 copy-start.83
  47.7 4.8 copy-start.85
  53.9 354.6 %copy-start.18 = (f32[512,768]{1,0:T(8,128)}, f32[512,768]{1,0:T(8,128)S(1)}, u32[]{:S(2)}) copy-start(f32[512,768]{1,0:T(8,128)S(1)} %get-tuple-element.168) | copy-start | bytes 4718596
  53.9 354.6 %copy-start.52 = (f32[512]{0:T(512)}, f32[512]{0:T(512)S(1)}, u32[]{:S(2)}) copy-start(f32[512]{0:T(512)S(1)} %broadcast_multiply_fusion.8) | copy-start | bytes 6148
  57.1 7.1 copy-start.8
  57.5 6.7 copy-start.84
  376.5 25.2 %copy-start.6 = (bf16[768,1,768]{0,2,1:T(8,128)(2,1)S(1)}, bf16[768,1,768]{0,2,1:T(8,128)(2,1)}, u32[]{:S(2)}) copy-start(bf16[768,1,768]{0,2,1:T(8,128)(2,1)} %copy.63) | copy-start | bytes 3538948
  401.7 6.8 copy-start.35
  401.7 6.8 copy-start.60
  401.7 6.8 copy-start.78
  401.7 6.8 copy-start.81
  408.6 21.1 %slice-start.1 = ((s8[4718592]{0:T(1024)(128)(4,1)}), s8[4194304]{0:T(1024)(128)(4,1)S(1)}, s32[]{:S(2)}) async-start(s8[4718592]{0:T(1024)(128)(4,1)} %bitcast.259), calls=%async_computation.8 | async-start | bytes 8388608
  410.1 19.7 %slice-start.2 = ((s8[4718592]{0:T(1024)(128)(4,1)}), s8[524288]{0:T(1024)(128)(4,1)S(1)}, s32[]{:S(2)}) async-start(s8[4718592]{0:T(1024)(128)(4,1)} %bitcast.259), calls=%async_computation.9 | async-start | bytes 1048576
  410.1 19.7 %copy-start.88 = (f32[768]{0:T(1024)S(1)}, f32[768]{0:T(1024)}, u32[]{:S(2)}) copy-start(f32[768]{0:T(1024)} %param.26) | copy-start | bytes 9220
  429.8 3.2 copy-start.33
  429.8 3.2 copy-start.48
  429.8 3.2 copy-start.57
  429.8 3.2 copy-start.76
  448.7 6.5 copy-start.90
  455.3 3.4 copy-start.50
  459.4 3.6 copy-start.17
  466.2 12.1 %copy-start.10 = (bf16[512,768]{0,1:T(8,128)(2,1)}, bf16[512,768]{0,1:T(8,128)(2,1)S(1)}, u32[]{:S(2)}) copy-start(bf16[512,768]{0,1:T(8,128)(2,1)S(1)} %copy.65) | copy-start | bytes 2359300
  466.2 3.9 copy-start.21
  472.3 4.8 copy-start.23
  517.9 23.5 %collective-permute-start.1 = (bf16[8192,768]{1,0:T(8,128)(2,1)}, bf16[8192,768]{1,0:T(8,128)(2,1)}, u32[]{:S(2)}, u32[]{:S(2)}) collective-permute-start(bf16[8192,768]{1,0:T(8,128)(2,1)} %get-tuple-element.54.own_ref), channel_id=1, source_target_pairs={{0,8},{8,0},{16,24},{24,16},{1,9},{9,1},{17,25},{25,17},{2,10},{10... | collective-permute-start | bytes 37748744 | tf_op jit(solution)/shard_map/ppermute | solution.py:867
  518.1 5.5 copy-start.9
  518.1 201.6 %all-gather.8.cloned.1.call-start = ((), (), s32[]{:S(2)}) async-start(), calls=%async_computation.4 | async-start | bytes 1658880 | tf_op jit(solution)/shard_map/all_gather | solution.py:589
  616.6 6.2 copy-start.19
  616.6 6.2 copy-start.53
  616.6 6.2 copy-start.55
  616.6 6.2 copy-start.61
  624.7 5.0 copy-start.11
  635.3 5.6 copy-start.16
  640.9 9.5 copy-start.31
  648.6 138.2 %collective-permute-start.2 = (bf16[4096,768]{1,0:T(8,128)(2,1)}, bf16[4096,768]{1,0:T(8,128)(2,1)}, u32[]{:S(2)}, u32[]{:S(2)}) collective-permute-start(bf16[4096,768]{1,0:T(8,128)(2,1)} %get-tuple-element.65), channel_id=1, source_target_pairs={{0,1},{1,0},{2,3},{3,2},{4,5},{5,4},{6,7},{7,6},{8,9},{9,8},{10,11... | collective-permute-start | bytes 18874376 | tf_op jit(solution)/shard_map/ppermute | solution.py:574
  650.4 144.4 %collective-permute-start.3 = (bf16[4096,768]{1,0:T(8,128)(2,1)}, bf16[4096,768]{1,0:T(8,128)(2,1)}, u32[]{:S(2)}, u32[]{:S(2)}) collective-permute-start(bf16[4096,768]{1,0:T(8,128)(2,1)} %get-tuple-element.66), channel_id=1, source_target_pairs={{0,16},{8,24},{16,0},{24,8},{1,17},{9,25},{17,1},{25,9},{2,18},{10... | collective-permute-start | bytes 18874376 | tf_op jit(solution)/shard_map/ppermute | solution.py:575
  657.4 7.1 copy-start.5
  664.7 4.0 copy-start.14
  668.7 4.9 copy-start.86
  668.7 4.9 copy-start.89
  691.0 5.2 copy-start.3
  691.0 5.6 copy-start.41
  696.2 28.1 %collective-permute-start.4 = (bf16[8,384,768]{2,1,0:T(8,128)(2,1)}, bf16[8,384,768]{2,1,0:T(8,128)(2,1)}, u32[]{:S(2)}, u32[]{:S(2)}) collective-permute-start(bf16[8,384,768]{2,1,0:T(8,128)(2,1)} %dynamic-slice_bitcast_fusion), channel_id=1, source_target_pairs={{0,8},{8,0},{16,24},{24,16},{1,9},{9,1},{17,25},{25,17},{2,10},{10... | collective-permute-start | bytes 14155784 | tf_op jit(solution)/shard_map/ppermute | solution.py:626
  719.8 3.6 copy-start.7
  972.9 6.3 copy-start.36
  980.7 9.2 copy-start.47
  (40 other events, 83.9 us)
Sparse Core Ops, SparseCore 0:
  12.8 5.5 sort.19.cloned.1.call-done
  696.8 22.9 all-gather.7
  (1 shorter events, 0.0 us)
Sparse Core Ops, SparseCore 1:
  16.6 156.3 all-gather.5
  176.2 151.8 all-gather.3
  518.2 140.4 reduce-scatter.1

commit v8 on v6

--- a/solution.py
+++ b/solution.py
@@ -104,34 +104,19 @@
 
 
 def is_dense(owners, rows_here):
-    fits = owners * rows_here <= DENSE_LIMIT and rows_here % (8 * CHUNK) == 0
+    fits = owners * rows_here <= DENSE_LIMIT and rows_here % (8 * CHUNK) == 0 and owners * rows_here % GATHER_BLOCK == 0
     return fits and owners == 8 and lax.axis_size("dp") == 4
-
-
-STORE_PARTS = 2
 
 
 def fetch_dense(datastore, indices, plan):
     copies = lax.axis_size("dp")
     rows_here = datastore.shape[0]
     share = rows_here // copies
-    part = share // STORE_PARTS
-    flat = indices.reshape(-1)
-    which = (flat % share) // part
-    local = (flat // share) * part + flat % part
-    start = lax.axis_index("dp") * share
-    found = []
-    earlier = None
-    for index in range(STORE_PARTS):
-        mine = lax.dynamic_slice_in_dim(datastore, start + index * part, part, axis=0)
-        if earlier is not None:
-            mine, earlier = lax.optimization_barrier((mine, earlier))
-        table = lax.all_gather(mine, ("store", "dp"), axis=0, tiled=True)
-        earlier = mine
-        if index == STORE_PARTS - 1:
-            which, plan = lax.optimization_barrier((which, plan))
-        found.append(table[local])
-    return found[0], found[1], which[:, None], plan
+    mine = lax.dynamic_slice_in_dim(datastore, lax.axis_index("dp") * share, share, axis=0)
+    table = lax.all_gather(mine, ("store", "dp"), axis=0, tiled=True)
+    picks = gather_plan(indices, table.shape[0])
+    picks, plan = lax.optimization_barrier((picks, plan))
+    return gather_rows(picks, table, indices.size), plan
 
 
 MESH_ID = pl.DeviceIdType.MESH
@@ -143,6 +128,90 @@
 
 
 SPLIT = D // 128
+
+
+def widen(ref, wide):
+    def strip(i, carry):
+        first = pl.multiple_of(i * 32, 32)
+        value = ref[pl.ds(first, 32), :].astype(jnp.float32)
+        for part in range(SPLIT):
+            wide[pl.ds(first * SPLIT + part, 32, stride=SPLIT), :] = value[:, part * 128 : (part + 1) * 128]
+        return carry
+
+    lax.fori_loop(0, ref.shape[0] // 32, strip, 0, unroll=4)
+
+
+def narrow(total, start, out_ref):
+    def strip(i, carry):
+        first = pl.multiple_of(start * SPLIT + i * (32 * SPLIT), 32 * SPLIT)
+        for part in range(SPLIT):
+            value = total[pl.ds(first + part, 32, stride=SPLIT), :]
+            out_ref[pl.ds(pl.multiple_of(i * 32, 32), 32), part * 128 : (part + 1) * 128] = value.astype(jnp.bfloat16)
+        return carry
+
+    lax.fori_loop(0, out_ref.shape[0] // 32, strip, 0, unroll=4)
+
+
+GATHER_BLOCK = 2048
+
+
+def gather_kernel(blocks, out_rows, row_ref, to_ref, start_ref, table_ref, out_ref, wide, found):
+    step = pl.program_id(0)
+
+    @pl.when(step < blocks)
+    def _():
+        widen(table_ref, wide)
+        base = step * (GATHER_BLOCK * SPLIT)
+        first = start_ref[step]
+
+        def group(i, carry):
+            at = first + i * GROUP
+            rows = [
+                jnp.minimum(row_ref[at + k] - base, (GATHER_BLOCK - 1) * SPLIT) for k in range(GROUP)
+            ]
+            places = [to_ref[at + k] for k in range(GROUP)]
+            values = [wide[pl.ds(row, SPLIT), :] for row in rows]
+            for place, value in zip(places, values):
+                found[pl.ds(place, SPLIT), :] = value
+            return carry
+
+        lax.fori_loop(0, lax.div(start_ref[step + 1] - first + GROUP - 1, GROUP), group, 0)
+
+    @pl.when(step >= blocks)
+    def _():
+        narrow(found, (step - blocks) * out_rows, out_ref)
+
+
+def gather_plan(indices, rows):
+    flat = indices.reshape(-1)
+    count = flat.shape[0]
+    row, place = lax.sort((flat, jnp.arange(count, dtype=jnp.int32)), dimension=0, num_keys=1)
+    bounds = jnp.arange(rows // GATHER_BLOCK + 1, dtype=jnp.int32) * GATHER_BLOCK
+    starts = jnp.sum((flat[:, None] < bounds[None, :]).astype(jnp.int32), axis=0)
+    row = jnp.concatenate([row, jnp.full((GROUP,), rows - 1, jnp.int32)])
+    place = jnp.concatenate([place, jnp.full((GROUP,), count, jnp.int32)])
+    return SPLIT * row, SPLIT * place, starts
+
+
+def gather_rows(plan, table, count, out_rows=1024):
+    blocks = table.shape[0] // GATHER_BLOCK
+    return pl.pallas_call(
+        functools.partial(gather_kernel, blocks, out_rows),
+        out_shape=jax.ShapeDtypeStruct((count, D), jnp.bfloat16),
+        grid_spec=pltpu.PrefetchScalarGridSpec(
+            num_scalar_prefetch=3,
+            grid=(blocks + count // out_rows,),
+            in_specs=[pl.BlockSpec((GATHER_BLOCK, D), lambda i, *_: (jnp.minimum(i, blocks - 1), 0))],
+            out_specs=pl.BlockSpec((out_rows, D), lambda i, *_: (jnp.maximum(i - blocks, 0), 0)),
+            scratch_shapes=[
+                pltpu.VMEM((GATHER_BLOCK * SPLIT, 128), jnp.float32),
+                pltpu.VMEM(((count + 8) * SPLIT, 128), jnp.float32),
+            ],
+        ),
+        compiler_params=pltpu.CompilerParams(vmem_limit_bytes=VMEM_LIMIT),
+        cost_estimate=pl.CostEstimate(flops=0, transcendentals=0, bytes_accessed=160_000_000),
+        name="gather_rows",
+    )(*plan, table)
 
 
 def scatter_kernel(steps, block, out_rows, row_ref, from_ref, twice_ref, groups_ref, own_ref, other_ref, *rest):
@@ -155,25 +224,15 @@
             total[pl.ds(i * 192, 192), :] = jnp.zeros((192, 128), jnp.float32)
             return carry
 
-        lax.fori_loop(0, total.shape[0] // 192, clear, 0)
-
-    def widen(ref):
-        def strip(i, carry):
-            first = pl.multiple_of(i * 32, 32)
-            value = ref[pl.ds(first, 32), :].astype(jnp.float32)
-            for part in range(SPLIT):
-                wide[pl.ds(first * SPLIT + part, 32, stride=SPLIT), :] = value[:, part * 128 : (part + 1) * 128]
-            return carry
-
-        lax.fori_loop(0, block // 32, strip, 0)
+        lax.fori_loop(0, total.shape[0] // 192, clear, 0, unroll=4)
 
     @pl.when(step < steps // 2)
     def _():
-        widen(own_ref)
+        widen(own_ref, wide)
 
     @pl.when((step >= steps // 2) & (step < steps))
     def _():
-        widen(other_ref)
+        widen(other_ref, wide)
 
     @pl.when(step < steps)
     def _():
@@ -198,23 +257,13 @@
 
         lax.fori_loop(0, groups_ref[step], group, 0)
 
-    def narrow(out_ref):
-        def strip(i, carry):
-            first = pl.multiple_of((step - steps) * out_rows * SPLIT + i * (32 * SPLIT), 32 * SPLIT)
-            for part in range(SPLIT):
-                value = total[pl.ds(first + part, 32, stride=SPLIT), :]
-                out_ref[pl.ds(pl.multiple_of(i * 32, 32), 32), part * 128 : (part + 1) * 128] = value.astype(jnp.bfloat16)
-            return carry
-
-        lax.fori_loop(0, out_rows // 32, strip, 0)
-
     quarter = (total.shape[0] // SPLIT // 4) // out_rows
     for index, out_ref in enumerate(outs):
         last = quarter * (index + 1 if index < 2 else 4)
 
         @pl.when((step >= steps + quarter * index) & (step < steps + last))
         def _(out_ref=out_ref):
-            narrow(out_ref)
+            narrow(total, (step - steps) * out_rows, out_ref)
 
 
 SCATTER_BLOCK = 1024
@@ -274,6 +323,7 @@
 
 
 SIGNALS = 26
+LAG = 2
 
 
 def plus(first, second):
@@ -482,7 +532,8 @@
     for some in loads[1:]:
         for copy in some:
             copy.start()
-    for step in range(chunks + 4):
+    stages = ("merge_second", "merge_third", "finish", "hand_on")
+    for step in range(chunks + LAG * len(stages)):
         if step < chunks:
             for copy in loads[step]:
                 copy.wait()
@@ -493,10 +544,10 @@
             for copy in extra_first:
                 copy.wait_recv()
             extra.merge_first()
-        for stage, name in enumerate(("merge_second", "merge_third", "finish", "hand_on")):
-            if 0 <= step - 1 - stage < chunks:
-                getattr(units[step - 1 - stage], name)()
-            if step == 4 + stage:
+        for stage, name in enumerate(stages, 1):
+            if 0 <= step - LAG * stage < chunks:
+                getattr(units[step - LAG * stage], name)()
+            if step == 2 + LAG * stage:
                 getattr(extra, name)()
     for copy in extra_first:
         copy.wait_send()
@@ -582,7 +633,9 @@
 
 
 def reduce_packed(packed):
-    return lax.psum_scatter(packed.reshape(-1, D), ("store", "dp"), scatter_dimension=0, tiled=True)
+    return lax.psum_scatter(
+        packed.reshape(-1, D), ("store", "dp"), scatter_dimension=0, tiled=True
+    )
 
 
 def all_copies(share):
@@ -653,13 +706,9 @@
         yield pl.ds(first, CROSS_TOKENS), pl.ds(first * K, CROSS_TOKENS * K)
 
 
-def cross_forward_kernel(folded_ref, first_ref, second_ref, which_ref, rows_ref, summary_ref):
+def cross_forward_kernel(folded_ref, rows_ref, summary_ref):
     for some, slots in cross_tiles(folded_ref):
-        which = which_ref[slots, :] != 0
-        rows = jnp.where(
-            which, second_ref[slots, :].astype(jnp.float32), first_ref[slots, :].astype(jnp.float32)
-        ).astype(jnp.bfloat16)
-        rows_ref[slots, :] = rows
+        rows = rows_ref[slots, :]
         probs = cross_probs_of(folded_ref[:, some, :].reshape(H * CROSS_TOKENS, D), rows)
         summary = jnp.dot(probs.astype(jnp.bfloat16), rows, preferred_element_type=jnp.float32)
         summary_ref[:, some, :] = summary.astype(jnp.bfloat16).reshape(H, CROSS_TOKENS, D)
@@ -696,21 +745,18 @@
     return heads, rows
 
 
-def cross_forward(folded, first, second, which):
+def cross_forward(folded, fetched):
     heads, rows = cross_specs()
     tokens = folded.shape[1]
     return pl.pallas_call(
         cross_forward_kernel,
-        out_shape=[
-            jax.ShapeDtypeStruct((tokens * K, D), jnp.bfloat16),
-            jax.ShapeDtypeStruct((H, tokens, D), jnp.bfloat16),
-        ],
+        out_shape=jax.ShapeDtypeStruct((H, tokens, D), jnp.bfloat16),
         grid=(tokens // CROSS_STEP,),
-        in_specs=[heads, rows, rows, pl.BlockSpec((CROSS_STEP * K, 1), lambda i: (i, 0))],
-        out_specs=[rows, heads],
-        cost_estimate=pl.CostEstimate(flops=0, transcendentals=0, bytes_accessed=65_000_000),
+        in_specs=[heads, rows],
+        out_specs=heads,
+        cost_estimate=pl.CostEstimate(flops=0, transcendentals=0, bytes_accessed=55_000_000),
         name="cross_forward",
-    )(folded, first, second, which)
+    )(folded, fetched)
 
 
 def cross_backward(folded, grad, fetched):
@@ -758,7 +804,7 @@
     dense = is_dense(owners, rows_here)
     if dense:
         plan = plan_store(indices, rows_here)
-        found_first, found_second, which_half, plan = fetch_dense(datastore, indices, plan)
+        fetched, plan = fetch_dense(datastore, indices, plan)
     else:
         target, request = route_slots(indices, rows_here, owners, capacity)
         returned, _ = fetch_rows(request, datastore)
@@ -796,8 +842,7 @@
     ).astype(jnp.bfloat16)
     if dense:
         folded_heads = jnp.transpose(folded, (1, 0, 2))
-        fetched, summary = cross_forward(folded_heads, found_first, found_second, which_half)
-        summary = jnp.transpose(summary, (1, 0, 2))
+        summary = jnp.transpose(cross_forward(folded_heads, fetched), (1, 0, 2))
     else:
         cross_scores = jnp.einsum("thd,tkd->thk", folded, fetched, preferred_element_type=jnp.float32)
         cross_lse = log_total(cross_scores)

time: 1000 us -> 954 us (0.954)
  local copies, waits for them, and re-layouts: 195 us -> 99.2 us
  Pallas kernels: 307 us -> 345 us
    gather x2 -> x0, local copies, waits for them, and re-layouts: 96.9 us -> none  [fetch_dense(): found.append(table[local])]
    pallas_call x1 -> x2, Pallas kernels: 25.4 us -> 64.9 us  [the longest x1 44 us: gather_rows(): pl.pallas_call(functools.partial(gather_kernel, blocks, out_rows), out_sh...]
    all_gather x2 -> x1, waiting for transfers between devices: 204 us -> 213 us  [fetch_dense(): table = lax.all_gather(mine, ('store', 'dp'), axis=0, tiled=True)]
    unnamed x212 -> x220, local copies, waits for them, and re-layouts: 39.7 us -> 42.9 us
  transfers between devices with their start and end apart: 9 -> 8, of which waited for: 7 -> 6; matrix products, arithmetic and copies ran while one was open for 21% -> 18% of each run, Pallas kernels for 7% -> 7%
where the time goes in v8:
time: 954 us; the launch traced here: 948 us
  Pallas kernels  345 us (36%)
  waiting for transfers between devices  294 us (31%)
  matrix products  137 us (14%)
  local copies, waits for them, and re-layouts  99.2 us (10%)
  other arithmetic  52.1 us (5%)
  between operations  17.9 us (2%)
    all_gather x1, waiting for transfers between devices, fetch_dense(): table = lax.all_gather(mine, ('store', 'dp'), axis=0, tiled=True)  213 us
    pallas_call x1, Pallas kernels, reduce_rows(): pl.pallas_call(functools.partial(reduce_kernel, chunks), out_shape=[jax.S...  176 us
    pallas_call x1, Pallas kernels, scatter_rows(): pl.pallas_call(functools.partial(scatter_kernel, steps, block, out_rows),...  69.8 us
    ppermute x1, waiting for transfers between devices, swap_store(): came_a = lax.ppermute(send_a, 'store', [(i, i ^ 1) for i in range(owners)])  54.1 us
    pallas_call x1, Pallas kernels, gather_rows(): pl.pallas_call(functools.partial(gather_kernel, blocks, out_rows), out_sh...  44 us
    unnamed x220, local copies, waits for them, and re-layouts  42.9 us
    pallas_call x1, Pallas kernels, cross_backward(): pl.pallas_call(cross_backward_kernel, out_shape=[jax.ShapeDtypeStruct((to...  34.5 us
    dot_general x6, matrix products, product(): return jnp.dot(matrix, factor, preferred_element_type=jnp.float32)  31 us
  transfers between devices with their start and end apart: 8, of which 6 were waited for; matrix products, arithmetic and copies ran while one was open for 18% of the time, Pallas kernels for 7%

profile of v8, /device:TPU:0, one launch (start us, length us, event | category | flops | bytes accessed | tf_op | source)
XLA Modules:
  0.0 948.0 jit_solution(5405222979414758489)
XLA Ops:
  12.7 2.7 constant_dynamic-slice_fusion
  18.0 6.8 sort.30
  24.8 3.6 copy-done.2
  28.3 1.6 fusion.118
  29.9 3.0 copy.85
  32.8 2.4 copy.82
  35.2 3.7 copy.103
  38.9 4.3 fusion.17
  45.3 2.1 fusion
  47.5 2.6 exponential_reduce_fusion
  50.1 1.8 copy-done
  52.0 3.4 convolution_convert_fusion.10
  55.4 4.7 fusion.122
  62.6 2.2 add_convert_fusion.2
  66.7 5.2 multiply_convert_fusion.folded_ref
  80.4 213.3 %all-gather.3.cloned.1.call-done.table_ref = bf16[32768,768]{1,0:T(8,128)(2,1)} async-done(((bf16[1024,768]{1,0:T(8,128)(2,1)}), bf16[32768,768]{1,0:T(8,128)(2,1)}) %all-gather.3.cloned.1.call-update) | async-done | bytes 50331664 | tf_op jit(solution)/shard_map/all_gather | solution.py:116
  293.7 44.0 %gather_rows.1.rows_ref = bf16[8192,768]{1,0:T(8,128)(2,1)} custom-call(s32[8200]{0:T(1024)} %get-tuple-element.51.row_ref, s32[8200]{0:T(1024)} %get-tuple-element.52.to_ref, s32[17]{0:T(128)} %convert_reduce_fusion.1.start_ref, bf16[32768,768]{1,0:T(8,128)(2,1)} %all-gather.3.cloned.1.call-done.table_ref), custom_call_target="tpu_custom_call" | custom-call | bytes 160000000 | tf_op jit(solution)/shard_map/gather_rows/pallas_call | solution.py:198
  337.7 20.9 %cross_forward.1 = bf16[12,512,768]{2,1,0:T(8,128)(2,1)} custom-call(bf16[12,512,768]{2,1,0:T(8,128)(2,1)} %multiply_convert_fusion.folded_ref, bf16[8192,768]{1,0:T(8,128)(2,1)} %gather_rows.1.rows_ref), custom_call_target="tpu_custom_call" | custom-call | bytes 55000000 | tf_op jit(solution)/shard_map/cross_forward/pallas_call | solution.py:751
  358.6 6.8 fusion.19
  367.0 19.6 %multiply_convert_fusion.2 = (bf16[512,3072]{1,0:T(8,128)(2,1)S(1)}, f32[512,3072]{1,0:T(8,128)}, f32[512,3072]{1,0:T(8,128)}) fusion(f32[3072]{0:T(1024)S(1)} %copy-done.91, bf16[768,3072]{1,0:T(8,128)(2,1)} %param.23, f32[512,768]{1,0:T(8,128)S(1)} %get-tuple-element.184, f32[768]{0:T(1024)S(1)} %copy-done.86, f32[768]{0:T(1024)S(1)} %copy-done.62, ...), kind=kOutput, calls=%fused_computation.23 | convolution fusion | flops 2521694208 | bytes 22042624 | tf_op jit(solution)/shard_map/dot_general | solution.py:21
  386.7 2.8 fusion.127
  389.8 1.7 multiply_reduce_fusion.1
  392.2 4.3 convolution_convert_fusion.2
  396.5 8.7 fusion.129
  405.2 6.6 multiply_reduce_fusion.2
  411.8 3.6 convolution_convert_fusion.3
  416.1 1.7 fusion.128
  417.8 1.9 fusion.119
  419.8 1.9 convolution_convert_fusion.6
  423.1 2.8 constant_dynamic-update-slice_fusion.5
  429.2 4.8 constant_dynamic-update-slice_fusion.1
  435.2 5.0 convolution_convert_fusion.grad_ref
  440.2 34.5 %cross_backward.1 = (bf16[8192,768]{1,0:T(8,128)(2,1)}, bf16[12,512,768]{2,1,0:T(8,128)(2,1)}) custom-call(bf16[12,512,768]{2,1,0:T(8,128)(2,1)} %multiply_convert_fusion.folded_ref, bf16[12,512,768]{2,1,0:T(8,128)(2,1)} %convolution_convert_fusion.grad_ref, bf16[8192,768]{1,0:T(8,128)(2,1)} %gather_rows.1.rows_ref), custom_call_target="tpu_custom_call" | custom-call | bytes 100000000 | tf_op jit(solution)/shard_map/cross_backward/pallas_call | solution.py:765
  480.3 5.9 fusion.30
  486.2 2.1 convert_element_type.301
  488.3 1.8 copy.96
  490.1 8.0 multiply_convert_fusion.6
  498.2 69.8 %scatter_rows.1 = (bf16[4096,768]{1,0:T(8,128)(2,1)}, bf16[4096,768]{1,0:T(8,128)(2,1)}, bf16[8192,768]{1,0:T(8,128)(2,1)}) custom-call(s32[16384]{0:T(1024)} %bitcast.253, s32[16384]{0:T(1024)} %bitcast.254, s32[2048]{0:T(1024)} %or_or_fusion.twice_ref, s32[16]{0:T(128)} %and_select_fusion.groups_ref, bf16[8192,768]{1,0:T(8,128)(2,1)} %get-tuple-element.56.own_ref, ...), custom_call_target="tpu_custom_call" | custom-call | bytes 220000000 | tf_op jit(solution)/shard_map/scatter_rows/pallas_call | solution.py:299
  570.1 4.9 multiply_reduce_fusion.3
  575.7 1.9 convert_reduce_fusion.3
  578.3 2.6 convolution_convert_fusion.7
  582.6 5.4 fusion.33
  588.1 2.6 convert_element_type.304
  590.7 2.9 copy.97
  593.6 7.5 bitcast_reduce_fusion
  601.2 1.6 collective-permute-start.2
  602.8 7.0 multiply_reduce_fusion
  609.7 7.1 multiply_convert_fusion.1
  620.9 4.9 multiply_convert_fusion.4
  625.8 2.0 convolution_convert_fusion.1
  627.9 1.6 fusion.120
  629.5 2.4 copy.108
  631.9 2.4 copy.107
  634.3 1.6 copy.106
  644.3 2.5 dynamic-slice_bitcast_fusion
  646.8 2.5 copy-done.3
  649.9 5.2 add_convert_fusion.1
  655.1 18.8 %all-gather.5.cloned.1.call-done = bf16[864,768]{1,0:T(8,128)(2,1)} async-done(((bf16[216,768]{1,0:T(8,128)(2,1)}), bf16[864,768]{1,0:T(8,128)(2,1)}) %all-gather.5.cloned.1.call-update) | async-done | bytes 1327120 | tf_op jit(solution)/shard_map/all_gather | solution.py:642
  674.0 2.4 fusion.124
  679.0 7.1 fusion.1
  686.1 54.1 %collective-permute-done.2 = bf16[4096,768]{1,0:T(8,128)(2,1)} collective-permute-done((bf16[4096,768]{1,0:T(8,128)(2,1)}, bf16[4096,768]{1,0:T(8,128)(2,1)}, u32[]{:S(2)}, u32[]{:S(2)}) %collective-permute-start.2) | collective-permute-done | bytes 6291488 | tf_op jit(solution)/shard_map/ppermute | solution.py:625
  740.2 7.2 collective-permute-done.3
  747.4 175.9 %reduce_rows.1 = (bf16[2,2,2,8,64,768]{5,4,3,2,1,0:T(8,128)(2,1)}, bf16[2,2,2,96,768]{4,3,2,1,0:T(8,128)(2,1)}) custom-call(bf16[2,4,2,8,64,768]{5,4,3,2,1,0:T(8,128)(2,1)} %bitcast.206, bf16[4,2,8,64,768]{4,3,2,1,0:T(8,128)(2,1)} %bitcast.39.came_a, bf16[4,2,8,64,768]{4,3,2,1,0:T(8,128)(2,1)} %bitcast.40.came_b, bf16[4,2,2,2,96,768]{5,4,3,2,1,0:T(8,128)(2,1)} %bitcast.205), custom_call_target="tpu_custom_call" | custom-call | bytes 450000000 | tf_op jit(solution)/shard_map/reduce_rows/pallas_call | solution.py:569
  931.1 9.2 bitcast_convert_fusion
  (324 shorter events, 64.5 us)
Async XLA Ops:
  8.0 64.4 %sort.33.cloned.1.call-start = ((), (), s32[]{:S(2)}) async-start(), calls=%async_computation.4 | async-start | bytes 393248 | tf_op jit(solution)/shard_map/sort | solution.py:276
  9.1 8.9 copy-start.44
  9.1 1.4 collective-permute-start
  12.6 3.5 copy-start.64
  12.7 281.0 %all-gather.3.cloned.1.call-start = ((), (), s32[]{:S(2)}) async-start(), calls=%async_computation.1 | async-start | bytes 51904512 | tf_op jit(solution)/shard_map/all_gather | solution.py:116
  15.4 634.5 %reduce-scatter.2.cloned.1.call-start = ((), (), s32[]{:S(2)}) async-start(), calls=%async_computation.2 | async-start | bytes 10948608 | tf_op jit(solution)/shard_map/reduce_scatter | solution.py:636
  24.8 3.6 copy-start.2
  29.9 5.3 slice-start
  43.7 3.7 copy-start.4
  44.0 3.4 copy-start.13
  44.3 5.8 copy-start.32
  45.2 16.6 %copy-start.59 = (f32[768]{0:T(1024)}, f32[768]{0:T(1024)S(1)}, u32[]{:S(2)}) copy-start(f32[768]{0:T(1024)S(1)} %get-tuple-element.201) | copy-start | bytes 9220
  45.2 16.6 %copy-start.83 = (f32[768]{0:T(1024)}, f32[768]{0:T(1024)S(1)}, u32[]{:S(2)}) copy-start(f32[768]{0:T(1024)S(1)} %get-tuple-element.137) | copy-start | bytes 9220
  45.3 4.7 copy-start.15
  47.4 4.5 copy-start
  52.0 3.4 copy-start.12
  55.4 4.7 copy-start.39
  55.4 4.7 copy-start.89
  62.6 3.4 copy-start.52
  62.6 3.4 copy-start.53
  65.2 6.7 copy-start.8
  66.7 5.2 copy-start.88
  337.7 20.9 %copy-start.6 = (bf16[768,1,768]{0,2,1:T(8,128)(2,1)S(1)}, bf16[768,1,768]{0,2,1:T(8,128)(2,1)}, u32[]{:S(2)}) copy-start(bf16[768,1,768]{0,2,1:T(8,128)(2,1)} %copy.85) | copy-start | bytes 3538948
  337.7 20.9 %copy-start.54 = (f32[12,64]{1,0:T(8,128)S(1)}, f32[12,64]{1,0:T(8,128)}, u32[]{:S(2)}) copy-start(f32[12,64]{1,0:T(8,128)} %add.352) | copy-start | bytes 9220
  358.6 6.8 copy-start.19
  358.6 6.8 copy-start.37
  358.6 6.8 copy-start.57
  358.6 6.8 copy-start.60
  358.6 6.8 copy-start.66
  358.6 6.8 copy-start.84
  358.6 6.8 copy-start.87
  365.5 21.1 %slice-start.1 = ((s8[4718592]{0:T(1024)(128)(4,1)}), s8[4194304]{0:T(1024)(128)(4,1)S(1)}, s32[]{:S(2)}) async-start(s8[4718592]{0:T(1024)(128)(4,1)} %bitcast.255), calls=%async_computation.7 | async-start | bytes 8388608
  366.9 19.7 %slice-start.2 = ((s8[4718592]{0:T(1024)(128)(4,1)}), s8[524288]{0:T(1024)(128)(4,1)S(1)}, s32[]{:S(2)}) async-start(s8[4718592]{0:T(1024)(128)(4,1)} %bitcast.255), calls=%async_computation.8 | async-start | bytes 1048576
  367.0 19.7 %copy-start.92 = (f32[768]{0:T(1024)S(1)}, f32[768]{0:T(1024)}, u32[]{:S(2)}) copy-start(f32[768]{0:T(1024)} %param.26) | copy-start | bytes 9220
  386.6 3.2 copy-start.35
  386.7 3.2 copy-start.49
  386.7 3.2 copy-start.63
  405.2 6.6 copy-start.94
  411.8 3.6 copy-start.51
  416.1 3.7 copy-start.17
  423.1 12.1 %copy-start.10 = (bf16[512,768]{0,1:T(8,128)(2,1)}, bf16[512,768]{0,1:T(8,128)(2,1)S(1)}, u32[]{:S(2)}) copy-start(bf16[512,768]{0,1:T(8,128)(2,1)S(1)} %copy.87) | copy-start | bytes 2359300
  423.1 3.9 copy-start.22
  429.2 4.8 copy-start.24
  474.7 23.5 %collective-permute-start.1 = (bf16[8192,768]{1,0:T(8,128)(2,1)}, bf16[8192,768]{1,0:T(8,128)(2,1)}, u32[]{:S(2)}, u32[]{:S(2)}) collective-permute-start(bf16[8192,768]{1,0:T(8,128)(2,1)} %get-tuple-element.56.own_ref), channel_id=1, source_target_pairs={{0,8},{8,0},{16,24},{24,16},{1,9},{9,1},{17,25},{25,17},{2,10},{10... | collective-permute-start | bytes 37748744 | tf_op jit(solution)/shard_map/ppermute | solution.py:912
  475.1 5.2 copy-start.9
  475.1 198.9 %all-gather.5.cloned.1.call-start = ((), (), s32[]{:S(2)}) async-start(), calls=%async_computation.3 | async-start | bytes 1658880 | tf_op jit(solution)/shard_map/all_gather | solution.py:642
  570.1 5.6 copy-start.20
  570.1 5.6 copy-start.58
  570.1 5.6 copy-start.61
  570.1 5.6 copy-start.67
  578.3 4.4 copy-start.11
  588.1 5.5 copy-start.16
  593.6 9.1 copy-start.33
  601.2 139.0 %collective-permute-start.2 = (bf16[4096,768]{1,0:T(8,128)(2,1)}, bf16[4096,768]{1,0:T(8,128)(2,1)}, u32[]{:S(2)}, u32[]{:S(2)}) collective-permute-start(bf16[4096,768]{1,0:T(8,128)(2,1)} %get-tuple-element.67), channel_id=1, source_target_pairs={{0,1},{1,0},{2,3},{3,2},{4,5},{5,4},{6,7},{7,6},{8,9},{9,8},{10,11... | collective-permute-start | bytes 18874376 | tf_op jit(solution)/shard_map/ppermute | solution.py:625
  602.8 144.6 %collective-permute-start.3 = (bf16[4096,768]{1,0:T(8,128)(2,1)}, bf16[4096,768]{1,0:T(8,128)(2,1)}, u32[]{:S(2)}, u32[]{:S(2)}) collective-permute-start(bf16[4096,768]{1,0:T(8,128)(2,1)} %get-tuple-element.68), channel_id=1, source_target_pairs={{0,16},{8,24},{16,0},{24,8},{1,17},{9,25},{17,1},{25,9},{2,18},{10... | collective-permute-start | bytes 18874376 | tf_op jit(solution)/shard_map/ppermute | solution.py:626
  609.7 7.1 copy-start.5
  617.0 3.9 copy-start.14
  620.9 4.9 copy-start.90
  620.9 4.9 copy-start.93
  644.3 5.0 copy-start.3
  644.3 5.6 copy-start.43
  649.3 29.7 %collective-permute-start.4 = (bf16[8,384,768]{2,1,0:T(8,128)(2,1)}, bf16[8,384,768]{2,1,0:T(8,128)(2,1)}, u32[]{:S(2)}, u32[]{:S(2)}) collective-permute-start(bf16[8,384,768]{2,1,0:T(8,128)(2,1)} %dynamic-slice_bitcast_fusion), channel_id=1, source_target_pairs={{0,8},{8,0},{16,24},{24,16},{1,9},{9,1},{17,25},{25,17},{2,10},{10... | collective-permute-start | bytes 14155784 | tf_op jit(solution)/shard_map/ppermute | solution.py:679
  924.7 4.9 copy-start.38
  931.0 9.2 copy-start.48
  (43 other events, 87.5 us)
Sparse Core Ops, SparseCore 0:
  12.8 5.5 sort.35.cloned.1.call-done
  650.0 23.8 all-gather.4
  (1 shorter events, 0.0 us)
Sparse Core Ops, SparseCore 1:
  16.6 277.0 all-gather.2
  475.2 141.9 reduce-scatter.1

commit v9 on v8

--- a/solution.py
+++ b/solution.py
@@ -152,7 +152,7 @@
     lax.fori_loop(0, out_ref.shape[0] // 32, strip, 0, unroll=4)
 
 
-GATHER_BLOCK = 2048
+GATHER_BLOCK = 4096
 
 
 def gather_kernel(blocks, out_rows, row_ref, to_ref, start_ref, table_ref, out_ref, wide, found):
@@ -193,7 +193,7 @@
     return SPLIT * row, SPLIT * place, starts
 
 
-def gather_rows(plan, table, count, out_rows=1024):
+def gather_rows(plan, table, count, out_rows=2048):
     blocks = table.shape[0] // GATHER_BLOCK
     return pl.pallas_call(
         functools.partial(gather_kernel, blocks, out_rows),
@@ -527,28 +527,29 @@
         unit.loads((keep_ref.at[0, :, :, q], keep_ref.at[1, :, :, q], came_a.at[:, :, q], came_b.at[:, :, q]))
         for q, unit in enumerate(units)
     ]
-    for copy in loads[0] + extra_first + extra_loads:
-        copy.start()
-    for some in loads[1:]:
+    for some in loads + [extra_loads]:
         for copy in some:
             copy.start()
     stages = ("merge_second", "merge_third", "finish", "hand_on")
-    for step in range(chunks + LAG * len(stages)):
+    for step in range(chunks + LAG * len(stages) + 1):
         if step < chunks:
             for copy in loads[step]:
                 copy.wait()
             units[step].merge_first()
-        if step == 2:
+        for stage, name in enumerate(stages, 1):
+            if 0 <= step - LAG * stage < chunks:
+                getattr(units[step - LAG * stage], name)()
+            if step == chunks + LAG * stage:
+                getattr(extra, name)()
+        if step == 3:
+            for copy in extra_first:
+                copy.start()
+        if step == chunks:
             for copy in extra_loads:
                 copy.wait()
             for copy in extra_first:
                 copy.wait_recv()
             extra.merge_first()
-        for stage, name in enumerate(stages, 1):
-            if 0 <= step - LAG * stage < chunks:
-                getattr(units[step - LAG * stage], name)()
-            if step == 2 + LAG * stage:
-                getattr(extra, name)()
     for copy in extra_first:
         copy.wait_send()
     for unit in units + [extra]:

time: 954 us -> 944 us (0.990)
  Pallas kernels: 345 us -> 335 us
where the time goes in v9:
time: 944 us; the launch traced here: 938 us
  Pallas kernels  335 us (35%)
  waiting for transfers between devices  294 us (31%)
  matrix products  137 us (15%)
  local copies, waits for them, and re-layouts  99.2 us (11%)
  other arithmetic  52 us (6%)
  between operations  17.9 us (2%)
    all_gather x1, waiting for transfers between devices, fetch_dense(): table = lax.all_gather(mine, ('store', 'dp'), axis=0, tiled=True)  213 us
    pallas_call x1, Pallas kernels, reduce_rows(): pl.pallas_call(functools.partial(reduce_kernel, chunks), out_shape=[jax.S...  166 us
    pallas_call x1, Pallas kernels, scatter_rows(): pl.pallas_call(functools.partial(scatter_kernel, steps, block, out_rows),...  69.8 us
    ppermute x1, waiting for transfers between devices, swap_store(): came_a = lax.ppermute(send_a, 'store', [(i, i ^ 1) for i in range(owners)])  54.1 us
    pallas_call x1, Pallas kernels, gather_rows(): pl.pallas_call(functools.partial(gather_kernel, blocks, out_rows), out_sh...  43.6 us
    unnamed x220, local copies, waits for them, and re-layouts  42.9 us
    pallas_call x1, Pallas kernels, cross_backward(): pl.pallas_call(cross_backward_kernel, out_shape=[jax.ShapeDtypeStruct((to...  34.5 us
    dot_general x6, matrix products, product(): return jnp.dot(matrix, factor, preferred_element_type=jnp.float32)  31 us
  transfers between devices with their start and end apart: 8, of which 6 were waited for; matrix products, arithmetic and copies ran while one was open for 18% of the time, Pallas kernels for 7%

profile of v9, /device:TPU:0, one launch (start us, length us, event | category | flops | bytes accessed | tf_op | source)
XLA Modules:
  0.0 938.0 jit_solution(4802197072424241558)
XLA Ops:
  12.7 2.7 constant_dynamic-slice_fusion
  18.0 6.8 sort.30
  24.8 3.6 copy-done.2
  28.3 1.6 fusion.118
  29.9 3.0 copy.85
  32.8 2.4 copy.82
  35.2 3.7 copy.103
  38.9 4.3 fusion.17
  45.3 2.1 fusion
  47.5 2.6 exponential_reduce_fusion
  50.1 1.8 copy-done
  52.0 3.4 convolution_convert_fusion.10
  55.4 4.7 fusion.122
  62.6 2.2 add_convert_fusion.2
  66.7 5.2 multiply_convert_fusion.folded_ref
  80.4 213.3 %all-gather.3.cloned.1.call-done.table_ref = bf16[32768,768]{1,0:T(8,128)(2,1)} async-done(((bf16[1024,768]{1,0:T(8,128)(2,1)}), bf16[32768,768]{1,0:T(8,128)(2,1)}) %all-gather.3.cloned.1.call-update) | async-done | bytes 50331664 | tf_op jit(solution)/shard_map/all_gather | solution.py:116
  293.7 43.6 %gather_rows.1.rows_ref = bf16[8192,768]{1,0:T(8,128)(2,1)} custom-call(s32[8200]{0:T(1024)} %get-tuple-element.51.row_ref, s32[8200]{0:T(1024)} %get-tuple-element.52.to_ref, s32[9]{0:T(128)} %convert_reduce_fusion.1.start_ref, bf16[32768,768]{1,0:T(8,128)(2,1)} %all-gather.3.cloned.1.call-done.table_ref), custom_call_target="tpu_custom_call" | custom-call | bytes 160000000 | tf_op jit(solution)/shard_map/gather_rows/pallas_call | solution.py:198
  337.3 20.9 %cross_forward.1 = bf16[12,512,768]{2,1,0:T(8,128)(2,1)} custom-call(bf16[12,512,768]{2,1,0:T(8,128)(2,1)} %multiply_convert_fusion.folded_ref, bf16[8192,768]{1,0:T(8,128)(2,1)} %gather_rows.1.rows_ref), custom_call_target="tpu_custom_call" | custom-call | bytes 55000000 | tf_op jit(solution)/shard_map/cross_forward/pallas_call | solution.py:752
  358.2 6.8 fusion.19
  366.6 19.6 %multiply_convert_fusion.2 = (bf16[512,3072]{1,0:T(8,128)(2,1)S(1)}, f32[512,3072]{1,0:T(8,128)}, f32[512,3072]{1,0:T(8,128)}) fusion(f32[3072]{0:T(1024)S(1)} %copy-done.91, bf16[768,3072]{1,0:T(8,128)(2,1)} %param.23, f32[512,768]{1,0:T(8,128)S(1)} %get-tuple-element.184, f32[768]{0:T(1024)S(1)} %copy-done.86, f32[768]{0:T(1024)S(1)} %copy-done.62, ...), kind=kOutput, calls=%fused_computation.23 | convolution fusion | flops 2521694208 | bytes 22042624 | tf_op jit(solution)/shard_map/dot_general | solution.py:21
  386.3 2.8 fusion.127
  389.4 1.7 multiply_reduce_fusion.1
  391.7 4.3 convolution_convert_fusion.2
  396.1 8.7 fusion.129
  404.8 6.6 multiply_reduce_fusion.2
  411.4 3.6 convolution_convert_fusion.3
  415.7 1.7 fusion.128
  417.4 1.9 fusion.119
  419.4 1.9 convolution_convert_fusion.6
  422.7 2.8 constant_dynamic-update-slice_fusion.5
  428.8 4.8 constant_dynamic-update-slice_fusion.1
  434.8 5.0 convolution_convert_fusion.grad_ref
  439.8 34.5 %cross_backward.1 = (bf16[8192,768]{1,0:T(8,128)(2,1)}, bf16[12,512,768]{2,1,0:T(8,128)(2,1)}) custom-call(bf16[12,512,768]{2,1,0:T(8,128)(2,1)} %multiply_convert_fusion.folded_ref, bf16[12,512,768]{2,1,0:T(8,128)(2,1)} %convolution_convert_fusion.grad_ref, bf16[8192,768]{1,0:T(8,128)(2,1)} %gather_rows.1.rows_ref), custom_call_target="tpu_custom_call" | custom-call | bytes 100000000 | tf_op jit(solution)/shard_map/cross_backward/pallas_call | solution.py:766
  479.8 5.9 fusion.30
  485.6 2.1 convert_element_type.301
  487.8 1.8 copy.96
  489.6 8.0 multiply_convert_fusion.6
  497.8 69.8 %scatter_rows.1 = (bf16[4096,768]{1,0:T(8,128)(2,1)}, bf16[4096,768]{1,0:T(8,128)(2,1)}, bf16[8192,768]{1,0:T(8,128)(2,1)}) custom-call(s32[16384]{0:T(1024)} %bitcast.253, s32[16384]{0:T(1024)} %bitcast.254, s32[2048]{0:T(1024)} %or_or_fusion.twice_ref, s32[16]{0:T(128)} %and_select_fusion.groups_ref, bf16[8192,768]{1,0:T(8,128)(2,1)} %get-tuple-element.56.own_ref, ...), custom_call_target="tpu_custom_call" | custom-call | bytes 220000000 | tf_op jit(solution)/shard_map/scatter_rows/pallas_call | solution.py:299
  569.7 4.9 multiply_reduce_fusion.3
  575.3 1.9 convert_reduce_fusion.3
  577.9 2.6 convolution_convert_fusion.7
  582.2 5.4 fusion.33
  587.7 2.6 convert_element_type.304
  590.3 2.9 copy.97
  593.2 7.5 bitcast_reduce_fusion
  600.8 1.6 collective-permute-start.2
  602.4 7.0 multiply_reduce_fusion
  609.4 7.1 multiply_convert_fusion.1
  620.5 4.9 multiply_convert_fusion.4
  625.5 2.0 convolution_convert_fusion.1
  627.5 1.6 fusion.120
  629.1 2.4 copy.108
  631.5 2.4 copy.107
  633.9 1.6 copy.106
  643.9 2.5 dynamic-slice_bitcast_fusion
  646.4 2.5 copy-done.3
  649.4 5.2 add_convert_fusion.1
  654.6 18.9 %all-gather.5.cloned.1.call-done = bf16[864,768]{1,0:T(8,128)(2,1)} async-done(((bf16[216,768]{1,0:T(8,128)(2,1)}), bf16[864,768]{1,0:T(8,128)(2,1)}) %all-gather.5.cloned.1.call-update) | async-done | bytes 1327120 | tf_op jit(solution)/shard_map/all_gather | solution.py:643
  673.5 2.4 fusion.124
  678.6 7.1 fusion.1
  685.6 54.1 %collective-permute-done.2 = bf16[4096,768]{1,0:T(8,128)(2,1)} collective-permute-done((bf16[4096,768]{1,0:T(8,128)(2,1)}, bf16[4096,768]{1,0:T(8,128)(2,1)}, u32[]{:S(2)}, u32[]{:S(2)}) %collective-permute-start.2) | collective-permute-done | bytes 6291488 | tf_op jit(solution)/shard_map/ppermute | solution.py:626
  739.7 7.1 collective-permute-done.3
  746.9 166.5 %reduce_rows.1 = (bf16[2,2,2,8,64,768]{5,4,3,2,1,0:T(8,128)(2,1)}, bf16[2,2,2,96,768]{4,3,2,1,0:T(8,128)(2,1)}) custom-call(bf16[2,4,2,8,64,768]{5,4,3,2,1,0:T(8,128)(2,1)} %bitcast.206, bf16[4,2,8,64,768]{4,3,2,1,0:T(8,128)(2,1)} %bitcast.39.came_a, bf16[4,2,8,64,768]{4,3,2,1,0:T(8,128)(2,1)} %bitcast.40.came_b, bf16[4,2,2,2,96,768]{5,4,3,2,1,0:T(8,128)(2,1)} %bitcast.205), custom_call_target="tpu_custom_call" | custom-call | bytes 450000000 | tf_op jit(solution)/shard_map/reduce_rows/pallas_call | solution.py:570
  921.1 9.2 bitcast_convert_fusion
  (324 shorter events, 64.3 us)
Async XLA Ops:
  8.0 64.4 %sort.33.cloned.1.call-start = ((), (), s32[]{:S(2)}) async-start(), calls=%async_computation.4 | async-start | bytes 393248 | tf_op jit(solution)/shard_map/sort | solution.py:276
  9.1 8.9 copy-start.44
  9.1 1.4 collective-permute-start
  12.6 3.5 copy-start.64
  12.7 281.0 %all-gather.3.cloned.1.call-start = ((), (), s32[]{:S(2)}) async-start(), calls=%async_computation.1 | async-start | bytes 51904512 | tf_op jit(solution)/shard_map/all_gather | solution.py:116
  15.4 634.0 %reduce-scatter.2.cloned.1.call-start = ((), (), s32[]{:S(2)}) async-start(), calls=%async_computation.2 | async-start | bytes 10948608 | tf_op jit(solution)/shard_map/reduce_scatter | solution.py:637
  24.8 3.6 copy-start.2
  29.9 5.3 slice-start
  43.7 3.7 copy-start.4
  44.0 3.4 copy-start.13
  44.3 5.8 copy-start.32
  45.2 16.6 %copy-start.59 = (f32[768]{0:T(1024)}, f32[768]{0:T(1024)S(1)}, u32[]{:S(2)}) copy-start(f32[768]{0:T(1024)S(1)} %get-tuple-element.201) | copy-start | bytes 9220
  45.2 16.6 %copy-start.83 = (f32[768]{0:T(1024)}, f32[768]{0:T(1024)S(1)}, u32[]{:S(2)}) copy-start(f32[768]{0:T(1024)S(1)} %get-tuple-element.137) | copy-start | bytes 9220
  45.3 4.7 copy-start.15
  47.4 4.5 copy-start
  52.0 3.4 copy-start.12
  55.4 4.7 copy-start.39
  55.4 4.7 copy-start.89
  62.6 3.4 copy-start.52
  62.6 3.4 copy-start.53
  65.2 6.7 copy-start.8
  66.7 5.2 copy-start.88
  337.3 20.9 %copy-start.6 = (bf16[768,1,768]{0,2,1:T(8,128)(2,1)S(1)}, bf16[768,1,768]{0,2,1:T(8,128)(2,1)}, u32[]{:S(2)}) copy-start(bf16[768,1,768]{0,2,1:T(8,128)(2,1)} %copy.85) | copy-start | bytes 3538948
  337.3 20.9 %copy-start.54 = (f32[12,64]{1,0:T(8,128)S(1)}, f32[12,64]{1,0:T(8,128)}, u32[]{:S(2)}) copy-start(f32[12,64]{1,0:T(8,128)} %add.352) | copy-start | bytes 9220
  358.1 6.8 copy-start.19
  358.2 6.8 copy-start.37
  358.2 6.8 copy-start.57
  358.2 6.8 copy-start.60
  358.2 6.8 copy-start.66
  358.2 6.8 copy-start.84
  358.2 6.8 copy-start.87
  365.1 21.1 %slice-start.1 = ((s8[4718592]{0:T(1024)(128)(4,1)}), s8[4194304]{0:T(1024)(128)(4,1)S(1)}, s32[]{:S(2)}) async-start(s8[4718592]{0:T(1024)(128)(4,1)} %bitcast.255), calls=%async_computation.7 | async-start | bytes 8388608
  366.5 19.7 %slice-start.2 = ((s8[4718592]{0:T(1024)(128)(4,1)}), s8[524288]{0:T(1024)(128)(4,1)S(1)}, s32[]{:S(2)}) async-start(s8[4718592]{0:T(1024)(128)(4,1)} %bitcast.255), calls=%async_computation.8 | async-start | bytes 1048576
  366.5 19.7 %copy-start.92 = (f32[768]{0:T(1024)S(1)}, f32[768]{0:T(1024)}, u32[]{:S(2)}) copy-start(f32[768]{0:T(1024)} %param.26) | copy-start | bytes 9220
  386.2 3.2 copy-start.35
  386.2 3.2 copy-start.49
  386.3 3.2 copy-start.63
  404.8 6.6 copy-start.94
  411.4 3.6 copy-start.51
  415.7 3.7 copy-start.17
  422.6 12.1 %copy-start.10 = (bf16[512,768]{0,1:T(8,128)(2,1)}, bf16[512,768]{0,1:T(8,128)(2,1)S(1)}, u32[]{:S(2)}) copy-start(bf16[512,768]{0,1:T(8,128)(2,1)S(1)} %copy.87) | copy-start | bytes 2359300
  422.7 3.9 copy-start.22
  428.7 4.8 copy-start.24
  474.3 23.5 %collective-permute-start.1 = (bf16[8192,768]{1,0:T(8,128)(2,1)}, bf16[8192,768]{1,0:T(8,128)(2,1)}, u32[]{:S(2)}, u32[]{:S(2)}) collective-permute-start(bf16[8192,768]{1,0:T(8,128)(2,1)} %get-tuple-element.56.own_ref), channel_id=1, source_target_pairs={{0,8},{8,0},{16,24},{24,16},{1,9},{9,1},{17,25},{25,17},{2,10},{10... | collective-permute-start | bytes 37748744 | tf_op jit(solution)/shard_map/ppermute | solution.py:913
  474.5 5.2 copy-start.9
  474.6 198.9 %all-gather.5.cloned.1.call-start = ((), (), s32[]{:S(2)}) async-start(), calls=%async_computation.3 | async-start | bytes 1658880 | tf_op jit(solution)/shard_map/all_gather | solution.py:643
  569.7 5.6 copy-start.20
  569.7 5.6 copy-start.58
  569.7 5.6 copy-start.61
  569.7 5.6 copy-start.67
  577.9 4.4 copy-start.11
  587.7 5.5 copy-start.16
  593.2 9.2 copy-start.33
  600.8 139.0 %collective-permute-start.2 = (bf16[4096,768]{1,0:T(8,128)(2,1)}, bf16[4096,768]{1,0:T(8,128)(2,1)}, u32[]{:S(2)}, u32[]{:S(2)}) collective-permute-start(bf16[4096,768]{1,0:T(8,128)(2,1)} %get-tuple-element.67), channel_id=1, source_target_pairs={{0,1},{1,0},{2,3},{3,2},{4,5},{5,4},{6,7},{7,6},{8,9},{9,8},{10,11... | collective-permute-start | bytes 18874376 | tf_op jit(solution)/shard_map/ppermute | solution.py:626
  602.4 144.5 %collective-permute-start.3 = (bf16[4096,768]{1,0:T(8,128)(2,1)}, bf16[4096,768]{1,0:T(8,128)(2,1)}, u32[]{:S(2)}, u32[]{:S(2)}) collective-permute-start(bf16[4096,768]{1,0:T(8,128)(2,1)} %get-tuple-element.68), channel_id=1, source_target_pairs={{0,16},{8,24},{16,0},{24,8},{1,17},{9,25},{17,1},{25,9},{2,18},{10... | collective-permute-start | bytes 18874376 | tf_op jit(solution)/shard_map/ppermute | solution.py:627
  609.3 7.1 copy-start.5
  616.6 3.9 copy-start.14
  620.5 4.9 copy-start.90
  620.5 4.9 copy-start.93
  643.9 5.0 copy-start.3
  643.9 5.5 copy-start.43
  649.0 29.6 %collective-permute-start.4 = (bf16[8,384,768]{2,1,0:T(8,128)(2,1)}, bf16[8,384,768]{2,1,0:T(8,128)(2,1)}, u32[]{:S(2)}, u32[]{:S(2)}) collective-permute-start(bf16[8,384,768]{2,1,0:T(8,128)(2,1)} %dynamic-slice_bitcast_fusion), channel_id=1, source_target_pairs={{0,8},{8,0},{16,24},{24,16},{1,9},{9,1},{17,25},{25,17},{2,10},{10... | collective-permute-start | bytes 14155784 | tf_op jit(solution)/shard_map/ppermute | solution.py:680
  914.8 4.9 copy-start.38
  921.1 9.2 copy-start.48
  (43 other events, 87.5 us)
Sparse Core Ops, SparseCore 0:
  12.8 5.5 sort.35.cloned.1.call-done
  649.5 23.9 all-gather.4
  (1 shorter events, 0.0 us)
Sparse Core Ops, SparseCore 1:
  16.6 277.0 all-gather.2
  474.6 142.0 reduce-scatter.1
